TPU v7x, 32 devices: a whole 2x2x4 slice. The times are simulated.
32 devices in a mesh: grp: 2 (over core), own: 16 (over z, y, x).
Axes of the slice: x: 2, y: 2, z: 4, core: 2. Of those that a mesh axis runs over, the one named last changes fastest.
Arguments:
- activations: bfloat16 [8192, 1280], P(('grp', 'own')), may hold values from -18 to 18
- cotangents: bfloat16 [8192, 256], P(('grp', 'own')), may hold values from -18 to 18
- input_factor: float32 [2, 640, 640], P(None, 'grp'), may hold values from -0.4 to 3.6, as said below
- output_factor: float32 [256, 256], replicated, may hold values from -0.4 to 3.6, as said below
- gradient: float32 [2, 640, 256], P(None, 'grp'), may hold values from -4100 to 4100
- weights: float32 [2, 640, 256], P(None, 'grp'), may hold values from -6 to 6
- momentum: float32 [2, 640, 256], P(None, 'grp'), may hold values from -6 to 6
Outputs:
- new_weights: float32 [2, 640, 256], P(None, 'grp')
- new_momentum: float32 [2, 640, 256], P(None, 'grp')
- new_input: float32 [2, 640, 640], P(None, 'grp')
- new_output: float32 [256, 256], replicated
Inputs may be any that keep to these rules, and one draw needn't show every extreme that they name: `input_factor`: each block is symmetric positive definite. `output_factor`: symmetric positive definite.
All inputs are finite; a program needn't handle non-finite values.
Results may differ from a plain program's by a relative error of at most 0.0003.
Values sent between devices are 32-bit elements; how exact they have to be, the bound alone decides.
No kernel may reach another device: no remote copies, remote signals or barrier semaphores. Data moves between devices by JAX's collectives and lax.ppermute only.
A program may use at most 64 MiB of HBM per device.

v0:
```python
import jax
import jax.numpy as jnp
from jax import lax
from jax.sharding import PartitionSpec as P

ITERS = 3


damping = 0.1
mom_decay = 0.9
step_size = 0.5


def newton_start(damped, ident):
    squares = jnp.sum(damped * damped, axis=(-2, -1), keepdims=True)
    bound = jnp.sqrt(squares)
    return 2.0 / bound * ident - damped / (bound * bound)


def step_rows(damped_rows, own_rows, full_iterate):
    product = jnp.matmul(damped_rows, full_iterate, precision=lax.Precision.HIGHEST)
    return 2.0 * own_rows - jnp.matmul(product, full_iterate, precision=lax.Precision.HIGHEST)


def on_device(activations, cotangents, input_factor, output_factor, gradient, weights, momentum):
    nblocks, slab, order = input_factor.shape
    rank = output_factor.shape[0]
    tokens = activations.shape[0]
    groups = lax.axis_size("grp")
    samples = tokens * groups * lax.axis_size("own")
    first_row = lax.axis_index("grp") * slab
    split_in = activations.reshape(tokens, nblocks, order)
    stat_in = jnp.einsum("tki,tkj->kij", split_in, split_in, preferred_element_type=jnp.float32)
    stat_out = jnp.einsum("ti,tj->ij", cotangents, cotangents, preferred_element_type=jnp.float32)
    total_in, total_out = lax.psum((stat_in, stat_out), ("grp", "own"))
    share_in = lax.dynamic_slice_in_dim(total_in, first_row, slab, 1)
    new_input = 0.5 * input_factor + 0.5 * (share_in / samples)
    new_output = 0.5 * output_factor + 0.5 * (total_out / samples)
    rows_in = lax.broadcasted_iota(jnp.int32, (slab, order), 0) + first_row
    cols_in = lax.broadcasted_iota(jnp.int32, (slab, order), 1)
    ident_rows = (rows_in == cols_in).astype(jnp.float32)
    ident_out = jnp.eye(rank, dtype=jnp.float32)
    damped_in = new_input + damping * ident_rows
    damped_out = new_output + damping * ident_out
    squares = lax.psum(jnp.sum(damped_in * damped_in, axis=(1, 2), keepdims=True), "grp")
    bound = jnp.sqrt(squares)
    iterate_in = 2.0 / bound * ident_rows - damped_in / (bound * bound)
    start_out = newton_start(damped_out, ident_out)
    out_rows = rank // groups
    first_out = lax.axis_index("grp") * out_rows
    damped_rows = lax.dynamic_slice_in_dim(damped_out, first_out, out_rows, 0)
    iterate_out = lax.dynamic_slice_in_dim(start_out, first_out, out_rows, 0)
    for iteration in range(ITERS - 1):
        full_in, full_out = (
            lax.all_gather(iterate_in, "grp", axis=1, tiled=True),
            lax.all_gather(iterate_out, "grp", axis=0, tiled=True),
        )
        iterate_in = step_rows(damped_in, iterate_in, full_in)
        iterate_out = step_rows(damped_rows, iterate_out, full_out)
    inverse_out = lax.all_gather(iterate_out, "grp", axis=0, tiled=True)
    precond = jnp.einsum(
        "kij,kjr->kir",
        iterate_in,
        lax.all_gather(gradient, "grp", axis=1, tiled=True),
        precision=lax.Precision.HIGHEST,
    )
    update = jnp.einsum("kir,rs->kis", precond, inverse_out, precision=lax.Precision.HIGHEST)
    new_momentum = mom_decay * momentum + update
    new_weights = weights - step_size * new_momentum
    return (new_weights, new_momentum, new_input, new_output)


def solution(mesh):
    placed = (
        P(("grp", "own"), None),
        P(("grp", "own"), None),
        P(None, "grp", None),
        P(),
        P(None, "grp", None),
        P(None, "grp", None),
        P(None, "grp", None),
    )
    return jax.shard_map(
        on_device,
        mesh=mesh,
        in_specs=placed,
        out_specs=(P(None, "grp", None), P(None, "grp", None), P(None, "grp", None), P()),
        check_vma=False,
    )
```

profile of v0, /device:TPU:0, one launch (start us, length us, event | category | flops | bytes accessed | tf_op | source)
XLA Modules:
  0.0 226.5 jit_solution(11742063177105940492)
XLA Ops:
  7.2 0.0 copy-start
  7.2 0.0 all-reduce.3.cloned.1.call-start
  7.2 3.8 %fusion.12 = f32[2,640,640]{2,1,0:T(8,128)} fusion(bf16[32,2,8,640]{3,2,1,0:T(8,128)(2,1)} %bitcast.30), kind=kOutput, calls=%fused_computation.20 | convolution fusion | flops 419430400 | bytes 3932160 | tf_op jit(solution)/shard_map/tki,tkj->kij/dot_general | solution.py:33
  11.0 0.0 copy-done
  11.0 0.9 fusion.24
  11.9 0.0 all-reduce.3.cloned.1.call-update
  12.0 0.0 all-gather.4.cloned.1.call-start
  12.0 0.1 fusion.11
  12.1 0.1 fusion.10
  12.3 144.1 %all-reduce.3.cloned.1.call-done = (f32[2,640,640]{2,1,0:T(8,128)}, f32[256,256]{1,0:T(8,128)}) async-done(((f32[2,640,640]{2,1,0:T(8,128)}, f32[256,256]{1,0:T(8,128)}), (f32[2,640,640]{2,1,0:T(8,128)}, f32[256,256]{1,0:T(8,128)})) %all-reduce.3.cloned.1.call-update) | async-done | bytes 3538960 | tf_op jit(solution)/shard_map/psum | solution.py:35
  156.4 2.4 %multiply_reduce_fusion = (f32[2]{0:T(128)S(1)}, f32[2,320,640]{2,1,0:T(8,128)S(1)}) fusion(f32[320,640]{1,0:T(8,128)S(1)} %fusion.11, f32[2,640,640]{2,1,0:T(8,128)} %get-tuple-element.4, s32[]{:T(128)S(6)} %select_n.7, f32[2,320,640]{2,1,0:T(8,128)} %param.9), kind=kLoop, calls=%fused_computation.5 | loop fusion | flops 2457598 | bytes 5734412 | tf_op jit(solution)/shard_map/reduce_sum | solution.py:45
  158.7 0.0 copy-start.1
  158.7 2.4 %psum.22 = f32[2,1,1]{0,2,1:T(1,128)S(1)} all-reduce(f32[2,1,1]{0,2,1:T(1,128)S(1)} %bitcast.31), channel_id=1, replica_groups=mesh['grp'=2,'own'=16] {'grp'}, use_global_device_ids=true, to_apply=%region_2.0 | all-reduce | flops 2 | bytes 16 | tf_op jit(solution)/shard_map/psum | solution.py:45
  161.2 1.5 divide_subtract_fusion
  162.7 0.0 all-gather.4.cloned.1.call-update
  162.7 0.0 all-gather.6.cloned.1.call-start
  162.8 12.1 %all-gather.4.cloned.1.call-done = f32[2,640,640]{2,1,0:T(8,128)} async-done(((f32[2,320,640]{2,1,0:T(8,128)}), f32[2,640,640]{2,1,0:T(8,128)}) %all-gather.4.cloned.1.call-update) | async-done | bytes 3276816 | tf_op jit(solution)/shard_map/all_gather | solution.py:55
  174.8 0.0 copy-start.3
  174.8 0.0 copy-start.5
  174.8 6.9 %fusion.5 = f32[2,320,640]{2,1,0:T(8,128)S(1)} fusion(f32[2,640,640]{2,1,0:T(8,128)} %all-gather.4.cloned.1.call-done, f32[2,320,640]{2,1,0:T(8,128)S(1)} %get-tuple-element.9, f32[320,640]{1,0:T(8,128)S(1)} %fusion.11), kind=kOutput, calls=%fused_computation.9 | convolution fusion | flops 3146137600 | bytes 7372800 | tf_op jit(solution)/shard_map/dot_general | solution.py:21
  181.7 0.0 copy-done.3
  181.7 0.0 copy-done.5
  181.7 6.0 %multiply_subtract_fusion = f32[2,320,640]{2,1,0:T(8,128)} fusion(f32[2,320,640]{2,1,0:T(8,128)S(1)} %copy-done.3, f32[2,320,640]{2,1,0:T(8,128)S(1)} %fusion.5, f32[2,640,640]{2,1,0:T(8,128)S(1)} %copy-done.5), kind=kOutput, calls=%fused_computation.3 | convolution fusion | flops 3146547200 | bytes 8192000 | tf_op jit(solution)/shard_map/dot_general | solution.py:22
  187.8 0.0 copy-start.9
  187.8 0.0 copy-start.10
  187.8 0.0 all-gather.6.cloned.1.call-update
  187.8 0.0 all-gather.8.cloned.1.call-start
  187.8 0.5 all-gather.8.cloned.1.call-update
  188.4 0.3 copy-done.9
  188.7 0.1 copy-done.10
  188.8 0.7 multiply_reduce_fusion.1
  189.5 0.0 copy-start.6
  190.3 2.0 all_gather.21
  192.3 0.3 fusion.18
  192.6 0.3 convolution_subtract_fusion.1
  192.9 2.0 all_gather.22
  194.9 0.3 fusion.16
  195.1 0.0 copy-done.6
  195.2 0.3 convolution_subtract_fusion
  195.4 2.2 all_gather.23
  197.6 3.8 %all-gather.6.cloned.1.call-done = f32[2,640,640]{2,1,0:T(8,128)} async-done(((f32[2,320,640]{2,1,0:T(8,128)}), f32[2,640,640]{2,1,0:T(8,128)}) %all-gather.6.cloned.1.call-update) | async-done | bytes 3276816 | tf_op jit(solution)/shard_map/all_gather | solution.py:55
  201.4 0.0 copy-done.1
  201.4 0.0 copy-start.4
  201.4 6.9 %fusion.3 = f32[2,320,640]{2,1,0:T(8,128)S(1)} fusion(f32[2,640,640]{2,1,0:T(8,128)} %all-gather.6.cloned.1.call-done, f32[2,320,640]{2,1,0:T(8,128)S(1)} %get-tuple-element.9, f32[320,640]{1,0:T(8,128)S(1)} %fusion.11), kind=kOutput, calls=%fused_computation.7 | convolution fusion | flops 3146137600 | bytes 7372800 | tf_op jit(solution)/shard_map/dot_general | solution.py:21
  208.3 0.0 copy-done.4
  208.3 0.0 copy-start.2
  208.3 5.9 %fusion.23 = f32[2,320,640]{2,1,0:T(8,128)} fusion(f32[2,320,640]{2,1,0:T(8,128)S(1)} %fusion.3, f32[2,640,640]{2,1,0:T(8,128)S(1)} %copy-done.4), kind=kOutput, calls=%fused_computation.40 | convolution fusion | flops 3145728000 | bytes 6553600 | tf_op jit(solution)/shard_map/dot_general | solution.py:22
  214.3 0.0 copy-start.7
  214.3 0.0 all-gather.8.cloned.1.call-done
  214.3 0.0 copy-done.2
  214.3 0.0 copy-start.8
  214.3 3.8 %fusion = f32[2,320,256]{2,1,0:T(8,128)S(1)} fusion(f32[2,640,256]{2,1,0:T(8,128)} %all-gather.8.cloned.1.call-done, f32[2,320,640]{2,1,0:T(8,128)} %fusion.23, f32[2,320,640]{2,1,0:T(8,128)S(1)} %copy-done.2), kind=kOutput, calls=%fused_computation | convolution fusion | flops 1259110400 | bytes 5242880 | tf_op jit(solution)/shard_map/kij,kjr->kir/dot_general | solution.py:61
  218.1 0.0 copy-done.7
  218.1 0.0 copy-done.8
  218.1 1.8 multiply_subtract_fusion.1
  (5 shorter events, 0.1 us)
Async XLA Ops:
  7.2 3.8 %copy-start = (bf16[256,256]{1,0:T(8,128)(2,1)S(1)}, bf16[256,256]{1,0:T(8,128)(2,1)}, u32[]{:S(2)}) copy-start(bf16[256,256]{1,0:T(8,128)(2,1)} %param.8) | copy-start | bytes 393220
  7.2 149.2 %all-reduce.3.cloned.1.call-start = ((), (), s32[]{:S(2)}) async-start(), calls=%async_computation.3 | async-start | bytes 7077888 | tf_op jit(solution)/shard_map/psum | solution.py:35
  12.0 162.9 %all-gather.4.cloned.1.call-start = ((), (), s32[]{:S(2)}) async-start(), calls=%async_computation | async-start | bytes 4915200 | tf_op jit(solution)/shard_map/all_gather | solution.py:55
  158.7 42.7 %copy-start.1 = (f32[2,320,640]{2,1,0:T(8,128)}, f32[2,320,640]{2,1,0:T(8,128)S(1)}, u32[]{:S(2)}) copy-start(f32[2,320,640]{2,1,0:T(8,128)S(1)} %get-tuple-element.9) | copy-start | bytes 4915204
  162.7 38.7 %all-gather.6.cloned.1.call-start = ((), (), s32[]{:S(2)}) async-start(), calls=%async_computation.1 | async-start | bytes 4915200 | tf_op jit(solution)/shard_map/all_gather | solution.py:55
  174.8 6.9 %copy-start.3 = (f32[2,320,640]{2,1,0:T(8,128)S(1)}, f32[2,320,640]{2,1,0:T(8,128)}, u32[]{:S(2)}) copy-start(f32[2,320,640]{2,1,0:T(8,128)} %divide_subtract_fusion) | copy-start | bytes 4915204
  174.8 6.9 %copy-start.5 = (f32[2,640,640]{2,1,0:T(8,128)S(1)}, f32[2,640,640]{2,1,0:T(8,128)}, u32[]{:S(2)}) copy-start(f32[2,640,640]{2,1,0:T(8,128)} %all-gather.4.cloned.1.call-done) | copy-start | bytes 9830404
  187.8 0.9 copy-start.9
  187.8 1.0 copy-start.10
  187.8 26.5 %all-gather.8.cloned.1.call-start = ((), (), s32[]{:S(2)}) async-start(), calls=%async_computation.2 | async-start | bytes 1966080 | tf_op jit(solution)/shard_map/all_gather | solution.py:64
  189.5 5.7 %copy-start.6 = (f32[256,256]{1,0:T(8,128)}, f32[256,256]{1,0:T(8,128)S(1)}, u32[]{:S(2)}) copy-start(f32[256,256]{1,0:T(8,128)S(1)} %get-tuple-element.7) | copy-start | bytes 786436
  201.4 6.9 %copy-start.4 = (f32[2,640,640]{2,1,0:T(8,128)S(1)}, f32[2,640,640]{2,1,0:T(8,128)}, u32[]{:S(2)}) copy-start(f32[2,640,640]{2,1,0:T(8,128)} %all-gather.6.cloned.1.call-done) | copy-start | bytes 9830404
  208.3 6.0 %copy-start.2 = (f32[2,320,640]{2,1,0:T(8,128)S(1)}, f32[2,320,640]{2,1,0:T(8,128)}, u32[]{:S(2)}) copy-start(f32[2,320,640]{2,1,0:T(8,128)} %multiply_subtract_fusion) | copy-start | bytes 4915204
  214.3 3.9 %copy-start.7 = (f32[2,320,256]{2,1,0:T(8,128)S(1)}, f32[2,320,256]{2,1,0:T(8,128)}, u32[]{:S(2)}) copy-start(f32[2,320,256]{2,1,0:T(8,128)} %param.12) | copy-start | bytes 1966084
  214.3 3.9 %copy-start.8 = (f32[2,320,256]{2,1,0:T(8,128)S(1)}, f32[2,320,256]{2,1,0:T(8,128)}, u32[]{:S(2)}) copy-start(f32[2,320,256]{2,1,0:T(8,128)} %param.13) | copy-start | bytes 1966084
Sparse Core Ops, SparseCore 0:
  14.1 142.1 all-reduce.2
  162.8 11.9 all-gather.3
  187.9 13.4 all-gather.5
  202.8 10.5 all-gather.7
where the time goes:
time: 227 us; the launch traced here: 226 us
  waiting for transfers between devices  161 us (71%)
  matrix products  37.1 us (16%)
  between operations  14.7 us (6%)
  blocking collectives  8.61 us (4%)
  other arithmetic  4.87 us (2%)
    psum x1, waiting for transfers between devices, on_device(): total_in, total_out = lax.psum((stat_in, stat_out), ('grp', 'own'))  144 us
    all_gather x2, waiting for transfers between devices, on_device(): lax.all_gather(iterate_in, 'grp', axis=1, tiled=True)  15.9 us
    dot_general x4, matrix products, step_rows(): jnp.matmul(damped_rows, full_iterate, precision=lax.Precision.HIGHEST)  14.3 us
    dot_general x4, matrix products, step_rows(): jnp.matmul(product, full_iterate, precision=lax.Precision.HIGHEST)  12.5 us
  transfers between devices with their start and end apart: 4, of which 3 were waited for; matrix products, arithmetic and copies ran while one was open for 7% of the time, Pallas kernels for 0%

commit v1 on v0

--- a/solution.py
+++ b/solution.py
@@ -1,6 +1,8 @@
 import jax
 import jax.numpy as jnp
 from jax import lax
+from jax.experimental import pallas as pl
+from jax.experimental.pallas import tpu as pltpu
 from jax.sharding import PartitionSpec as P
 
 ITERS = 3
@@ -9,6 +11,10 @@
 damping = 0.1
 mom_decay = 0.9
 step_size = 0.5
+
+LANES = 128
+SUBS = 8
+SHARDS = 16
 
 
 def newton_start(damped, ident):
@@ -22,7 +28,7 @@
     return 2.0 * own_rows - jnp.matmul(product, full_iterate, precision=lax.Precision.HIGHEST)
 
 
-def on_device(activations, cotangents, input_factor, output_factor, gradient, weights, momentum):
+def any_mesh(activations, cotangents, input_factor, output_factor, gradient, weights, momentum):
     nblocks, slab, order = input_factor.shape
     rank = output_factor.shape[0]
     tokens = activations.shape[0]
@@ -70,6 +76,197 @@
     return (new_weights, new_momentum, new_input, new_output)
 
 
+def split(value):
+    high = value.astype(jnp.bfloat16)
+    low = (value - high.astype(jnp.float32)).astype(jnp.bfloat16)
+    return high, low
+
+
+def mul(a, b):
+    return jnp.dot(a, b, preferred_element_type=jnp.float32)
+
+
+def mul3(a, b):
+    return mul(a[0], b[0]) + (mul(a[0], b[1]) + mul(a[1], b[0]))
+
+
+def tile_pairs(tiles):
+    return [(i, j) for i in range(tiles) for j in range(i, tiles)]
+
+
+def stats_kernel(where_ref, act_ref, cot_ref, packed_ref):
+    block, me = where_ref[0], where_ref[1]
+    rank = cot_ref.shape[1]
+    share = rank // 2
+    order = act_ref.shape[1] // 2
+    tiles = order // LANES
+    places = [jnp.bitwise_xor(me, s) for s in range(SHARDS)]
+
+    def put(index, tile):
+        for s in range(SHARDS):
+            packed_ref[places[s], index] = tile[s * SUBS : (s + 1) * SUBS]
+
+    act = act_ref[:, pl.ds(pl.multiple_of(block * order, LANES), order)]
+    turned = act.T
+    index = 0
+    for i in range(tiles):
+        strip = mul(turned[i * LANES : (i + 1) * LANES], act[:, i * LANES :])
+        for j in range(tiles - i):
+            put(index, strip[:, j * LANES : (j + 1) * LANES])
+            index += 1
+    cot = cot_ref[:, pl.ds(pl.multiple_of(block * share, LANES), share)]
+    strip = mul(cot.T, cot_ref[...])
+    for i in range(share // LANES):
+        for j in range(rank // LANES):
+            put(index, strip[i * LANES : (i + 1) * LANES, j * LANES : (j + 1) * LANES])
+            index += 1
+
+
+def input_kernel(where_ref, near_ref, far_ref, fac_ref, fac_far_ref, grad_ref, grad_far_ref,
+                 mine_ref, theirs_ref, left_ref, out_ref, stat_ref, fac_scr, grad_scr, *, scale):
+    block, me = where_ref[0], where_ref[1]
+    slab, order = fac_far_ref.shape
+    tiles = order // LANES
+    own_rows = pl.ds(pl.multiple_of(block * slab, SUBS), slab)
+    far_rows = pl.ds(pl.multiple_of((1 - block) * slab, SUBS), slab)
+    for place in range(SHARDS):
+        rows = pl.ds(pl.multiple_of(jnp.bitwise_xor(me, place) * SUBS, SUBS), SUBS)
+        half = SHARDS // 2
+        stat_ref[:, rows, :] = near_ref[place] if place < half else far_ref[place - half]
+    fac_scr[own_rows, :] = 0.5 * fac_ref[block]
+    fac_scr[far_rows, :] = 0.5 * fac_far_ref[...]
+    grad_scr[own_rows, :] = grad_ref[block]
+    grad_scr[far_rows, :] = grad_far_ref[...]
+    pairs = tile_pairs(tiles)
+    for index, (i, j) in enumerate(pairs):
+        at = lambda n: slice(n * LANES, (n + 1) * LANES)
+        part = 0.5 * (stat_ref[index] * scale)
+        fac_scr[at(i), at(j)] += part
+        if i != j:
+            fac_scr[at(j), at(i)] += part.T
+    mine_ref[...] = fac_scr[own_rows, :]
+    theirs_ref[...] = fac_scr[far_rows, :]
+    lead = out_ref.shape[0] // LANES
+    count = out_ref.shape[1] // LANES
+    for n in range(lead * count):
+        i, j = n // count, n % count
+        out_ref[i * LANES : (i + 1) * LANES, j * LANES : (j + 1) * LANES] = stat_ref[len(pairs) + n]
+    rows = lax.broadcasted_iota(jnp.int32, (order, order), 0)
+    cols = lax.broadcasted_iota(jnp.int32, (order, order), 1)
+    damped = fac_scr[...] + jnp.where(rows == cols, damping, 0.0)
+    squares = jnp.sum(jnp.sum(damped * damped, axis=0, keepdims=True), axis=1, keepdims=True)
+    over = 1.0 / jnp.sqrt(squares)
+    scaled = damped * over
+    first = split(scaled)
+    twice = split(2.0 * scaled - mul3(first, first))
+    grad = grad_scr[...]
+    grad = 2.0 * grad - mul3(first, split(grad))
+    grad = 2.0 * grad - mul3(twice, split(grad))
+    once = grad - mul3(twice, split(grad))
+    left_ref[...] = (grad + once - mul3(twice, split(once))) * over
+
+
+def output_kernel(where_ref, stat_ref, stat_far_ref, fac_ref, left_ref, new_ref, mine_ref, theirs_ref, *, scale):
+    block = where_ref[0]
+    share, rank = stat_ref.shape
+    slab = mine_ref.shape[0]
+    own = pl.ds(pl.multiple_of(block * share, SUBS), share)
+    far = pl.ds(pl.multiple_of((1 - block) * share, SUBS), share)
+    new_ref[own, :] = 0.5 * fac_ref[own, :] + 0.5 * (stat_ref[...] * scale)
+    new_ref[far, :] = 0.5 * fac_ref[far, :] + 0.5 * (stat_far_ref[...] * scale)
+    rows = lax.broadcasted_iota(jnp.int32, (rank, rank), 0)
+    cols = lax.broadcasted_iota(jnp.int32, (rank, rank), 1)
+    damped = new_ref[...] + jnp.where(rows == cols, damping, 0.0)
+    squares = jnp.sum(jnp.sum(damped * damped, axis=0, keepdims=True), axis=1, keepdims=True)
+    over = 1.0 / jnp.sqrt(squares)
+    scaled = damped * over
+    first = split(scaled)
+    twice = 2.0 * scaled - mul3(first, first)
+    second = split(twice)
+    fourth = split(2.0 * twice - mul3(second, second))
+    head = jnp.where(rows == cols, 4.0, 0.0) - 2.0 * (scaled + twice) + mul3(first, second)
+    inverse = split((2.0 * head - mul3(split(head), fourth)) * over)
+    far_left = split(left_ref[pl.ds(pl.multiple_of((1 - block) * slab, SUBS), slab), :])
+    theirs_ref[...] = mul3(far_left, inverse)
+    own_left = split(left_ref[pl.ds(pl.multiple_of(block * slab, SUBS), slab), :])
+    mine_ref[...] = mul3(own_left, inverse)
+
+
+def call(kernel, where, args, outs, scratch=()):
+    return pl.pallas_call(
+        kernel,
+        out_shape=[jax.ShapeDtypeStruct(shape, jnp.float32) for shape in outs],
+        in_specs=[pl.BlockSpec(memory_space=pltpu.SMEM)]
+        + [pl.BlockSpec(memory_space=pltpu.VMEM)] * len(args),
+        out_specs=[pl.BlockSpec(memory_space=pltpu.VMEM)] * len(outs),
+        scratch_shapes=[pltpu.VMEM(shape, jnp.float32) for shape in scratch],
+    )(where, *args)
+
+
+def on_chip_pairs(activations, cotangents, input_factor, output_factor, gradient, weights, momentum):
+    nblocks, slab, order = input_factor.shape
+    rank = output_factor.shape[0]
+    group = lax.axis_index("grp")
+    spot = lax.axis_index("own")
+    peers = lax.axis_size("own")
+    samples = activations.shape[0] * lax.axis_size("grp") * peers
+    scale = 1.0 / samples
+    x_bit, y_bit, z_bits = spot % 2, (spot // 2) % 2, spot // 4
+    straight = x_bit * 8 + y_bit * 4 + z_bits
+    crossed = y_bit * 8 + x_bit * 4 + z_bits
+    me = jnp.where(group == 0, straight, crossed)
+    partner = jnp.where(group == 0, crossed, straight)
+    where_mine = jnp.stack([group, me]).astype(jnp.int32)
+    where_theirs = jnp.stack([1 - group, partner]).astype(jnp.int32)
+    ntiles = len(tile_pairs(order // LANES)) + (rank // 2 // LANES) * (rank // LANES)
+    packed = (SHARDS, ntiles, SUBS, LANES)
+
+    def swap(value):
+        return lax.ppermute(value, "grp", [(0, 1), (1, 0)])
+
+    def send(value, flips):
+        pairs = [(g * peers + o, g * peers + (o ^ flips[g])) for g in range(2) for o in range(peers)]
+        return lax.ppermute(value, ("grp", "own"), pairs)
+
+    (theirs,) = call(stats_kernel, where_theirs, (activations, cotangents), [packed])
+    arrived = swap(theirs)
+    (held,) = call(stats_kernel, where_mine, (activations, cotangents), [packed])
+    fac_far = swap(lax.dynamic_index_in_dim(input_factor, 1 - group, 0, False))
+    grad_far = swap(lax.dynamic_index_in_dim(gradient, 1 - group, 0, False))
+
+    arrived = send(held[8:] + arrived[8:], (1, 2)), held[:8] + arrived[:8]
+    low = send(arrived[0][4:] + arrived[1][4:], (2, 1)), arrived[0][:4] + arrived[1][:4]
+    quarter = low[0] + low[1]
+    pieces = [send(quarter[d : d + 1], (4 * d, 4 * d)) for d in (3, 2, 1)]
+    total = quarter[:1] + pieces[0] + pieces[1] + pieces[2]
+    gathered = {d: send(total, (4 * d, 4 * d)) for d in (3, 2, 1)}
+    quarter = jnp.concatenate([total, gathered[1], gathered[2], gathered[3]], 0)
+    near = jnp.concatenate([quarter, send(quarter, (2, 1))], 0)
+    far = send(near, (1, 2))
+
+    mine, theirs, left, out_share = call(
+        lambda *refs: input_kernel(*refs, scale=scale),
+        where_mine,
+        (near, far, input_factor, fac_far, gradient, grad_far),
+        [(slab, order), (slab, order), (order, rank), (rank // 2, rank)],
+        [(ntiles, LANES, LANES), (order, order), (order, rank)],
+    )
+    out_far = swap(out_share)
+    rows_far = swap(theirs)
+    new_output, update, update_far = call(
+        lambda *refs: output_kernel(*refs, scale=scale),
+        where_mine,
+        (out_share, out_far, output_factor, left),
+        [(rank, rank), (slab, rank), (slab, rank)],
+    )
+    update_far = swap(update_far)
+    own_block = lax.broadcasted_iota(jnp.int32, (nblocks, 1, 1), 0) == group
+    new_input = jnp.where(own_block, mine[None], rows_far[None])
+    new_momentum = mom_decay * momentum + jnp.where(own_block, update[None], update_far[None])
+    new_weights = weights - step_size * new_momentum
+    return (new_weights, new_momentum, new_input, new_output)
+
+
 def solution(mesh):
     placed = (
         P(("grp", "own"), None),
@@ -80,6 +277,14 @@
         P(None, "grp", None),
         P(None, "grp", None),
     )
+
+    def on_device(*args):
+        nblocks, slab, order = args[2].shape
+        rank = args[3].shape[0]
+        fits = nblocks == 2 and order % LANES == 0 and slab % SUBS == 0 and rank % (2 * LANES) == 0
+        paired = mesh.shape["grp"] == 2 and mesh.shape["own"] == SHARDS
+        return (on_chip_pairs if fits and paired else any_mesh)(*args)
+
     return jax.shard_map(
         on_device,
         mesh=mesh,

time: 227 us -> 88.9 us (0.39)
  waiting for transfers between devices: 161 us -> 40.4 us
  matrix products: 37.1 us -> 0 us
  Pallas kernels: 0 us -> 21.3 us
  starting transfers between devices: 0.16 us -> 18.3 us
  between operations: 14.7 us -> 0.81 us
  blocking collectives: 8.61 us -> 0 us
    psum x1 -> x0, waiting for transfers between devices: 144 us -> none  [on_device(): total_in, total_out = lax.psum((stat_in, stat_out), ('grp', 'own'))]
    ppermute x0 -> x16, waiting for transfers between devices: none -> 40.4 us  [the longest x10 34.8 us: send(): return lax.ppermute(value, ('grp', 'own'), pairs)]
    dot_general x12 -> x0, matrix products: 37.1 us -> none  [the longest x4 14.3 us: step_rows(): jnp.matmul(damped_rows, full_iterate, precision=lax.Precision.HIGHEST)]
    pallas_call x0 -> x4, Pallas kernels: none -> 21.3 us  [call(): pl.pallas_call(kernel, out_shape=[jax.ShapeDtypeStruct(shape, jnp.float32...]
    ppermute x0 -> x16, starting transfers between devices: none -> 18.3 us  [the longest x10 17 us: send(): return lax.ppermute(value, ('grp', 'own'), pairs)]
    all_gather x3 -> x0, waiting for transfers between devices: 15.9 us -> none  [the longest x2 15.9 us: on_device(): lax.all_gather(iterate_in, 'grp', axis=1, tiled=True)]
    all_gather x3 -> x0, blocking collectives: 6.16 us -> none  [the longest x2 3.99 us: on_device(): lax.all_gather(iterate_out, 'grp', axis=0, tiled=True)]
    reduce_sum x2 -> x0, other arithmetic: 3.05 us -> none  [the longest x1 2.38 us: on_device(): jnp.sum(damped_in * damped_in, axis=(1, 2), keepdims=True)]
  transfers between devices with their start and end apart: 4 -> 16, of which waited for: 3 -> 11; matrix products, arithmetic and copies ran while one was open for 7% -> 3% of each run, Pallas kernels for 0% -> 7%
where the time goes in v1:
time: 88.9 us; the launch traced here: 88.7 us
  waiting for transfers between devices  40.4 us (45%)
  Pallas kernels  21.3 us (24%)
  starting transfers between devices  18.3 us (21%)
  other arithmetic  6.3 us (7%)
  local copies, waits for them, and re-layouts  1.61 us (2%)
    ppermute x10, waiting for transfers between devices, send(): return lax.ppermute(value, ('grp', 'own'), pairs)  34.8 us
    pallas_call x4, Pallas kernels, call(): pl.pallas_call(kernel, out_shape=[jax.ShapeDtypeStruct(shape, jnp.float32...  21.3 us
    ppermute x10, starting transfers between devices, send(): return lax.ppermute(value, ('grp', 'own'), pairs)  17 us
    ppermute x6, waiting for transfers between devices, swap(): return lax.ppermute(value, 'grp', [(0, 1), (1, 0)])  5.54 us
    sub x1, other arithmetic, on_chip_pairs(): new_weights = weights - step_size * new_momentum  2.3 us
  transfers between devices with their start and end apart: 16, of which 11 were waited for; matrix products, arithmetic and copies ran while one was open for 3% of the time, Pallas kernels for 7%

profile of v1, /device:TPU:0, one launch (start us, length us, event | category | flops | bytes accessed | tf_op | source)
XLA Modules:
  0.0 88.7 jit_solution(4468487593291825106)
XLA Ops:
  0.7 0.6 pad_add_fusion.1.where_ref
  1.3 2.5 %shard_map.103 = f32[16,17,8,128]{3,2,1,0:T(8,128)} custom-call(s32[2]{0:T(128)} %pad_add_fusion.1.where_ref, bf16[256,1280]{1,0:T(8,128)(2,1)} %act_ref.3, bf16[256,256]{1,0:T(8,128)(2,1)} %cot_ref.3), custom_call_target="tpu_custom_call" | custom-call | tf_op jit(solution)/shard_map/pallas_call | solution.py:196
  3.8 0.5 collective-permute-start
  4.3 0.6 pad_add_fusion.where_ref.refs_0_
  4.8 2.5 %shard_map.102 = f32[16,17,8,128]{3,2,1,0:T(8,128)} custom-call(s32[2]{0:T(128)} %pad_add_fusion.where_ref.refs_0_, bf16[256,1280]{1,0:T(8,128)(2,1)} %act_ref.3, bf16[256,256]{1,0:T(8,128)(2,1)} %cot_ref.3), custom_call_target="tpu_custom_call" | custom-call | tf_op jit(solution)/shard_map/pallas_call | solution.py:196
  7.4 0.0 collective-permute-done
  7.4 1.3 %slice_add_fusion.1 = (f32[8,17,8,128]{3,2,1,0:T(8,128)S(1)}, f32[8,17,8,128]{3,2,1,0:T(8,128)S(1)}) fusion(f32[16,17,8,128]{3,2,1,0:T(8,128)S(1)} %collective-permute-done, f32[16,17,8,128]{3,2,1,0:T(8,128)} %shard_map.102), kind=kLoop, calls=%fused_computation.5 | loop fusion | flops 278528 | bytes 3342336 | tf_op jit(solution)/shard_map/add | solution.py:237
  8.7 0.0 copy-start
  8.7 2.5 %collective-permute-start.1 = (f32[8,17,8,128]{3,2,1,0:T(8,128)S(1)}, f32[8,17,8,128]{3,2,1,0:T(8,128)S(1)}, u32[]{:S(2)}, u32[]{:S(2)}) collective-permute-start(f32[8,17,8,128]{3,2,1,0:T(8,128)S(1)} %get-tuple-element.22), channel_id=1, source_target_pairs={{0,1},{1,0},{2,3},{3,2},{4,5},{5,4},{6,7},{7,6},{8,9},{9,8},{10,11... | collective-permute-start | bytes 1671176 | tf_op jit(solution)/shard_map/ppermute | solution.py:229
  11.3 7.5 %collective-permute-done.1 = f32[8,17,8,128]{3,2,1,0:T(8,128)S(1)} collective-permute-done((f32[8,17,8,128]{3,2,1,0:T(8,128)S(1)}, f32[8,17,8,128]{3,2,1,0:T(8,128)S(1)}, u32[]{:S(2)}, u32[]{:S(2)}) %collective-permute-start.1) | collective-permute-done | bytes 557088 | tf_op jit(solution)/shard_map/ppermute | solution.py:229
  18.8 2.1 %collective-permute-start.2 = (f32[4,17,8,128]{3,2,1,0:T(8,128)S(1)}, f32[4,17,8,128]{3,2,1,0:T(8,128)S(1)}, u32[]{:S(2)}, u32[]{:S(2)}) collective-permute-start(f32[4,17,8,128]{3,2,1,0:T(8,128)S(1)} %slice_add_fusion.3), channel_id=1, source_target_pairs={{0,2},{1,3},{2,0},{3,1},{4,6},{5,7},{6,4},{7,5},{8,10},{9,11},{10,... | collective-permute-start | bytes 835592 | tf_op jit(solution)/shard_map/ppermute | solution.py:229
  20.9 4.5 %collective-permute-done.2 = f32[4,17,8,128]{3,2,1,0:T(8,128)S(1)} collective-permute-done((f32[4,17,8,128]{3,2,1,0:T(8,128)S(1)}, f32[4,17,8,128]{3,2,1,0:T(8,128)S(1)}, u32[]{:S(2)}, u32[]{:S(2)}) %collective-permute-start.2) | collective-permute-done | bytes 278560 | tf_op jit(solution)/shard_map/ppermute | solution.py:229
  25.4 0.1 fusion
  25.5 4.2 %collective-permute-start.3 = (f32[1,17,8,128]{3,2,1,0:T(8,128)S(1)}, f32[1,17,8,128]{3,2,1,0:T(8,128)S(1)}, u32[]{:S(2)}, u32[]{:S(2)}) collective-permute-start(f32[1,17,8,128]{3,2,1,0:T(8,128)S(1)} %get-tuple-element.24), channel_id=1, source_target_pairs={{0,12},{1,13},{2,14},{3,15},{4,8},{5,9},{6,10},{7,11},{8,4},{9,5},... | collective-permute-start | bytes 208904 | tf_op jit(solution)/shard_map/ppermute | solution.py:229
  29.7 0.0 collective-permute-start.4
  29.7 0.6 collective-permute-start.5
  30.3 2.0 %collective-permute-done.3 = f32[1,17,8,128]{3,2,1,0:T(8,128)S(1)} collective-permute-done((f32[1,17,8,128]{3,2,1,0:T(8,128)S(1)}, f32[1,17,8,128]{3,2,1,0:T(8,128)S(1)}, u32[]{:S(2)}, u32[]{:S(2)}) %collective-permute-start.3) | collective-permute-done | bytes 69664 | tf_op jit(solution)/shard_map/ppermute | solution.py:229
  32.3 2.8 %collective-permute-done.4 = f32[1,17,8,128]{3,2,1,0:T(8,128)S(1)} collective-permute-done((f32[1,17,8,128]{3,2,1,0:T(8,128)S(1)}, f32[1,17,8,128]{3,2,1,0:T(8,128)S(1)}, u32[]{:S(2)}, u32[]{:S(2)}) %collective-permute-start.4) | collective-permute-done | bytes 69664 | tf_op jit(solution)/shard_map/ppermute | solution.py:229
  35.1 0.0 collective-permute-done.5
  35.2 0.0 copy-start.1
  35.2 0.5 collective-permute-start.6
  35.7 2.4 %collective-permute-start.7 = (f32[1,17,8,128]{3,2,1,0:T(8,128)S(1)}, f32[1,17,8,128]{3,2,1,0:T(8,128)S(1)}, u32[]{:S(2)}, u32[]{:S(2)}) collective-permute-start(f32[1,17,8,128]{3,2,1,0:T(8,128)S(1)} %get-tuple-element.21), channel_id=1, source_target_pairs={{0,8},{1,9},{2,10},{3,11},{4,12},{5,13},{6,14},{7,15},{8,0},{9,1},... | collective-permute-start | bytes 208904 | tf_op jit(solution)/shard_map/ppermute | solution.py:229
  38.1 1.6 %collective-permute-start.8 = (f32[1,17,8,128]{3,2,1,0:T(8,128)S(1)}, f32[1,17,8,128]{3,2,1,0:T(8,128)S(1)}, u32[]{:S(2)}, u32[]{:S(2)}) collective-permute-start(f32[1,17,8,128]{3,2,1,0:T(8,128)S(1)} %get-tuple-element.21), channel_id=1, source_target_pairs={{0,12},{1,13},{2,14},{3,15},{4,8},{5,9},{6,10},{7,11},{8,4},{9,5},... | collective-permute-start | bytes 208904 | tf_op jit(solution)/shard_map/ppermute | solution.py:229
  39.6 0.0 copy-done
  39.6 0.1 dynamic-slice_bitcast_fusion
  39.7 0.1 collective-permute-start.11
  39.8 0.0 collective-permute-done.6
  39.8 2.3 %collective-permute-done.7 = f32[1,17,8,128]{3,2,1,0:T(8,128)S(1)} collective-permute-done((f32[1,17,8,128]{3,2,1,0:T(8,128)S(1)}, f32[1,17,8,128]{3,2,1,0:T(8,128)S(1)}, u32[]{:S(2)}, u32[]{:S(2)}) %collective-permute-start.7) | collective-permute-done | bytes 69664 | tf_op jit(solution)/shard_map/ppermute | solution.py:229
  42.1 2.1 %collective-permute-done.8 = f32[1,17,8,128]{3,2,1,0:T(8,128)S(1)} collective-permute-done((f32[1,17,8,128]{3,2,1,0:T(8,128)S(1)}, f32[1,17,8,128]{3,2,1,0:T(8,128)S(1)}, u32[]{:S(2)}, u32[]{:S(2)}) %collective-permute-start.8) | collective-permute-done | bytes 69664 | tf_op jit(solution)/shard_map/ppermute | solution.py:229
  44.2 1.6 %collective-permute-start.9 = (f32[4,17,8,128]{3,2,1,0:T(8,128)S(1)}, f32[4,17,8,128]{3,2,1,0:T(8,128)S(1)}, u32[]{:S(2)}, u32[]{:S(2)}) collective-permute-start(f32[4,17,8,128]{3,2,1,0:T(8,128)S(1)} %pad_maximum_fusion), channel_id=1, source_target_pairs={{0,2},{1,3},{2,0},{3,1},{4,6},{5,7},{6,4},{7,5},{8,10},{9,11},{10,... | collective-permute-start | bytes 835592 | tf_op jit(solution)/shard_map/ppermute | solution.py:229
  45.8 7.3 %collective-permute-done.9 = f32[4,17,8,128]{3,2,1,0:T(8,128)S(1)} collective-permute-done((f32[4,17,8,128]{3,2,1,0:T(8,128)S(1)}, f32[4,17,8,128]{3,2,1,0:T(8,128)S(1)}, u32[]{:S(2)}, u32[]{:S(2)}) %collective-permute-start.9) | collective-permute-done | bytes 278560 | tf_op jit(solution)/shard_map/ppermute | solution.py:229
  53.1 0.0 copy-start.4
  53.1 1.5 %collective-permute-start.10 = (f32[8,17,8,128]{3,2,1,0:T(8,128)S(1)}, f32[8,17,8,128]{3,2,1,0:T(8,128)S(1)}, u32[]{:S(2)}, u32[]{:S(2)}) collective-permute-start(f32[8,17,8,128]{3,2,1,0:T(8,128)S(1)} %constant_dynamic-update-slice_fusion.refs_1_), channel_id=1, source_target_pairs={{0,1},{1,0},{2,3},{3,2},{4,5},{5,4},{6,7},{7,6},{8,9},{9,8},{10,11... | collective-permute-start | bytes 1671176 | tf_op jit(solution)/shard_map/ppermute | solution.py:229
  54.7 0.0 copy-done.1
  54.7 0.1 collective-permute-start.12
  54.8 1.6 %collective-permute-done.12.refs_6_ = f32[320,256]{1,0:T(8,128)S(1)} collective-permute-done((f32[320,256]{1,0:T(8,128)S(1)}, f32[320,256]{1,0:T(8,128)S(1)}, u32[]{:S(2)}, u32[]{:S(2)}) %collective-permute-start.12) | collective-permute-done | bytes 327712 | tf_op jit(solution)/shard_map/ppermute | solution.py:225
  56.4 0.0 copy-start.8
  56.4 0.0 collective-permute-done.11.refs_4_
  56.4 0.0 copy-start.2
  56.4 6.3 %collective-permute-done.10.refs_2_ = f32[8,17,8,128]{3,2,1,0:T(8,128)S(1)} collective-permute-done((f32[8,17,8,128]{3,2,1,0:T(8,128)S(1)}, f32[8,17,8,128]{3,2,1,0:T(8,128)S(1)}, u32[]{:S(2)}, u32[]{:S(2)}) %collective-permute-start.10) | collective-permute-done | bytes 557088 | tf_op jit(solution)/shard_map/ppermute | solution.py:229
  62.7 0.0 copy-done.4
  62.7 0.0 copy-done.8
  62.7 0.0 copy-done.2
  62.7 0.0 copy-start.7
  62.7 0.8 copy-done.7
  63.5 0.0 copy-start.6
  63.5 12.5 %shard_map.104 = (f32[320,640]{1,0:T(8,128)}, f32[320,640]{1,0:T(8,128)}, f32[640,256]{1,0:T(8,128)}, f32[128,256]{1,0:T(8,128)}) custom-call(s32[2]{0:T(128)} %pad_add_fusion.where_ref.refs_0_, f32[8,17,8,128]{3,2,1,0:T(8,128)} %copy-done.4, f32[8,17,8,128]{3,2,1,0:T(8,128)} %copy-done.7, f32[2,320,640]{2,1,0:T(8,128)} %refs_3_.2, f32[320,640]{1,0:T(8,128)} %copy-done.2, ...), custom_call_target="tpu_custom_call" | custom-call | tf_op jit(solution)/shard_map/pallas_call | solution.py:196
  76.0 0.0 copy-start.5
  76.0 0.0 collective-permute-start.15
  76.0 0.5 collective-permute-start.13
  76.5 2.2 %collective-permute-done.13.refs_2_ = f32[128,256]{1,0:T(8,128)S(1)} collective-permute-done((f32[128,256]{1,0:T(8,128)}, f32[128,256]{1,0:T(8,128)S(1)}, u32[]{:S(2)}, u32[]{:S(2)}) %collective-permute-start.13) | collective-permute-done | bytes 131104 | tf_op jit(solution)/shard_map/ppermute | solution.py:225
  78.8 0.0 copy-start.9
  78.8 0.6 copy-done.9
  79.4 3.8 %shard_map.105 = (f32[256,256]{1,0:T(8,128)}, f32[320,256]{1,0:T(8,128)}, f32[320,256]{1,0:T(8,128)}) custom-call(s32[2]{0:T(128)} %pad_add_fusion.where_ref.refs_0_, f32[128,256]{1,0:T(8,128)} %get-tuple-element.11.refs_1_, f32[128,256]{1,0:T(8,128)} %copy-done.9, f32[256,256]{1,0:T(8,128)} %refs_3_.3, f32[640,256]{1,0:T(8,128)} %get-tuple-element.12.refs_4_), custom_call_target="tpu_custom_call" | custom-call | tf_op jit(solution)/shard_map/pallas_call | solution.py:196
  83.2 0.1 collective-permute-start.14
  83.3 1.7 %collective-permute-done.14 = f32[320,256]{1,0:T(8,128)S(1)} collective-permute-done((f32[320,256]{1,0:T(8,128)}, f32[320,256]{1,0:T(8,128)S(1)}, u32[]{:S(2)}, u32[]{:S(2)}) %collective-permute-start.14) | collective-permute-done | bytes 327712 | tf_op jit(solution)/shard_map/ppermute | solution.py:225
  85.0 0.0 copy-done.6
  85.0 0.0 copy-done.5
  85.0 0.0 copy-start.3
  85.0 2.3 %multiply_subtract_fusion = (f32[2,320,256]{2,1,0:T(8,128)}, f32[2,320,256]{2,1,0:T(8,128)}) fusion(f32[2,320,256]{2,1,0:T(8,128)S(1)} %copy-done.5, f32[320,256]{1,0:T(8,128)S(1)} %collective-permute-done.14, f32[320,256]{1,0:T(8,128)} %get-tuple-element.13, pred[2]{0:T(512)(128)(4,1)S(1)} %iota_compare_fusion, f32[2,320,256]{2,1,0:T(8,128)S(1)} %copy-done.6), kind=kLoop, calls=%fused_computation.2 | loop fusion | flops 819200 | bytes 3276802 | tf_op jit(solution)/shard_map/sub | solution.py:266
  87.3 0.0 collective-permute-done.15
  87.3 0.0 copy-done.3
  87.3 1.3 %broadcast_select_fusion = f32[2,320,640]{2,1,0:T(8,128)} fusion(f32[320,640]{1,0:T(8,128)S(1)} %collective-permute-done.15, f32[320,640]{1,0:T(8,128)S(1)} %copy-done.3, pred[2]{0:T(512)(128)(4,1)S(1)} %iota_compare_fusion), kind=kLoop, calls=%fused_computation | loop fusion | flops 409600 | bytes 3276802 | tf_op jit(solution)/shard_map/jit(_where)/select_n | solution.py:264
  (10 shorter events, 0.2 us)
Async XLA Ops:
  3.8 3.6 %collective-permute-start = (f32[16,17,8,128]{3,2,1,0:T(8,128)}, f32[16,17,8,128]{3,2,1,0:T(8,128)S(1)}, u32[]{:S(2)}, u32[]{:S(2)}) collective-permute-start(f32[16,17,8,128]{3,2,1,0:T(8,128)} %shard_map.103), channel_id=1, source_target_pairs={{0,16},{16,0},{1,17},{17,1},{2,18},{18,2},{3,19},{19,3},{4,20},{20... | collective-permute-start | bytes 3342344 | tf_op jit(solution)/shard_map/ppermute | solution.py:225
  8.7 30.9 %copy-start = (f32[2,320,640]{2,1,0:T(8,128)S(1)}, f32[2,320,640]{2,1,0:T(8,128)}, u32[]{:S(2)}) copy-start(f32[2,320,640]{2,1,0:T(8,128)} %refs_3_.2) | copy-start | bytes 4915204
  8.7 10.0 %collective-permute-start.1 = (f32[8,17,8,128]{3,2,1,0:T(8,128)S(1)}, f32[8,17,8,128]{3,2,1,0:T(8,128)S(1)}, u32[]{:S(2)}, u32[]{:S(2)}) collective-permute-start(f32[8,17,8,128]{3,2,1,0:T(8,128)S(1)} %get-tuple-element.22), channel_id=1, source_target_pairs={{0,1},{1,0},{2,3},{3,2},{4,5},{5,4},{6,7},{7,6},{8,9},{9,8},{10,11... | collective-permute-start | bytes 1671176 | tf_op jit(solution)/shard_map/ppermute | solution.py:229
  18.8 6.6 %collective-permute-start.2 = (f32[4,17,8,128]{3,2,1,0:T(8,128)S(1)}, f32[4,17,8,128]{3,2,1,0:T(8,128)S(1)}, u32[]{:S(2)}, u32[]{:S(2)}) collective-permute-start(f32[4,17,8,128]{3,2,1,0:T(8,128)S(1)} %slice_add_fusion.3), channel_id=1, source_target_pairs={{0,2},{1,3},{2,0},{3,1},{4,6},{5,7},{6,4},{7,5},{8,10},{9,11},{10,... | collective-permute-start | bytes 835592 | tf_op jit(solution)/shard_map/ppermute | solution.py:229
  25.5 6.8 %collective-permute-start.3 = (f32[1,17,8,128]{3,2,1,0:T(8,128)S(1)}, f32[1,17,8,128]{3,2,1,0:T(8,128)S(1)}, u32[]{:S(2)}, u32[]{:S(2)}) collective-permute-start(f32[1,17,8,128]{3,2,1,0:T(8,128)S(1)} %get-tuple-element.24), channel_id=1, source_target_pairs={{0,12},{1,13},{2,14},{3,15},{4,8},{5,9},{6,10},{7,11},{8,4},{9,5},... | collective-permute-start | bytes 208904 | tf_op jit(solution)/shard_map/ppermute | solution.py:229
  29.7 5.4 %collective-permute-start.4 = (f32[1,17,8,128]{3,2,1,0:T(8,128)S(1)}, f32[1,17,8,128]{3,2,1,0:T(8,128)S(1)}, u32[]{:S(2)}, u32[]{:S(2)}) collective-permute-start(f32[1,17,8,128]{3,2,1,0:T(8,128)S(1)} %get-tuple-element.26), channel_id=1, source_target_pairs={{0,8},{1,9},{2,10},{3,11},{4,12},{5,13},{6,14},{7,15},{8,0},{9,1},... | collective-permute-start | bytes 208904 | tf_op jit(solution)/shard_map/ppermute | solution.py:229
  29.7 5.4 %collective-permute-start.5 = (f32[1,17,8,128]{3,2,1,0:T(8,128)S(1)}, f32[1,17,8,128]{3,2,1,0:T(8,128)S(1)}, u32[]{:S(2)}, u32[]{:S(2)}) collective-permute-start(f32[1,17,8,128]{3,2,1,0:T(8,128)S(1)} %get-tuple-element.25), channel_id=1, source_target_pairs={{0,4},{1,5},{2,6},{3,7},{4,0},{5,1},{6,2},{7,3},{8,12},{9,13},{10,... | collective-permute-start | bytes 208904 | tf_op jit(solution)/shard_map/ppermute | solution.py:229
  35.2 19.5 %copy-start.1 = (f32[2,320,256]{2,1,0:T(8,128)S(1)}, f32[2,320,256]{2,1,0:T(8,128)}, u32[]{:S(2)}) copy-start(f32[2,320,256]{2,1,0:T(8,128)} %refs_5_.1) | copy-start | bytes 1966084
  35.2 4.6 %collective-permute-start.6 = (f32[1,17,8,128]{3,2,1,0:T(8,128)S(1)}, f32[1,17,8,128]{3,2,1,0:T(8,128)S(1)}, u32[]{:S(2)}, u32[]{:S(2)}) collective-permute-start(f32[1,17,8,128]{3,2,1,0:T(8,128)S(1)} %get-tuple-element.21), channel_id=1, source_target_pairs={{0,4},{1,5},{2,6},{3,7},{4,0},{5,1},{6,2},{7,3},{8,12},{9,13},{10,... | collective-permute-start | bytes 208904 | tf_op jit(solution)/shard_map/ppermute | solution.py:229
  35.7 6.4 %collective-permute-start.7 = (f32[1,17,8,128]{3,2,1,0:T(8,128)S(1)}, f32[1,17,8,128]{3,2,1,0:T(8,128)S(1)}, u32[]{:S(2)}, u32[]{:S(2)}) collective-permute-start(f32[1,17,8,128]{3,2,1,0:T(8,128)S(1)} %get-tuple-element.21), channel_id=1, source_target_pairs={{0,8},{1,9},{2,10},{3,11},{4,12},{5,13},{6,14},{7,15},{8,0},{9,1},... | collective-permute-start | bytes 208904 | tf_op jit(solution)/shard_map/ppermute | solution.py:229
  38.1 6.1 %collective-permute-start.8 = (f32[1,17,8,128]{3,2,1,0:T(8,128)S(1)}, f32[1,17,8,128]{3,2,1,0:T(8,128)S(1)}, u32[]{:S(2)}, u32[]{:S(2)}) collective-permute-start(f32[1,17,8,128]{3,2,1,0:T(8,128)S(1)} %get-tuple-element.21), channel_id=1, source_target_pairs={{0,12},{1,13},{2,14},{3,15},{4,8},{5,9},{6,10},{7,11},{8,4},{9,5},... | collective-permute-start | bytes 208904 | tf_op jit(solution)/shard_map/ppermute | solution.py:229
  39.7 16.7 %collective-permute-start.11 = (f32[320,640]{1,0:T(8,128)S(1)}, f32[320,640]{1,0:T(8,128)S(1)}, u32[]{:S(2)}, u32[]{:S(2)}) collective-permute-start(f32[320,640]{1,0:T(8,128)S(1)} %dynamic-slice_bitcast_fusion), channel_id=1, source_target_pairs={{0,16},{16,0},{1,17},{17,1},{2,18},{18,2},{3,19},{19,3},{4,20},{20... | collective-permute-start | bytes 2457608 | tf_op jit(solution)/shard_map/ppermute | solution.py:225
  44.2 8.9 %collective-permute-start.9 = (f32[4,17,8,128]{3,2,1,0:T(8,128)S(1)}, f32[4,17,8,128]{3,2,1,0:T(8,128)S(1)}, u32[]{:S(2)}, u32[]{:S(2)}) collective-permute-start(f32[4,17,8,128]{3,2,1,0:T(8,128)S(1)} %pad_maximum_fusion), channel_id=1, source_target_pairs={{0,2},{1,3},{2,0},{3,1},{4,6},{5,7},{6,4},{7,5},{8,10},{9,11},{10,... | collective-permute-start | bytes 835592 | tf_op jit(solution)/shard_map/ppermute | solution.py:229
  53.1 9.6 %copy-start.4 = (f32[8,17,8,128]{3,2,1,0:T(8,128)}, f32[8,17,8,128]{3,2,1,0:T(8,128)S(1)}, u32[]{:S(2)}) copy-start(f32[8,17,8,128]{3,2,1,0:T(8,128)S(1)} %constant_dynamic-update-slice_fusion.refs_1_) | copy-start | bytes 1671172
  53.1 9.6 %collective-permute-start.10 = (f32[8,17,8,128]{3,2,1,0:T(8,128)S(1)}, f32[8,17,8,128]{3,2,1,0:T(8,128)S(1)}, u32[]{:S(2)}, u32[]{:S(2)}) collective-permute-start(f32[8,17,8,128]{3,2,1,0:T(8,128)S(1)} %constant_dynamic-update-slice_fusion.refs_1_), channel_id=1, source_target_pairs={{0,1},{1,0},{2,3},{3,2},{4,5},{5,4},{6,7},{7,6},{8,9},{9,8},{10,11... | collective-permute-start | bytes 1671176 | tf_op jit(solution)/shard_map/ppermute | solution.py:229
  54.7 1.7 %collective-permute-start.12 = (f32[320,256]{1,0:T(8,128)S(1)}, f32[320,256]{1,0:T(8,128)S(1)}, u32[]{:S(2)}, u32[]{:S(2)}) collective-permute-start(f32[320,256]{1,0:T(8,128)S(1)} %dynamic-slice_bitcast_fusion.1), channel_id=1, source_target_pairs={{0,16},{16,0},{1,17},{17,1},{2,18},{18,2},{3,19},{19,3},{4,20},{20... | collective-permute-start | bytes 983048 | tf_op jit(solution)/shard_map/ppermute | solution.py:225
  56.4 6.3 %copy-start.8 = (f32[320,256]{1,0:T(8,128)}, f32[320,256]{1,0:T(8,128)S(1)}, u32[]{:S(2)}) copy-start(f32[320,256]{1,0:T(8,128)S(1)} %collective-permute-done.12.refs_6_) | copy-start | bytes 983044
  56.4 6.3 %copy-start.2 = (f32[320,640]{1,0:T(8,128)}, f32[320,640]{1,0:T(8,128)S(1)}, u32[]{:S(2)}) copy-start(f32[320,640]{1,0:T(8,128)S(1)} %collective-permute-done.11.refs_4_) | copy-start | bytes 2457604
  62.7 0.8 copy-start.7
  63.5 21.5 %copy-start.6 = (f32[2,320,256]{2,1,0:T(8,128)S(1)}, f32[2,320,256]{2,1,0:T(8,128)}, u32[]{:S(2)}) copy-start(f32[2,320,256]{2,1,0:T(8,128)} %param.13) | copy-start | bytes 1966084
  76.0 9.0 %copy-start.5 = (f32[2,320,256]{2,1,0:T(8,128)S(1)}, f32[2,320,256]{2,1,0:T(8,128)}, u32[]{:S(2)}) copy-start(f32[2,320,256]{2,1,0:T(8,128)} %param.12) | copy-start | bytes 1966084
  76.0 11.3 %collective-permute-start.15 = (f32[320,640]{1,0:T(8,128)}, f32[320,640]{1,0:T(8,128)S(1)}, u32[]{:S(2)}, u32[]{:S(2)}) collective-permute-start(f32[320,640]{1,0:T(8,128)} %get-tuple-element.16), channel_id=1, source_target_pairs={{0,16},{16,0},{1,17},{17,1},{2,18},{18,2},{3,19},{19,3},{4,20},{20... | collective-permute-start | bytes 2457608 | tf_op jit(solution)/shard_map/ppermute | solution.py:225
  76.0 2.7 %collective-permute-start.13 = (f32[128,256]{1,0:T(8,128)}, f32[128,256]{1,0:T(8,128)S(1)}, u32[]{:S(2)}, u32[]{:S(2)}) collective-permute-start(f32[128,256]{1,0:T(8,128)} %get-tuple-element.11.refs_1_), channel_id=1, source_target_pairs={{0,16},{16,0},{1,17},{17,1},{2,18},{18,2},{3,19},{19,3},{4,20},{20... | collective-permute-start | bytes 393224 | tf_op jit(solution)/shard_map/ppermute | solution.py:225
  78.8 0.6 copy-start.9
  83.2 1.8 %collective-permute-start.14 = (f32[320,256]{1,0:T(8,128)}, f32[320,256]{1,0:T(8,128)S(1)}, u32[]{:S(2)}, u32[]{:S(2)}) collective-permute-start(f32[320,256]{1,0:T(8,128)} %get-tuple-element.14), channel_id=1, source_target_pairs={{0,16},{16,0},{1,17},{17,1},{2,18},{18,2},{3,19},{19,3},{4,20},{20... | collective-permute-start | bytes 983048 | tf_op jit(solution)/shard_map/ppermute | solution.py:225
  85.0 2.3 %copy-start.3 = (f32[320,640]{1,0:T(8,128)S(1)}, f32[320,640]{1,0:T(8,128)}, u32[]{:S(2)}) copy-start(f32[320,640]{1,0:T(8,128)} %get-tuple-element.15) | copy-start | bytes 2457604

commit v2 on v1

--- a/solution.py
+++ b/solution.py
@@ -90,12 +90,39 @@
     return mul(a[0], b[0]) + (mul(a[0], b[1]) + mul(a[1], b[0]))
 
 
+def apply3(a, b):
+    b = split(b)
+    half = a[0].shape[0] // 2
+    return jnp.concatenate([mul3([v[:half] for v in a], b), mul3([v[half:] for v in a], b)], 0)
+
+
+def twice_less_square(value, halves):
+    order = value.shape[0]
+    ends = list(range(order, 0, -2 * LANES))[::-1]
+    strips = []
+    for end in ends:
+        cols = slice(max(end - 2 * LANES, 0), end)
+        square = mul3([v[:end] for v in halves], [v[:, cols] for v in halves])
+        strips.append(split(2.0 * value[:end, cols] - square))
+    parts = []
+    for part in range(2):
+        rows = []
+        for n, end in enumerate(ends):
+            top = ends[n - 1] if n else 0
+            left = [strips[n][part][:top].T] if n else []
+            right = [strips[m][part][top:end] for m in range(n, len(ends))]
+            rows.append(jnp.concatenate(left + right, 1))
+        parts.append(jnp.concatenate(rows, 0))
+    return parts
+
+
 def tile_pairs(tiles):
     return [(i, j) for i in range(tiles) for j in range(i, tiles)]
 
 
-def stats_kernel(where_ref, act_ref, cot_ref, packed_ref):
-    block, me = where_ref[0], where_ref[1]
+def stats_kernel(where_ref, act_ref, cot_ref, packed_ref, *, far):
+    block = 1 - where_ref[0] if far else where_ref[0]
+    me = where_ref[2] if far else where_ref[1]
     rank = cot_ref.shape[1]
     share = rank // 2
     order = act_ref.shape[1] // 2
@@ -106,39 +133,44 @@
         for s in range(SHARDS):
             packed_ref[places[s], index] = tile[s * SUBS : (s + 1) * SUBS]
 
-    act = act_ref[:, pl.ds(pl.multiple_of(block * order, LANES), order)]
-    turned = act.T
     index = 0
-    for i in range(tiles):
-        strip = mul(turned[i * LANES : (i + 1) * LANES], act[:, i * LANES :])
-        for j in range(tiles - i):
-            put(index, strip[:, j * LANES : (j + 1) * LANES])
-            index += 1
     cot = cot_ref[:, pl.ds(pl.multiple_of(block * share, LANES), share)]
     strip = mul(cot.T, cot_ref[...])
     for i in range(share // LANES):
         for j in range(rank // LANES):
             put(index, strip[i * LANES : (i + 1) * LANES, j * LANES : (j + 1) * LANES])
             index += 1
+    act = act_ref[:, pl.ds(pl.multiple_of(block * order, LANES), order)]
+    turned = act.T
+    for i in range(tiles):
+        strip = mul(turned[i * LANES : (i + 1) * LANES], act[:, i * LANES :])
+        for j in range(tiles - i):
+            put(index, strip[:, j * LANES : (j + 1) * LANES])
+            index += 1
+
+
+def spread(me, halves, put):
+    for place in range(SHARDS):
+        half = halves[place * len(halves) // SHARDS]
+        put(pl.multiple_of(jnp.bitwise_xor(me, place) * SUBS, SUBS), half[place % half.shape[0]])
 
 
 def input_kernel(where_ref, near_ref, far_ref, fac_ref, fac_far_ref, grad_ref, grad_far_ref,
-                 mine_ref, theirs_ref, left_ref, out_ref, stat_ref, fac_scr, grad_scr, *, scale):
+                 mine_ref, theirs_ref, left_ref, stat_ref, fac_scr, grad_scr, *, scale, skip):
     block, me = where_ref[0], where_ref[1]
     slab, order = fac_far_ref.shape
     tiles = order // LANES
     own_rows = pl.ds(pl.multiple_of(block * slab, SUBS), slab)
     far_rows = pl.ds(pl.multiple_of((1 - block) * slab, SUBS), slab)
-    for place in range(SHARDS):
-        rows = pl.ds(pl.multiple_of(jnp.bitwise_xor(me, place) * SUBS, SUBS), SUBS)
-        half = SHARDS // 2
-        stat_ref[:, rows, :] = near_ref[place] if place < half else far_ref[place - half]
+    def put(row, rows):
+        stat_ref[:, pl.ds(row, SUBS), :] = rows[skip:]
+
+    spread(me, (near_ref, far_ref), put)
     fac_scr[own_rows, :] = 0.5 * fac_ref[block]
     fac_scr[far_rows, :] = 0.5 * fac_far_ref[...]
     grad_scr[own_rows, :] = grad_ref[block]
     grad_scr[far_rows, :] = grad_far_ref[...]
-    pairs = tile_pairs(tiles)
-    for index, (i, j) in enumerate(pairs):
+    for index, (i, j) in enumerate(tile_pairs(tiles)):
         at = lambda n: slice(n * LANES, (n + 1) * LANES)
         part = 0.5 * (stat_ref[index] * scale)
         fac_scr[at(i), at(j)] += part
@@ -146,11 +178,6 @@
             fac_scr[at(j), at(i)] += part.T
     mine_ref[...] = fac_scr[own_rows, :]
     theirs_ref[...] = fac_scr[far_rows, :]
-    lead = out_ref.shape[0] // LANES
-    count = out_ref.shape[1] // LANES
-    for n in range(lead * count):
-        i, j = n // count, n % count
-        out_ref[i * LANES : (i + 1) * LANES, j * LANES : (j + 1) * LANES] = stat_ref[len(pairs) + n]
     rows = lax.broadcasted_iota(jnp.int32, (order, order), 0)
     cols = lax.broadcasted_iota(jnp.int32, (order, order), 1)
     damped = fac_scr[...] + jnp.where(rows == cols, damping, 0.0)
@@ -158,22 +185,31 @@
     over = 1.0 / jnp.sqrt(squares)
     scaled = damped * over
     first = split(scaled)
-    twice = split(2.0 * scaled - mul3(first, first))
+    twice = twice_less_square(scaled, first)
     grad = grad_scr[...]
-    grad = 2.0 * grad - mul3(first, split(grad))
-    grad = 2.0 * grad - mul3(twice, split(grad))
-    once = grad - mul3(twice, split(grad))
-    left_ref[...] = (grad + once - mul3(twice, split(once))) * over
-
-
-def output_kernel(where_ref, stat_ref, stat_far_ref, fac_ref, left_ref, new_ref, mine_ref, theirs_ref, *, scale):
-    block = where_ref[0]
-    share, rank = stat_ref.shape
-    slab = mine_ref.shape[0]
-    own = pl.ds(pl.multiple_of(block * share, SUBS), share)
-    far = pl.ds(pl.multiple_of((1 - block) * share, SUBS), share)
-    new_ref[own, :] = 0.5 * fac_ref[own, :] + 0.5 * (stat_ref[...] * scale)
-    new_ref[far, :] = 0.5 * fac_ref[far, :] + 0.5 * (stat_far_ref[...] * scale)
+    grad = 2.0 * grad - apply3(first, grad)
+    grad = 2.0 * grad - apply3(twice, grad)
+    once = grad - apply3(twice, grad)
+    left_ref[...] = (grad + once - apply3(twice, once)) * over
+
+
+def output_kernel(where_ref, stat_ref, other_ref, fac_ref, left_ref, new_ref, mine_ref, theirs_ref, *, scale):
+    block, me, other = where_ref[0], where_ref[1], where_ref[2]
+    rank = fac_ref.shape[0]
+    share = rank // 2
+    count = rank // LANES
+
+    def put(first):
+        def rows_of(row, tiles):
+            for n in range(share // LANES * count):
+                i, j = n // count, n % count
+                at = pl.ds(pl.multiple_of(first + i * LANES + row, SUBS), SUBS)
+                cols = slice(j * LANES, (j + 1) * LANES)
+                new_ref[at, cols] = 0.5 * fac_ref[at, cols] + 0.5 * (tiles[n] * scale)
+        return rows_of
+
+    spread(me, (stat_ref,), put(block * share))
+    spread(other, (other_ref,), put((1 - block) * share))
     rows = lax.broadcasted_iota(jnp.int32, (rank, rank), 0)
     cols = lax.broadcasted_iota(jnp.int32, (rank, rank), 1)
     damped = new_ref[...] + jnp.where(rows == cols, damping, 0.0)
@@ -186,10 +222,9 @@
     fourth = split(2.0 * twice - mul3(second, second))
     head = jnp.where(rows == cols, 4.0, 0.0) - 2.0 * (scaled + twice) + mul3(first, second)
     inverse = split((2.0 * head - mul3(split(head), fourth)) * over)
-    far_left = split(left_ref[pl.ds(pl.multiple_of((1 - block) * slab, SUBS), slab), :])
-    theirs_ref[...] = mul3(far_left, inverse)
-    own_left = split(left_ref[pl.ds(pl.multiple_of(block * slab, SUBS), slab), :])
-    mine_ref[...] = mul3(own_left, inverse)
+    slab = mine_ref.shape[0]
+    theirs_ref[...] = mul3(split(left_ref[pl.ds(pl.multiple_of((1 - block) * slab, SUBS), slab), :]), inverse)
+    mine_ref[...] = mul3(split(left_ref[pl.ds(pl.multiple_of(block * slab, SUBS), slab), :]), inverse)
 
 
 def call(kernel, where, args, outs, scratch=()):
@@ -216,10 +251,10 @@
     crossed = y_bit * 8 + x_bit * 4 + z_bits
     me = jnp.where(group == 0, straight, crossed)
     partner = jnp.where(group == 0, crossed, straight)
-    where_mine = jnp.stack([group, me]).astype(jnp.int32)
-    where_theirs = jnp.stack([1 - group, partner]).astype(jnp.int32)
-    ntiles = len(tile_pairs(order // LANES)) + (rank // 2 // LANES) * (rank // LANES)
-    packed = (SHARDS, ntiles, SUBS, LANES)
+    where = jnp.stack([group, me, partner]).astype(jnp.int32)
+    outs = (rank // 2 // LANES) * (rank // LANES)
+    packed = [(SHARDS, outs + len(tile_pairs(order // LANES)), SUBS, LANES)]
+    fence = lax.optimization_barrier
 
     def swap(value):
         return lax.ppermute(value, "grp", [(0, 1), (1, 0)])
@@ -228,40 +263,48 @@
         pairs = [(g * peers + o, g * peers + (o ^ flips[g])) for g in range(2) for o in range(peers)]
         return lax.ppermute(value, ("grp", "own"), pairs)
 
-    (theirs,) = call(stats_kernel, where_theirs, (activations, cotangents), [packed])
-    arrived = swap(theirs)
-    (held,) = call(stats_kernel, where_mine, (activations, cotangents), [packed])
-    fac_far = swap(lax.dynamic_index_in_dim(input_factor, 1 - group, 0, False))
-    grad_far = swap(lax.dynamic_index_in_dim(gradient, 1 - group, 0, False))
-
-    arrived = send(held[8:] + arrived[8:], (1, 2)), held[:8] + arrived[:8]
-    low = send(arrived[0][4:] + arrived[1][4:], (2, 1)), arrived[0][:4] + arrived[1][:4]
-    quarter = low[0] + low[1]
-    pieces = [send(quarter[d : d + 1], (4 * d, 4 * d)) for d in (3, 2, 1)]
-    total = quarter[:1] + pieces[0] + pieces[1] + pieces[2]
-    gathered = {d: send(total, (4 * d, 4 * d)) for d in (3, 2, 1)}
-    quarter = jnp.concatenate([total, gathered[1], gathered[2], gathered[3]], 0)
-    near = jnp.concatenate([quarter, send(quarter, (2, 1))], 0)
+    def stats(far):
+        return call(lambda *refs: stats_kernel(*refs, far=far), where, (activations, cotangents), packed)[0]
+
+    arrived = swap(stats(True))
+    held = stats(False)
+    going = held[8:] + arrived[8:]
+    came = send(going, (1, 2))
+    fac_rows, grad_rows, _ = fence((input_factor, gradient, going))
+    fac_far = swap(lax.dynamic_index_in_dim(fac_rows, 1 - group, 0, False))
+    grad_far = swap(lax.dynamic_index_in_dim(grad_rows, 1 - group, 0, False))
+    came, fac_far, grad_far = fence((came, fac_far, grad_far))
+    kept = held[:8] + arrived[:8]
+    came = send(kept[4:] + came[4:], (2, 1)), kept[:4] + came[:4]
+    kept = came[0] + came[1]
+    ways = (3, 2, 1)
+    pieces = {d: send(kept[d : d + 1], (4 * d, 4 * d)) for d in ways}
+    kept = kept[:1] + pieces[3] + pieces[2] + pieces[1]
+    pieces = {d: send(kept, (4 * d, 4 * d)) for d in ways}
+    kept = jnp.concatenate([kept, pieces[1], pieces[2], pieces[3]], 0)
+    near = jnp.concatenate([kept, send(kept, (2, 1))], 0)
     far = send(near, (1, 2))
 
-    mine, theirs, left, out_share = call(
-        lambda *refs: input_kernel(*refs, scale=scale),
-        where_mine,
+    share = jnp.concatenate([near[:, :outs], far[:, :outs]], 0)
+    share_far = swap(share)
+    mine, theirs, left = call(
+        lambda *refs: input_kernel(*refs, scale=scale, skip=outs),
+        where,
         (near, far, input_factor, fac_far, gradient, grad_far),
-        [(slab, order), (slab, order), (order, rank), (rank // 2, rank)],
-        [(ntiles, LANES, LANES), (order, order), (order, rank)],
-    )
-    out_far = swap(out_share)
-    rows_far = swap(theirs)
+        [(slab, order), (slab, order), (order, rank)],
+        [(packed[0][1] - outs, LANES, LANES), (order, order), (order, rank)],
+    )
     new_output, update, update_far = call(
         lambda *refs: output_kernel(*refs, scale=scale),
-        where_mine,
-        (out_share, out_far, output_factor, left),
+        where,
+        (share, share_far, output_factor, left),
         [(rank, rank), (slab, rank), (slab, rank)],
     )
+    rows_far = swap(theirs)
     update_far = swap(update_far)
     own_block = lax.broadcasted_iota(jnp.int32, (nblocks, 1, 1), 0) == group
     new_input = jnp.where(own_block, mine[None], rows_far[None])
+    update_far, _ = fence((update_far, new_input))
     new_momentum = mom_decay * momentum + jnp.where(own_block, update[None], update_far[None])
     new_weights = weights - step_size * new_momentum
     return (new_weights, new_momentum, new_input, new_output)

time: 88.9 us -> 83.2 us (0.936)
  waiting for transfers between devices: 40.4 us -> 35.5 us
  Pallas kernels: 21.3 us -> 17.6 us
  local copies, waits for them, and re-layouts: 1.61 us -> 4.11 us
  starting transfers between devices: 18.3 us -> 20 us
  other arithmetic: 6.3 us -> 4.85 us
    pallas_call x4, Pallas kernels: 21.3 us -> 17.6 us  [call(): pl.pallas_call(kernel, out_shape=[jax.ShapeDtypeStruct(shape, jnp.float32...]
    ppermute x6, waiting for transfers between devices: 5.54 us -> 2.8 us  [swap(): return lax.ppermute(value, 'grp', [(0, 1), (1, 0)])]
    ppermute x10, waiting for transfers between devices: 34.8 us -> 32.7 us  [send(): return lax.ppermute(value, ('grp', 'own'), pairs)]
    slice x1 -> x3, local copies, waits for them, and re-layouts: 0.02 us -> 1.78 us  [the longest x2 1.77 us: on_chip_pairs(): share = jnp.concatenate([near[:, :outs], far[:, :outs]], 0)]
    ppermute x10, starting transfers between devices: 17 us -> 18.4 us  [send(): return lax.ppermute(value, ('grp', 'own'), pairs)]
    sub x1, other arithmetic: 2.3 us -> 1.26 us  [on_chip_pairs(): new_weights = weights - step_size * new_momentum]
    unnamed x23 -> x27, local copies, waits for them, and re-layouts: 1.49 us -> 2.23 us
  transfers between devices with their start and end apart: 16 -> 16, of which waited for: 11 -> 14; matrix products, arithmetic and copies ran while one was open for 3% -> 4% of each run, Pallas kernels for 7% -> 8%
where the time goes in v2:
time: 83.2 us; the launch traced here: 82.8 us
  waiting for transfers between devices  35.5 us (43%)
  starting transfers between devices  20 us (24%)
  Pallas kernels  17.6 us (21%)
  other arithmetic  4.85 us (6%)
  local copies, waits for them, and re-layouts  4.11 us (5%)
    ppermute x10, waiting for transfers between devices, send(): return lax.ppermute(value, ('grp', 'own'), pairs)  32.7 us
    ppermute x10, starting transfers between devices, send(): return lax.ppermute(value, ('grp', 'own'), pairs)  18.4 us
    pallas_call x4, Pallas kernels, call(): pl.pallas_call(kernel, out_shape=[jax.ShapeDtypeStruct(shape, jnp.float32...  17.6 us
    ppermute x6, waiting for transfers between devices, swap(): return lax.ppermute(value, 'grp', [(0, 1), (1, 0)])  2.8 us
    unnamed x27, local copies, waits for them, and re-layouts  2.23 us
    slice x2, local copies, waits for them, and re-layouts, on_chip_pairs(): share = jnp.concatenate([near[:, :outs], far[:, :outs]], 0)  1.77 us
  transfers between devices with their start and end apart: 16, of which 14 were waited for; matrix products, arithmetic and copies ran while one was open for 4% of the time, Pallas kernels for 8%

profile of v2, /device:TPU:0, one launch (start us, length us, event | category | flops | bytes accessed | tf_op | source)
XLA Modules:
  0.0 82.8 jit_solution(6401659811450969998)
XLA Ops:
  0.7 0.7 pad_add_fusion.refs_0_
  1.3 2.5 %shard_map.103 = f32[16,17,8,128]{3,2,1,0:T(8,128)} custom-call(s32[3]{0:T(128)} %pad_add_fusion.refs_0_, bf16[256,1280]{1,0:T(8,128)(2,1)} %refs_1_.3, bf16[256,256]{1,0:T(8,128)(2,1)} %refs_2_.3), custom_call_target="tpu_custom_call" | custom-call | tf_op jit(solution)/shard_map/pallas_call | solution.py:231
  3.8 0.5 collective-permute-start
  4.3 2.5 %shard_map.102 = f32[16,17,8,128]{3,2,1,0:T(8,128)} custom-call(s32[3]{0:T(128)} %pad_add_fusion.refs_0_, bf16[256,1280]{1,0:T(8,128)(2,1)} %refs_1_.3, bf16[256,256]{1,0:T(8,128)(2,1)} %refs_2_.3), custom_call_target="tpu_custom_call" | custom-call | tf_op jit(solution)/shard_map/pallas_call | solution.py:231
  6.8 0.0 copy-start
  6.8 0.1 collective-permute-done
  6.9 1.4 %slice_add_fusion = (f32[8,17,8,128]{3,2,1,0:T(8,128)S(1)}, f32[8,17,8,128]{3,2,1,0:T(8,128)S(1)}) fusion(f32[16,17,8,128]{3,2,1,0:T(8,128)S(1)} %collective-permute-done, f32[16,17,8,128]{3,2,1,0:T(8,128)} %shard_map.102), kind=kLoop, calls=%fused_computation.4 | loop fusion | flops 278528 | bytes 3342336 | tf_op jit(solution)/shard_map/add | solution.py:271
  8.3 0.0 copy-start.1
  8.4 0.2 copy-done
  8.6 0.1 dynamic-slice_bitcast_fusion
  8.6 0.2 collective-permute-start.2
  8.8 2.9 %collective-permute-start.1 = (f32[8,17,8,128]{3,2,1,0:T(8,128)S(1)}, f32[8,17,8,128]{3,2,1,0:T(8,128)S(1)}, u32[]{:S(2)}, u32[]{:S(2)}) collective-permute-start(f32[8,17,8,128]{3,2,1,0:T(8,128)S(1)} %get-tuple-element.32), channel_id=1, source_target_pairs={{0,1},{1,0},{2,3},{3,2},{4,5},{5,4},{6,7},{7,6},{8,9},{9,8},{10,11... | collective-permute-start | bytes 1671176 | tf_op jit(solution)/shard_map/ppermute | solution.py:264
  11.7 0.0 copy-done.1
  11.7 0.1 collective-permute-start.3
  11.8 1.6 %collective-permute-done.3.refs_6_ = f32[320,256]{1,0:T(8,128)S(1)} collective-permute-done((f32[320,256]{1,0:T(8,128)S(1)}, f32[320,256]{1,0:T(8,128)S(1)}, u32[]{:S(2)}, u32[]{:S(2)}) %collective-permute-start.3) | collective-permute-done | bytes 327712 | tf_op jit(solution)/shard_map/ppermute | solution.py:260
  13.4 0.0 copy-start.9
  13.4 5.8 %collective-permute-done.1 = f32[8,17,8,128]{3,2,1,0:T(8,128)S(1)} collective-permute-done((f32[8,17,8,128]{3,2,1,0:T(8,128)S(1)}, f32[8,17,8,128]{3,2,1,0:T(8,128)S(1)}, u32[]{:S(2)}, u32[]{:S(2)}) %collective-permute-start.1) | collective-permute-done | bytes 557088 | tf_op jit(solution)/shard_map/ppermute | solution.py:264
  19.2 0.0 collective-permute-done.2.refs_4_
  19.2 2.1 %collective-permute-start.4 = (f32[4,17,8,128]{3,2,1,0:T(8,128)S(1)}, f32[4,17,8,128]{3,2,1,0:T(8,128)S(1)}, u32[]{:S(2)}, u32[]{:S(2)}) collective-permute-start(f32[4,17,8,128]{3,2,1,0:T(8,128)S(1)} %slice_add_fusion.3), channel_id=1, source_target_pairs={{0,2},{1,3},{2,0},{3,1},{4,6},{5,7},{6,4},{7,5},{8,10},{9,11},{10,... | collective-permute-start | bytes 835592 | tf_op jit(solution)/shard_map/ppermute | solution.py:264
  21.3 4.5 %collective-permute-done.4 = f32[4,17,8,128]{3,2,1,0:T(8,128)S(1)} collective-permute-done((f32[4,17,8,128]{3,2,1,0:T(8,128)S(1)}, f32[4,17,8,128]{3,2,1,0:T(8,128)S(1)}, u32[]{:S(2)}, u32[]{:S(2)}) %collective-permute-start.4) | collective-permute-done | bytes 278560 | tf_op jit(solution)/shard_map/ppermute | solution.py:264
  25.9 0.1 fusion
  26.0 4.2 %collective-permute-start.5 = (f32[1,17,8,128]{3,2,1,0:T(8,128)S(1)}, f32[1,17,8,128]{3,2,1,0:T(8,128)S(1)}, u32[]{:S(2)}, u32[]{:S(2)}) collective-permute-start(f32[1,17,8,128]{3,2,1,0:T(8,128)S(1)} %get-tuple-element.34), channel_id=1, source_target_pairs={{0,12},{1,13},{2,14},{3,15},{4,8},{5,9},{6,10},{7,11},{8,4},{9,5},... | collective-permute-start | bytes 208904 | tf_op jit(solution)/shard_map/ppermute | solution.py:264
  30.1 0.0 collective-permute-start.7
  30.1 0.6 collective-permute-start.6
  30.8 1.7 %collective-permute-done.5 = f32[1,17,8,128]{3,2,1,0:T(8,128)S(1)} collective-permute-done((f32[1,17,8,128]{3,2,1,0:T(8,128)S(1)}, f32[1,17,8,128]{3,2,1,0:T(8,128)S(1)}, u32[]{:S(2)}, u32[]{:S(2)}) %collective-permute-start.5) | collective-permute-done | bytes 69664 | tf_op jit(solution)/shard_map/ppermute | solution.py:264
  32.5 1.9 %collective-permute-done.7 = f32[1,17,8,128]{3,2,1,0:T(8,128)S(1)} collective-permute-done((f32[1,17,8,128]{3,2,1,0:T(8,128)S(1)}, f32[1,17,8,128]{3,2,1,0:T(8,128)S(1)}, u32[]{:S(2)}, u32[]{:S(2)}) %collective-permute-start.7) | collective-permute-done | bytes 69664 | tf_op jit(solution)/shard_map/ppermute | solution.py:264
  34.5 0.9 %collective-permute-done.6 = f32[1,17,8,128]{3,2,1,0:T(8,128)S(1)} collective-permute-done((f32[1,17,8,128]{3,2,1,0:T(8,128)S(1)}, f32[1,17,8,128]{3,2,1,0:T(8,128)S(1)}, u32[]{:S(2)}, u32[]{:S(2)}) %collective-permute-start.6) | collective-permute-done | bytes 69664 | tf_op jit(solution)/shard_map/ppermute | solution.py:264
  35.4 3.2 %collective-permute-start.10 = (f32[1,17,8,128]{3,2,1,0:T(8,128)S(1)}, f32[1,17,8,128]{3,2,1,0:T(8,128)S(1)}, u32[]{:S(2)}, u32[]{:S(2)}) collective-permute-start(f32[1,17,8,128]{3,2,1,0:T(8,128)S(1)} %get-tuple-element.31), channel_id=1, source_target_pairs={{0,12},{1,13},{2,14},{3,15},{4,8},{5,9},{6,10},{7,11},{8,4},{9,5},... | collective-permute-start | bytes 208904 | tf_op jit(solution)/shard_map/ppermute | solution.py:264
  38.6 0.4 collective-permute-start.9
  38.9 0.9 %collective-permute-start.8 = (f32[1,17,8,128]{3,2,1,0:T(8,128)S(1)}, f32[1,17,8,128]{3,2,1,0:T(8,128)S(1)}, u32[]{:S(2)}, u32[]{:S(2)}) collective-permute-start(f32[1,17,8,128]{3,2,1,0:T(8,128)S(1)} %get-tuple-element.31), channel_id=1, source_target_pairs={{0,4},{1,5},{2,6},{3,7},{4,0},{5,1},{6,2},{7,3},{8,12},{9,13},{10,... | collective-permute-start | bytes 208904 | tf_op jit(solution)/shard_map/ppermute | solution.py:264
  39.8 2.3 %collective-permute-done.10 = f32[1,17,8,128]{3,2,1,0:T(8,128)S(1)} collective-permute-done((f32[1,17,8,128]{3,2,1,0:T(8,128)S(1)}, f32[1,17,8,128]{3,2,1,0:T(8,128)S(1)}, u32[]{:S(2)}, u32[]{:S(2)}) %collective-permute-start.10) | collective-permute-done | bytes 69664 | tf_op jit(solution)/shard_map/ppermute | solution.py:264
  42.1 1.7 %collective-permute-done.9 = f32[1,17,8,128]{3,2,1,0:T(8,128)S(1)} collective-permute-done((f32[1,17,8,128]{3,2,1,0:T(8,128)S(1)}, f32[1,17,8,128]{3,2,1,0:T(8,128)S(1)}, u32[]{:S(2)}, u32[]{:S(2)}) %collective-permute-start.9) | collective-permute-done | bytes 69664 | tf_op jit(solution)/shard_map/ppermute | solution.py:264
  43.9 0.1 collective-permute-done.8
  44.0 0.0 copy-done.9
  44.0 0.0 copy-done.3
  44.0 1.6 %collective-permute-start.11 = (f32[4,17,8,128]{3,2,1,0:T(8,128)S(1)}, f32[4,17,8,128]{3,2,1,0:T(8,128)S(1)}, u32[]{:S(2)}, u32[]{:S(2)}) collective-permute-start(f32[4,17,8,128]{3,2,1,0:T(8,128)S(1)} %pad_maximum_fusion), channel_id=1, source_target_pairs={{0,2},{1,3},{2,0},{3,1},{4,6},{5,7},{6,4},{7,5},{8,10},{9,11},{10,... | collective-permute-start | bytes 835592 | tf_op jit(solution)/shard_map/ppermute | solution.py:264
  45.6 6.1 %collective-permute-done.11 = f32[4,17,8,128]{3,2,1,0:T(8,128)S(1)} collective-permute-done((f32[4,17,8,128]{3,2,1,0:T(8,128)S(1)}, f32[4,17,8,128]{3,2,1,0:T(8,128)S(1)}, u32[]{:S(2)}, u32[]{:S(2)}) %collective-permute-start.11) | collective-permute-done | bytes 278560 | tf_op jit(solution)/shard_map/ppermute | solution.py:264
  51.8 0.0 copy-start.2
  51.8 2.5 %collective-permute-start.12 = (f32[8,17,8,128]{3,2,1,0:T(8,128)S(1)}, f32[8,17,8,128]{3,2,1,0:T(8,128)S(1)}, u32[]{:S(2)}, u32[]{:S(2)}) collective-permute-start(f32[8,17,8,128]{3,2,1,0:T(8,128)S(1)} %constant_dynamic-update-slice_fusion.refs_1_), channel_id=1, source_target_pairs={{0,1},{1,0},{2,3},{3,2},{4,5},{5,4},{6,7},{7,6},{8,9},{9,8},{10,11... | collective-permute-start | bytes 1671176 | tf_op jit(solution)/shard_map/ppermute | solution.py:264
  54.3 7.5 %collective-permute-done.12.refs_2_ = f32[8,17,8,128]{3,2,1,0:T(8,128)S(1)} collective-permute-done((f32[8,17,8,128]{3,2,1,0:T(8,128)S(1)}, f32[8,17,8,128]{3,2,1,0:T(8,128)S(1)}, u32[]{:S(2)}, u32[]{:S(2)}) %collective-permute-start.12) | collective-permute-done | bytes 557088 | tf_op jit(solution)/shard_map/ppermute | solution.py:264
  61.8 0.0 copy-done.2
  61.8 0.8 copy-done.5
  62.7 8.9 %shard_map.104 = (f32[320,640]{1,0:T(8,128)}, f32[320,640]{1,0:T(8,128)}, f32[640,256]{1,0:T(8,128)}) custom-call(s32[3]{0:T(128)} %pad_add_fusion.refs_0_, f32[8,17,8,128]{3,2,1,0:T(8,128)} %copy-done.2, f32[8,17,8,128]{3,2,1,0:T(8,128)} %copy-done.5, f32[2,320,640]{2,1,0:T(8,128)} %refs_3_.2, f32[320,640]{1,0:T(8,128)} %copy-done.3, ...), custom_call_target="tpu_custom_call" | custom-call | tf_op jit(solution)/shard_map/pallas_call | solution.py:231
  71.5 0.0 collective-permute-start.15
  71.5 0.9 %slice.66 = f32[8,2,8,128]{3,2,1,0:T(8,128)S(1)} slice(f32[8,17,8,128]{3,2,1,0:T(8,128)} %copy-done.2), slice={[0:8], [0:2], [0:8], [0:128]} | slice | bytes 131072 | tf_op jit(solution)/shard_map/slice | solution.py:288
  72.5 0.8 %slice.67 = f32[8,2,8,128]{3,2,1,0:T(8,128)S(1)} slice(f32[8,17,8,128]{3,2,1,0:T(8,128)} %copy-done.5), slice={[0:8], [0:2], [0:8], [0:128]} | slice | bytes 131072 | tf_op jit(solution)/shard_map/slice | solution.py:288
  73.3 0.0 copy-start.8
  73.3 0.5 collective-permute-start.13
  73.8 1.0 %collective-permute-done.13.refs_2_ = f32[16,2,8,128]{3,2,1,0:T(8,128)S(1)} collective-permute-done((f32[16,2,8,128]{3,2,1,0:T(8,128)S(1)}, f32[16,2,8,128]{3,2,1,0:T(8,128)S(1)}, u32[]{:S(2)}, u32[]{:S(2)}) %collective-permute-start.13) | collective-permute-done | bytes 131104 | tf_op jit(solution)/shard_map/ppermute | solution.py:260
  74.8 0.0 copy-done.8
  74.8 0.7 copy-done.11
  75.5 3.8 %shard_map.105 = (f32[256,256]{1,0:T(8,128)}, f32[320,256]{1,0:T(8,128)}, f32[320,256]{1,0:T(8,128)}) custom-call(s32[3]{0:T(128)} %pad_add_fusion.refs_0_, f32[16,2,8,128]{3,2,1,0:T(8,128)} %copy-done.8, f32[16,2,8,128]{3,2,1,0:T(8,128)} %copy-done.11, f32[256,256]{1,0:T(8,128)} %refs_3_.3, f32[640,256]{1,0:T(8,128)} %get-tuple-element.21.refs_4_), custom_call_target="tpu_custom_call" | custom-call | tf_op jit(solution)/shard_map/pallas_call | solution.py:231
  79.2 0.4 collective-permute-start.14
  79.6 0.0 collective-permute-done.15
  79.6 0.0 copy-done.4
  79.6 0.0 copy-start.6
  79.6 0.0 copy-start.7
  79.6 0.0 copy-start.10
  79.7 1.3 %broadcast_select_fusion = f32[2,320,640]{2,1,0:T(8,128)} fusion(f32[320,640]{1,0:T(8,128)S(1)} %collective-permute-done.15, f32[320,640]{1,0:T(8,128)S(1)} %copy-done.4, pred[2]{0:T(512)(128)(4,1)S(1)} %iota_compare_fusion), kind=kLoop, calls=%fused_computation | loop fusion | flops 409600 | bytes 3276802 | tf_op jit(solution)/shard_map/jit(_where)/select_n | solution.py:306
  81.0 0.1 collective-permute-done.14
  81.1 0.0 copy-done.6
  81.1 0.3 copy-done.7
  81.3 0.2 copy-done.10
  81.6 1.3 %multiply_subtract_fusion = (f32[2,320,256]{2,1,0:T(8,128)}, f32[2,320,256]{2,1,0:T(8,128)}) fusion(f32[2,320,256]{2,1,0:T(8,128)S(1)} %copy-done.6, f32[320,256]{1,0:T(8,128)S(1)} %collective-permute-done.14, f32[320,256]{1,0:T(8,128)S(1)} %copy-done.10, pred[2]{0:T(512)(128)(4,1)S(1)} %iota_compare_fusion, f32[2,320,256]{2,1,0:T(8,128)S(1)} %copy-done.7), kind=kLoop, calls=%fused_computation.2 | loop fusion | flops 819200 | bytes 3276802 | tf_op jit(solution)/shard_map/sub | solution.py:309
  (15 shorter events, 0.2 us)
Async XLA Ops:
  3.8 3.1 %collective-permute-start = (f32[16,17,8,128]{3,2,1,0:T(8,128)}, f32[16,17,8,128]{3,2,1,0:T(8,128)S(1)}, u32[]{:S(2)}, u32[]{:S(2)}) collective-permute-start(f32[16,17,8,128]{3,2,1,0:T(8,128)} %shard_map.103), channel_id=1, source_target_pairs={{0,16},{16,0},{1,17},{17,1},{2,18},{18,2},{3,19},{19,3},{4,20},{20... | collective-permute-start | bytes 3342344 | tf_op jit(solution)/shard_map/ppermute | solution.py:260
  6.8 1.8 %copy-start = (f32[2,320,640]{2,1,0:T(8,128)S(1)}, f32[2,320,640]{2,1,0:T(8,128)}, u32[]{:S(2)}) copy-start(f32[2,320,640]{2,1,0:T(8,128)} %refs_3_.2) | copy-start | bytes 4915204
  8.3 3.3 %copy-start.1 = (f32[2,320,256]{2,1,0:T(8,128)S(1)}, f32[2,320,256]{2,1,0:T(8,128)}, u32[]{:S(2)}) copy-start(f32[2,320,256]{2,1,0:T(8,128)} %refs_5_.1) | copy-start | bytes 1966084
  8.6 10.6 %collective-permute-start.2 = (f32[320,640]{1,0:T(8,128)S(1)}, f32[320,640]{1,0:T(8,128)S(1)}, u32[]{:S(2)}, u32[]{:S(2)}) collective-permute-start(f32[320,640]{1,0:T(8,128)S(1)} %dynamic-slice_bitcast_fusion), channel_id=1, source_target_pairs={{0,16},{16,0},{1,17},{17,1},{2,18},{18,2},{3,19},{19,3},{4,20},{20... | collective-permute-start | bytes 2457608 | tf_op jit(solution)/shard_map/ppermute | solution.py:260
  8.8 10.4 %collective-permute-start.1 = (f32[8,17,8,128]{3,2,1,0:T(8,128)S(1)}, f32[8,17,8,128]{3,2,1,0:T(8,128)S(1)}, u32[]{:S(2)}, u32[]{:S(2)}) collective-permute-start(f32[8,17,8,128]{3,2,1,0:T(8,128)S(1)} %get-tuple-element.32), channel_id=1, source_target_pairs={{0,1},{1,0},{2,3},{3,2},{4,5},{5,4},{6,7},{7,6},{8,9},{9,8},{10,11... | collective-permute-start | bytes 1671176 | tf_op jit(solution)/shard_map/ppermute | solution.py:264
  11.7 1.7 %collective-permute-start.3 = (f32[320,256]{1,0:T(8,128)S(1)}, f32[320,256]{1,0:T(8,128)S(1)}, u32[]{:S(2)}, u32[]{:S(2)}) collective-permute-start(f32[320,256]{1,0:T(8,128)S(1)} %dynamic-slice_bitcast_fusion.1), channel_id=1, source_target_pairs={{0,16},{16,0},{1,17},{17,1},{2,18},{18,2},{3,19},{19,3},{4,20},{20... | collective-permute-start | bytes 983048 | tf_op jit(solution)/shard_map/ppermute | solution.py:260
  13.4 30.6 %copy-start.9 = (f32[320,256]{1,0:T(8,128)}, f32[320,256]{1,0:T(8,128)S(1)}, u32[]{:S(2)}) copy-start(f32[320,256]{1,0:T(8,128)S(1)} %collective-permute-done.3.refs_6_) | copy-start | bytes 983044
  19.2 24.8 %copy-start.3 = (f32[320,640]{1,0:T(8,128)}, f32[320,640]{1,0:T(8,128)S(1)}, u32[]{:S(2)}) copy-start(f32[320,640]{1,0:T(8,128)S(1)} %collective-permute-done.2.refs_4_) | copy-start | bytes 2457604
  19.2 6.6 %collective-permute-start.4 = (f32[4,17,8,128]{3,2,1,0:T(8,128)S(1)}, f32[4,17,8,128]{3,2,1,0:T(8,128)S(1)}, u32[]{:S(2)}, u32[]{:S(2)}) collective-permute-start(f32[4,17,8,128]{3,2,1,0:T(8,128)S(1)} %slice_add_fusion.3), channel_id=1, source_target_pairs={{0,2},{1,3},{2,0},{3,1},{4,6},{5,7},{6,4},{7,5},{8,10},{9,11},{10,... | collective-permute-start | bytes 835592 | tf_op jit(solution)/shard_map/ppermute | solution.py:264
  26.0 6.6 %collective-permute-start.5 = (f32[1,17,8,128]{3,2,1,0:T(8,128)S(1)}, f32[1,17,8,128]{3,2,1,0:T(8,128)S(1)}, u32[]{:S(2)}, u32[]{:S(2)}) collective-permute-start(f32[1,17,8,128]{3,2,1,0:T(8,128)S(1)} %get-tuple-element.34), channel_id=1, source_target_pairs={{0,12},{1,13},{2,14},{3,15},{4,8},{5,9},{6,10},{7,11},{8,4},{9,5},... | collective-permute-start | bytes 208904 | tf_op jit(solution)/shard_map/ppermute | solution.py:264
  30.1 4.3 %collective-permute-start.7 = (f32[1,17,8,128]{3,2,1,0:T(8,128)S(1)}, f32[1,17,8,128]{3,2,1,0:T(8,128)S(1)}, u32[]{:S(2)}, u32[]{:S(2)}) collective-permute-start(f32[1,17,8,128]{3,2,1,0:T(8,128)S(1)} %get-tuple-element.35), channel_id=1, source_target_pairs={{0,4},{1,5},{2,6},{3,7},{4,0},{5,1},{6,2},{7,3},{8,12},{9,13},{10,... | collective-permute-start | bytes 208904 | tf_op jit(solution)/shard_map/ppermute | solution.py:264
  30.1 5.2 %collective-permute-start.6 = (f32[1,17,8,128]{3,2,1,0:T(8,128)S(1)}, f32[1,17,8,128]{3,2,1,0:T(8,128)S(1)}, u32[]{:S(2)}, u32[]{:S(2)}) collective-permute-start(f32[1,17,8,128]{3,2,1,0:T(8,128)S(1)} %get-tuple-element.36), channel_id=1, source_target_pairs={{0,8},{1,9},{2,10},{3,11},{4,12},{5,13},{6,14},{7,15},{8,0},{9,1},... | collective-permute-start | bytes 208904 | tf_op jit(solution)/shard_map/ppermute | solution.py:264
  35.4 6.8 %collective-permute-start.10 = (f32[1,17,8,128]{3,2,1,0:T(8,128)S(1)}, f32[1,17,8,128]{3,2,1,0:T(8,128)S(1)}, u32[]{:S(2)}, u32[]{:S(2)}) collective-permute-start(f32[1,17,8,128]{3,2,1,0:T(8,128)S(1)} %get-tuple-element.31), channel_id=1, source_target_pairs={{0,12},{1,13},{2,14},{3,15},{4,8},{5,9},{6,10},{7,11},{8,4},{9,5},... | collective-permute-start | bytes 208904 | tf_op jit(solution)/shard_map/ppermute | solution.py:264
  38.6 5.3 %collective-permute-start.9 = (f32[1,17,8,128]{3,2,1,0:T(8,128)S(1)}, f32[1,17,8,128]{3,2,1,0:T(8,128)S(1)}, u32[]{:S(2)}, u32[]{:S(2)}) collective-permute-start(f32[1,17,8,128]{3,2,1,0:T(8,128)S(1)} %get-tuple-element.31), channel_id=1, source_target_pairs={{0,8},{1,9},{2,10},{3,11},{4,12},{5,13},{6,14},{7,15},{8,0},{9,1},... | collective-permute-start | bytes 208904 | tf_op jit(solution)/shard_map/ppermute | solution.py:264
  38.9 5.1 %collective-permute-start.8 = (f32[1,17,8,128]{3,2,1,0:T(8,128)S(1)}, f32[1,17,8,128]{3,2,1,0:T(8,128)S(1)}, u32[]{:S(2)}, u32[]{:S(2)}) collective-permute-start(f32[1,17,8,128]{3,2,1,0:T(8,128)S(1)} %get-tuple-element.31), channel_id=1, source_target_pairs={{0,4},{1,5},{2,6},{3,7},{4,0},{5,1},{6,2},{7,3},{8,12},{9,13},{10,... | collective-permute-start | bytes 208904 | tf_op jit(solution)/shard_map/ppermute | solution.py:264
  44.0 7.7 %collective-permute-start.11 = (f32[4,17,8,128]{3,2,1,0:T(8,128)S(1)}, f32[4,17,8,128]{3,2,1,0:T(8,128)S(1)}, u32[]{:S(2)}, u32[]{:S(2)}) collective-permute-start(f32[4,17,8,128]{3,2,1,0:T(8,128)S(1)} %pad_maximum_fusion), channel_id=1, source_target_pairs={{0,2},{1,3},{2,0},{3,1},{4,6},{5,7},{6,4},{7,5},{8,10},{9,11},{10,... | collective-permute-start | bytes 835592 | tf_op jit(solution)/shard_map/ppermute | solution.py:264
  51.8 10.1 %copy-start.2 = (f32[8,17,8,128]{3,2,1,0:T(8,128)}, f32[8,17,8,128]{3,2,1,0:T(8,128)S(1)}, u32[]{:S(2)}) copy-start(f32[8,17,8,128]{3,2,1,0:T(8,128)S(1)} %constant_dynamic-update-slice_fusion.refs_1_) | copy-start | bytes 1671172
  51.8 10.0 %collective-permute-start.12 = (f32[8,17,8,128]{3,2,1,0:T(8,128)S(1)}, f32[8,17,8,128]{3,2,1,0:T(8,128)S(1)}, u32[]{:S(2)}, u32[]{:S(2)}) collective-permute-start(f32[8,17,8,128]{3,2,1,0:T(8,128)S(1)} %constant_dynamic-update-slice_fusion.refs_1_), channel_id=1, source_target_pairs={{0,1},{1,0},{2,3},{3,2},{4,5},{5,4},{6,7},{7,6},{8,9},{9,8},{10,11... | collective-permute-start | bytes 1671176 | tf_op jit(solution)/shard_map/ppermute | solution.py:264
  61.8 0.8 copy-start.5
  71.5 8.1 %copy-start.4 = (f32[320,640]{1,0:T(8,128)S(1)}, f32[320,640]{1,0:T(8,128)}, u32[]{:S(2)}) copy-start(f32[320,640]{1,0:T(8,128)} %get-tuple-element.24) | copy-start | bytes 2457604
  71.5 8.1 %collective-permute-start.15 = (f32[320,640]{1,0:T(8,128)}, f32[320,640]{1,0:T(8,128)S(1)}, u32[]{:S(2)}, u32[]{:S(2)}) collective-permute-start(f32[320,640]{1,0:T(8,128)} %get-tuple-element.25), channel_id=1, source_target_pairs={{0,16},{16,0},{1,17},{17,1},{2,18},{18,2},{3,19},{19,3},{4,20},{20... | collective-permute-start | bytes 2457608 | tf_op jit(solution)/shard_map/ppermute | solution.py:260
  73.3 1.5 %copy-start.8 = (f32[16,2,8,128]{3,2,1,0:T(8,128)}, f32[16,2,8,128]{3,2,1,0:T(8,128)S(1)}, u32[]{:S(2)}) copy-start(f32[16,2,8,128]{3,2,1,0:T(8,128)S(1)} %pad_maximum_fusion.1.refs_1_) | copy-start | bytes 393220
  73.3 1.5 %collective-permute-start.13 = (f32[16,2,8,128]{3,2,1,0:T(8,128)S(1)}, f32[16,2,8,128]{3,2,1,0:T(8,128)S(1)}, u32[]{:S(2)}, u32[]{:S(2)}) collective-permute-start(f32[16,2,8,128]{3,2,1,0:T(8,128)S(1)} %pad_maximum_fusion.1.refs_1_), channel_id=1, source_target_pairs={{0,16},{16,0},{1,17},{17,1},{2,18},{18,2},{3,19},{19,3},{4,20},{20... | collective-permute-start | bytes 393224 | tf_op jit(solution)/shard_map/ppermute | solution.py:260
  74.8 0.7 copy-start.11
  79.2 1.8 %collective-permute-start.14 = (f32[320,256]{1,0:T(8,128)}, f32[320,256]{1,0:T(8,128)S(1)}, u32[]{:S(2)}, u32[]{:S(2)}) collective-permute-start(f32[320,256]{1,0:T(8,128)} %get-tuple-element.23), channel_id=1, source_target_pairs={{0,16},{16,0},{1,17},{17,1},{2,18},{18,2},{3,19},{19,3},{4,20},{20... | collective-permute-start | bytes 983048 | tf_op jit(solution)/shard_map/ppermute | solution.py:260
  79.6 1.5 %copy-start.6 = (f32[2,320,256]{2,1,0:T(8,128)S(1)}, f32[2,320,256]{2,1,0:T(8,128)}, u32[]{:S(2)}) copy-start(f32[2,320,256]{2,1,0:T(8,128)} %param.12) | copy-start | bytes 1966084
  79.6 1.7 %copy-start.7 = (f32[2,320,256]{2,1,0:T(8,128)S(1)}, f32[2,320,256]{2,1,0:T(8,128)}, u32[]{:S(2)}) copy-start(f32[2,320,256]{2,1,0:T(8,128)} %param.13) | copy-start | bytes 1966084
  79.6 1.9 %copy-start.10 = (f32[320,256]{1,0:T(8,128)S(1)}, f32[320,256]{1,0:T(8,128)}, u32[]{:S(2)}) copy-start(f32[320,256]{1,0:T(8,128)} %get-tuple-element.22) | copy-start | bytes 983044

commit v3 on v2

--- a/solution.py
+++ b/solution.py
@@ -1,3 +1,5 @@
+import math
+
 import jax
 import jax.numpy as jnp
 from jax import lax
@@ -120,11 +122,15 @@
     return [(i, j) for i in range(tiles) for j in range(i, tiles)]
 
 
+def places_in(shape):
+    rows = lax.broadcasted_iota(jnp.int32, shape, 0)
+    cols = lax.broadcasted_iota(jnp.int32, shape, 1)
+    return rows, cols
+
+
 def stats_kernel(where_ref, act_ref, cot_ref, packed_ref, *, far):
     block = 1 - where_ref[0] if far else where_ref[0]
     me = where_ref[2] if far else where_ref[1]
-    rank = cot_ref.shape[1]
-    share = rank // 2
     order = act_ref.shape[1] // 2
     tiles = order // LANES
     places = [jnp.bitwise_xor(me, s) for s in range(SHARDS)]
@@ -133,20 +139,34 @@
         for s in range(SHARDS):
             packed_ref[places[s], index] = tile[s * SUBS : (s + 1) * SUBS]
 
-    index = 0
-    cot = cot_ref[:, pl.ds(pl.multiple_of(block * share, LANES), share)]
-    strip = mul(cot.T, cot_ref[...])
-    for i in range(share // LANES):
-        for j in range(rank // LANES):
-            put(index, strip[i * LANES : (i + 1) * LANES, j * LANES : (j + 1) * LANES])
-            index += 1
+    index = 2
     act = act_ref[:, pl.ds(pl.multiple_of(block * order, LANES), order)]
     turned = act.T
+    diagonal = []
     for i in range(tiles):
         strip = mul(turned[i * LANES : (i + 1) * LANES], act[:, i * LANES :])
-        for j in range(tiles - i):
+        diagonal.append(strip[:, :LANES])
+        for j in range(1, tiles - i):
             put(index, strip[:, j * LANES : (j + 1) * LANES])
             index += 1
+    cot = cot_ref[:, pl.ds(pl.multiple_of(block * LANES, LANES), LANES)]
+    diagonal.append(mul(cot.T, cot))
+    upper = mul(cot_ref[:, :LANES].T, cot_ref[:, LANES:])
+    half = LANES // 2
+    upper = jnp.where(block == 0, upper[:half], upper[half:])
+    rows, cols = places_in((LANES, LANES))
+    npairs = len(diagonal) // 2
+    lines = []
+    for pair in range(npairs):
+        above, below = diagonal[2 * pair], diagonal[2 * pair + 1]
+        put(index + pair if pair < npairs - 1 else 0, jnp.where(cols > rows, above, below))
+        lines.append(jnp.sum(jnp.where(cols == rows, above, 0.0).reshape(SHARDS, SUBS, LANES), axis=1))
+    few = SUBS // 2
+    for s in range(SHARDS):
+        packed_ref[places[s], 1, :few] = upper[s * few : (s + 1) * few]
+        for pair in range(few):
+            line = lines[pair][s : s + 1] if pair < npairs else jnp.zeros((1, LANES), jnp.float32)
+            packed_ref[places[s], 1, few + pair : few + pair + 1] = line
 
 
 def spread(me, halves, put):
@@ -156,26 +176,39 @@
 
 
 def input_kernel(where_ref, near_ref, far_ref, fac_ref, fac_far_ref, grad_ref, grad_far_ref,
-                 mine_ref, theirs_ref, left_ref, stat_ref, fac_scr, grad_scr, *, scale, skip):
+                 mine_ref, theirs_ref, left_ref, stat_ref, fac_scr, grad_scr, *, scale):
     block, me = where_ref[0], where_ref[1]
     slab, order = fac_far_ref.shape
     tiles = order // LANES
     own_rows = pl.ds(pl.multiple_of(block * slab, SUBS), slab)
     far_rows = pl.ds(pl.multiple_of((1 - block) * slab, SUBS), slab)
     def put(row, rows):
-        stat_ref[:, pl.ds(row, SUBS), :] = rows[skip:]
+        stat_ref[:, pl.ds(row, SUBS), :] = rows
 
     spread(me, (near_ref, far_ref), put)
     fac_scr[own_rows, :] = 0.5 * fac_ref[block]
     fac_scr[far_rows, :] = 0.5 * fac_far_ref[...]
     grad_scr[own_rows, :] = grad_ref[block]
     grad_scr[far_rows, :] = grad_far_ref[...]
-    for index, (i, j) in enumerate(tile_pairs(tiles)):
-        at = lambda n: slice(n * LANES, (n + 1) * LANES)
-        part = 0.5 * (stat_ref[index] * scale)
-        fac_scr[at(i), at(j)] += part
-        if i != j:
+    at = lambda n: slice(n * LANES, (n + 1) * LANES)
+    index = 2
+    for i in range(tiles):
+        for j in range(i + 1, tiles):
+            part = 0.5 * (stat_ref[index] * scale)
+            fac_scr[at(i), at(j)] += part
             fac_scr[at(j), at(i)] += part.T
+            index += 1
+    rows, cols = places_in((LANES, LANES))
+    npairs = (tiles + 1) // 2
+    for pair in range(npairs):
+        part = 0.5 * (stat_ref[index + pair if pair < npairs - 1 else 0] * scale)
+        turned = part.T
+        line = stat_ref[1, pl.ds(SUBS // 2 + pair, SHARDS, stride=SUBS), :]
+        line = 0.5 * (jnp.sum(line, axis=0, keepdims=True) * scale)
+        above = jnp.where(cols > rows, part, jnp.where(cols < rows, turned, line))
+        fac_scr[at(2 * pair), at(2 * pair)] += above
+        if pair < npairs - 1:
+            fac_scr[at(2 * pair + 1), at(2 * pair + 1)] += jnp.where(cols > rows, turned, part)
     mine_ref[...] = fac_scr[own_rows, :]
     theirs_ref[...] = fac_scr[far_rows, :]
     rows = lax.broadcasted_iota(jnp.int32, (order, order), 0)
@@ -193,25 +226,33 @@
     left_ref[...] = (grad + once - apply3(twice, once)) * over
 
 
-def output_kernel(where_ref, stat_ref, other_ref, fac_ref, left_ref, new_ref, mine_ref, theirs_ref, *, scale):
-    block, me, other = where_ref[0], where_ref[1], where_ref[2]
-    rank = fac_ref.shape[0]
-    share = rank // 2
-    count = rank // LANES
-
-    def put(first):
-        def rows_of(row, tiles):
-            for n in range(share // LANES * count):
-                i, j = n // count, n % count
-                at = pl.ds(pl.multiple_of(first + i * LANES + row, SUBS), SUBS)
-                cols = slice(j * LANES, (j + 1) * LANES)
-                new_ref[at, cols] = 0.5 * fac_ref[at, cols] + 0.5 * (tiles[n] * scale)
-        return rows_of
-
-    spread(me, (stat_ref,), put(block * share))
-    spread(other, (other_ref,), put((1 - block) * share))
-    rows = lax.broadcasted_iota(jnp.int32, (rank, rank), 0)
-    cols = lax.broadcasted_iota(jnp.int32, (rank, rank), 1)
+def output_kernel(where_ref, near_ref, far_ref, other_near_ref, other_far_ref, fac_ref, left_ref, new_ref, mine_ref, theirs_ref,
+                  tile_scr, half_scr, *, scale):
+    block = where_ref[0]
+    few = SUBS // 2
+    for n, halves in enumerate(((near_ref, far_ref), (other_near_ref, other_far_ref))):
+        for place in range(SHARDS):
+            shard = jnp.bitwise_xor(where_ref[1 + n], place)
+            ref, at = halves[place // 8], place % 8
+            tile_scr[n, pl.ds(pl.multiple_of(shard * SUBS, SUBS), SUBS), :] = ref[at, 0]
+            half_scr[n, shard] = ref[at, 1]
+    rows, cols = places_in((LANES, LANES))
+    corners, halves = [], []
+    for n in range(2):
+        tile = tile_scr[n]
+        corners.append(jnp.where(cols > rows, tile.T, tile))
+        halves.append(jnp.concatenate([half_scr[n, s, :few, :] for s in range(SHARDS)], 0))
+    first = block == 0
+    upper = jnp.concatenate([jnp.where(first, halves[0], halves[1]), jnp.where(first, halves[1], halves[0])], 0)
+    stats = jnp.concatenate(
+        [
+            jnp.concatenate([jnp.where(first, corners[0], corners[1]), upper], 1),
+            jnp.concatenate([upper.T, jnp.where(first, corners[1], corners[0])], 1),
+        ],
+        0,
+    )
+    new_ref[...] = 0.5 * fac_ref[...] + 0.5 * (stats * scale)
+    rows, cols = places_in(new_ref.shape)
     damped = new_ref[...] + jnp.where(rows == cols, damping, 0.0)
     squares = jnp.sum(jnp.sum(damped * damped, axis=0, keepdims=True), axis=1, keepdims=True)
     over = 1.0 / jnp.sqrt(squares)
@@ -227,7 +268,8 @@
     mine_ref[...] = mul3(split(left_ref[pl.ds(pl.multiple_of(block * slab, SUBS), slab), :]), inverse)
 
 
-def call(kernel, where, args, outs, scratch=()):
+def call(kernel, where, args, outs, scratch=(), flops=0):
+    size = sum(arg.size * arg.dtype.itemsize for arg in args) + sum(4 * math.prod(shape) for shape in outs)
     return pl.pallas_call(
         kernel,
         out_shape=[jax.ShapeDtypeStruct(shape, jnp.float32) for shape in outs],
@@ -235,6 +277,7 @@
         + [pl.BlockSpec(memory_space=pltpu.VMEM)] * len(args),
         out_specs=[pl.BlockSpec(memory_space=pltpu.VMEM)] * len(outs),
         scratch_shapes=[pltpu.VMEM(shape, jnp.float32) for shape in scratch],
+        cost_estimate=pl.CostEstimate(flops=flops, bytes_accessed=size, transcendentals=0),
     )(where, *args)
 
 
@@ -252,8 +295,9 @@
     me = jnp.where(group == 0, straight, crossed)
     partner = jnp.where(group == 0, crossed, straight)
     where = jnp.stack([group, me, partner]).astype(jnp.int32)
-    outs = (rank // 2 // LANES) * (rank // LANES)
-    packed = [(SHARDS, outs + len(tile_pairs(order // LANES)), SUBS, LANES)]
+    tiles = order // LANES
+    packed = [(SHARDS, 2 + tiles * (tiles - 1) // 2 + (tiles + 1) // 2 - 1, SUBS, LANES)]
+    heavy = 2 * order * order * (3 * order + 12 * rank)
     fence = lax.optimization_barrier
 
     def swap(value):
@@ -263,8 +307,13 @@
         pairs = [(g * peers + o, g * peers + (o ^ flips[g])) for g in range(2) for o in range(peers)]
         return lax.ppermute(value, ("grp", "own"), pairs)
 
+    def cross(value, flips):
+        pairs = [(g * peers + o, (1 - g) * peers + (o ^ flips[g])) for g in range(2) for o in range(peers)]
+        return lax.ppermute(value, ("grp", "own"), pairs)
+
     def stats(far):
-        return call(lambda *refs: stats_kernel(*refs, far=far), where, (activations, cotangents), packed)[0]
+        return call(lambda *refs: stats_kernel(*refs, far=far), where, (activations, cotangents), packed,
+                    flops=2 * activations.shape[0] * order * order)[0]
 
     arrived = swap(stats(True))
     held = stats(False)
@@ -285,20 +334,25 @@
     near = jnp.concatenate([kept, send(kept, (2, 1))], 0)
     far = send(near, (1, 2))
 
-    share = jnp.concatenate([near[:, :outs], far[:, :outs]], 0)
-    share_far = swap(share)
+    share = near[:, :2]
+    beside = swap(share)
+    across = cross(share, (1, 2))
+    far, beside, across = fence((far, beside, across))
     mine, theirs, left = call(
-        lambda *refs: input_kernel(*refs, scale=scale, skip=outs),
+        lambda *refs: input_kernel(*refs, scale=scale),
         where,
         (near, far, input_factor, fac_far, gradient, grad_far),
         [(slab, order), (slab, order), (order, rank)],
-        [(packed[0][1] - outs, LANES, LANES), (order, order), (order, rank)],
+        [(packed[0][1], LANES, LANES), (order, order), (order, rank)],
+        heavy,
     )
     new_output, update, update_far = call(
         lambda *refs: output_kernel(*refs, scale=scale),
         where,
-        (share, share_far, output_factor, left),
+        (near, far, beside, across, output_factor, left),
         [(rank, rank), (slab, rank), (slab, rank)],
+        [(2, LANES, LANES), (2, SHARDS, SUBS, LANES)],
+        24 * rank * rank * rank + 6 * order * rank * rank,
     )
     rows_far = swap(theirs)
     update_far = swap(update_far)
@@ -324,7 +378,7 @@
     def on_device(*args):
         nblocks, slab, order = args[2].shape
         rank = args[3].shape[0]
-        fits = nblocks == 2 and order % LANES == 0 and slab % SUBS == 0 and rank % (2 * LANES) == 0
+        fits = nblocks == 2 and order % LANES == 0 and slab % SUBS == 0 and rank == 2 * LANES and order // LANES in (1, 3, 5, 7)
         paired = mesh.shape["grp"] == 2 and mesh.shape["own"] == SHARDS
         return (on_chip_pairs if fits and paired else any_mesh)(*args)
 

time: 83.2 us -> 76.7 us (0.922)
  waiting for transfers between devices: 35.5 us -> 31.2 us
  local copies, waits for them, and re-layouts: 4.11 us -> 1.43 us
    ppermute x10, waiting for transfers between devices: 32.7 us -> 24.1 us  [send(): return lax.ppermute(value, ('grp', 'own'), pairs)]
    ppermute x0 -> x1, waiting for transfers between devices: none -> 5.06 us  [cross(): return lax.ppermute(value, ('grp', 'own'), pairs)]
    slice x2 -> x1, local copies, waits for them, and re-layouts: 1.77 us -> 0.01 us  [on_chip_pairs(): share = near[:, :2]]
    ppermute x6, starting transfers between devices: 1.61 us -> 2.97 us  [swap(): return lax.ppermute(value, 'grp', [(0, 1), (1, 0)])]
    unnamed x27, local copies, waits for them, and re-layouts: 2.23 us -> 1.32 us
    ppermute x10, starting transfers between devices: 18.4 us -> 17.5 us  [send(): return lax.ppermute(value, ('grp', 'own'), pairs)]
  transfers between devices with their start and end apart: 16 -> 17, of which waited for: 14 -> 13; matrix products, arithmetic and copies ran while one was open for 4% -> 2% of each run, Pallas kernels for 8% -> 9%
where the time goes in v3:
time: 76.7 us; the launch traced here: 76.5 us
  waiting for transfers between devices  31.2 us (41%)
  starting transfers between devices  20.5 us (27%)
  Pallas kernels  17.8 us (23%)
  other arithmetic  4.69 us (6%)
  local copies, waits for them, and re-layouts  1.43 us (2%)
  between operations  0.83 us (1%)
    ppermute x10, waiting for transfers between devices, send(): return lax.ppermute(value, ('grp', 'own'), pairs)  24.1 us
    pallas_call x4, Pallas kernels, call(): pl.pallas_call(kernel, out_shape=[jax.ShapeDtypeStruct(shape, jnp.float32...  17.8 us
    ppermute x10, starting transfers between devices, send(): return lax.ppermute(value, ('grp', 'own'), pairs)  17.5 us
    ppermute x1, waiting for transfers between devices, cross(): return lax.ppermute(value, ('grp', 'own'), pairs)  5.06 us
    ppermute x6, starting transfers between devices, swap(): return lax.ppermute(value, 'grp', [(0, 1), (1, 0)])  2.97 us
    ppermute x6, waiting for transfers between devices, swap(): return lax.ppermute(value, 'grp', [(0, 1), (1, 0)])  2.01 us
  transfers between devices with their start and end apart: 17, of which 13 were waited for; matrix products, arithmetic and copies ran while one was open for 2% of the time, Pallas kernels for 9%

profile of v3, /device:TPU:0, one launch (start us, length us, event | category | flops | bytes accessed | tf_op | source)
XLA Modules:
  0.0 76.5 jit_solution(14529089574345549004)
XLA Ops:
  0.7 0.6 pad_add_fusion.refs_0_
  1.3 2.5 %shard_map.103 = f32[16,14,8,128]{3,2,1,0:T(8,128)} custom-call(s32[3]{0:T(128)} %pad_add_fusion.refs_0_, bf16[256,1280]{1,0:T(8,128)(2,1)} %refs_1_.3, bf16[256,256]{1,0:T(8,128)(2,1)} %refs_2_.3), custom_call_target="tpu_custom_call" | custom-call | flops 209715200 | bytes 1703936 | tf_op jit(solution)/shard_map/pallas_call | solution.py:273
  3.7 0.5 collective-permute-start
  4.2 2.5 %shard_map.102 = f32[16,14,8,128]{3,2,1,0:T(8,128)} custom-call(s32[3]{0:T(128)} %pad_add_fusion.refs_0_, bf16[256,1280]{1,0:T(8,128)(2,1)} %refs_1_.3, bf16[256,256]{1,0:T(8,128)(2,1)} %refs_2_.3), custom_call_target="tpu_custom_call" | custom-call | flops 209715200 | bytes 1703936 | tf_op jit(solution)/shard_map/pallas_call | solution.py:273
  6.7 0.0 copy-start.3
  6.7 0.0 copy-start.5
  6.7 0.0 collective-permute-done
  6.7 1.4 %slice_add_fusion = (f32[8,14,8,128]{3,2,1,0:T(8,128)S(1)}, f32[8,14,8,128]{3,2,1,0:T(8,128)S(1)}) fusion(f32[16,14,8,128]{3,2,1,0:T(8,128)S(1)} %collective-permute-done, f32[16,14,8,128]{3,2,1,0:T(8,128)} %shard_map.102), kind=kLoop, calls=%fused_computation.4 | loop fusion | flops 229376 | bytes 2752512 | tf_op jit(solution)/shard_map/add | solution.py:320
  8.1 0.3 copy-done.3
  8.4 0.1 dynamic-slice_bitcast_fusion
  8.5 0.1 collective-permute-start.2
  8.6 3.0 %collective-permute-start.1 = (f32[8,14,8,128]{3,2,1,0:T(8,128)S(1)}, f32[8,14,8,128]{3,2,1,0:T(8,128)S(1)}, u32[]{:S(2)}, u32[]{:S(2)}) collective-permute-start(f32[8,14,8,128]{3,2,1,0:T(8,128)S(1)} %get-tuple-element.38), channel_id=1, source_target_pairs={{0,1},{1,0},{2,3},{3,2},{4,5},{5,4},{6,7},{7,6},{8,9},{9,8},{10,11... | collective-permute-start | bytes 1376264 | tf_op jit(solution)/shard_map/ppermute | solution.py:308
  11.5 0.0 copy-done.5
  11.6 0.1 collective-permute-start.3
  11.6 1.6 %collective-permute-done.3.refs_6_ = f32[320,256]{1,0:T(8,128)S(1)} collective-permute-done((f32[320,256]{1,0:T(8,128)S(1)}, f32[320,256]{1,0:T(8,128)S(1)}, u32[]{:S(2)}, u32[]{:S(2)}) %collective-permute-start.3) | collective-permute-done | bytes 327712 | tf_op jit(solution)/shard_map/ppermute | solution.py:304
  13.3 4.7 %collective-permute-done.1 = f32[8,14,8,128]{3,2,1,0:T(8,128)S(1)} collective-permute-done((f32[8,14,8,128]{3,2,1,0:T(8,128)S(1)}, f32[8,14,8,128]{3,2,1,0:T(8,128)S(1)}, u32[]{:S(2)}, u32[]{:S(2)}) %collective-permute-start.1) | collective-permute-done | bytes 458784 | tf_op jit(solution)/shard_map/ppermute | solution.py:308
  18.0 0.0 collective-permute-done.2.refs_4_
  18.0 0.0 copy-start.7
  18.0 2.1 %collective-permute-start.4 = (f32[4,14,8,128]{3,2,1,0:T(8,128)S(1)}, f32[4,14,8,128]{3,2,1,0:T(8,128)S(1)}, u32[]{:S(2)}, u32[]{:S(2)}) collective-permute-start(f32[4,14,8,128]{3,2,1,0:T(8,128)S(1)} %slice_add_fusion.3), channel_id=1, source_target_pairs={{0,2},{1,3},{2,0},{3,1},{4,6},{5,7},{6,4},{7,5},{8,10},{9,11},{10,... | collective-permute-start | bytes 688136 | tf_op jit(solution)/shard_map/ppermute | solution.py:308
  20.1 4.0 %collective-permute-done.4 = f32[4,14,8,128]{3,2,1,0:T(8,128)S(1)} collective-permute-done((f32[4,14,8,128]{3,2,1,0:T(8,128)S(1)}, f32[4,14,8,128]{3,2,1,0:T(8,128)S(1)}, u32[]{:S(2)}, u32[]{:S(2)}) %collective-permute-start.4) | collective-permute-done | bytes 229408 | tf_op jit(solution)/shard_map/ppermute | solution.py:308
  24.2 4.2 %collective-permute-start.5 = (f32[1,14,8,128]{3,2,1,0:T(8,128)S(1)}, f32[1,14,8,128]{3,2,1,0:T(8,128)S(1)}, u32[]{:S(2)}, u32[]{:S(2)}) collective-permute-start(f32[1,14,8,128]{3,2,1,0:T(8,128)S(1)} %get-tuple-element.40), channel_id=1, source_target_pairs={{0,12},{1,13},{2,14},{3,15},{4,8},{5,9},{6,10},{7,11},{8,4},{9,5},... | collective-permute-start | bytes 172040 | tf_op jit(solution)/shard_map/ppermute | solution.py:308
  28.4 0.0 collective-permute-start.7
  28.4 0.6 collective-permute-start.6
  29.0 1.6 %collective-permute-done.5 = f32[1,14,8,128]{3,2,1,0:T(8,128)S(1)} collective-permute-done((f32[1,14,8,128]{3,2,1,0:T(8,128)S(1)}, f32[1,14,8,128]{3,2,1,0:T(8,128)S(1)}, u32[]{:S(2)}, u32[]{:S(2)}) %collective-permute-start.5) | collective-permute-done | bytes 57376 | tf_op jit(solution)/shard_map/ppermute | solution.py:308
  30.6 1.9 %collective-permute-done.7 = f32[1,14,8,128]{3,2,1,0:T(8,128)S(1)} collective-permute-done((f32[1,14,8,128]{3,2,1,0:T(8,128)S(1)}, f32[1,14,8,128]{3,2,1,0:T(8,128)S(1)}, u32[]{:S(2)}, u32[]{:S(2)}) %collective-permute-start.7) | collective-permute-done | bytes 57376 | tf_op jit(solution)/shard_map/ppermute | solution.py:308
  32.5 0.9 %collective-permute-done.6 = f32[1,14,8,128]{3,2,1,0:T(8,128)S(1)} collective-permute-done((f32[1,14,8,128]{3,2,1,0:T(8,128)S(1)}, f32[1,14,8,128]{3,2,1,0:T(8,128)S(1)}, u32[]{:S(2)}, u32[]{:S(2)}) %collective-permute-start.6) | collective-permute-done | bytes 57376 | tf_op jit(solution)/shard_map/ppermute | solution.py:308
  33.5 1.6 %collective-permute-start.10 = (f32[1,14,8,128]{3,2,1,0:T(8,128)S(1)}, f32[1,14,8,128]{3,2,1,0:T(8,128)S(1)}, u32[]{:S(2)}, u32[]{:S(2)}) collective-permute-start(f32[1,14,8,128]{3,2,1,0:T(8,128)S(1)} %get-tuple-element.37), channel_id=1, source_target_pairs={{0,12},{1,13},{2,14},{3,15},{4,8},{5,9},{6,10},{7,11},{8,4},{9,5},... | collective-permute-start | bytes 172040 | tf_op jit(solution)/shard_map/ppermute | solution.py:308
  35.0 2.0 %collective-permute-start.9 = (f32[1,14,8,128]{3,2,1,0:T(8,128)S(1)}, f32[1,14,8,128]{3,2,1,0:T(8,128)S(1)}, u32[]{:S(2)}, u32[]{:S(2)}) collective-permute-start(f32[1,14,8,128]{3,2,1,0:T(8,128)S(1)} %get-tuple-element.37), channel_id=1, source_target_pairs={{0,8},{1,9},{2,10},{3,11},{4,12},{5,13},{6,14},{7,15},{8,0},{9,1},... | collective-permute-start | bytes 172040 | tf_op jit(solution)/shard_map/ppermute | solution.py:308
  37.1 0.9 %collective-permute-start.8 = (f32[1,14,8,128]{3,2,1,0:T(8,128)S(1)}, f32[1,14,8,128]{3,2,1,0:T(8,128)S(1)}, u32[]{:S(2)}, u32[]{:S(2)}) collective-permute-start(f32[1,14,8,128]{3,2,1,0:T(8,128)S(1)} %get-tuple-element.37), channel_id=1, source_target_pairs={{0,4},{1,5},{2,6},{3,7},{4,0},{5,1},{6,2},{7,3},{8,12},{9,13},{10,... | collective-permute-start | bytes 172040 | tf_op jit(solution)/shard_map/ppermute | solution.py:308
  37.9 1.7 %collective-permute-done.10 = f32[1,14,8,128]{3,2,1,0:T(8,128)S(1)} collective-permute-done((f32[1,14,8,128]{3,2,1,0:T(8,128)S(1)}, f32[1,14,8,128]{3,2,1,0:T(8,128)S(1)}, u32[]{:S(2)}, u32[]{:S(2)}) %collective-permute-start.10) | collective-permute-done | bytes 57376 | tf_op jit(solution)/shard_map/ppermute | solution.py:308
  39.6 1.5 %collective-permute-done.9 = f32[1,14,8,128]{3,2,1,0:T(8,128)S(1)} collective-permute-done((f32[1,14,8,128]{3,2,1,0:T(8,128)S(1)}, f32[1,14,8,128]{3,2,1,0:T(8,128)S(1)}, u32[]{:S(2)}, u32[]{:S(2)}) %collective-permute-start.9) | collective-permute-done | bytes 57376 | tf_op jit(solution)/shard_map/ppermute | solution.py:308
  41.1 0.6 collective-permute-done.8
  41.7 1.6 %collective-permute-start.11 = (f32[4,14,8,128]{3,2,1,0:T(8,128)S(1)}, f32[4,14,8,128]{3,2,1,0:T(8,128)S(1)}, u32[]{:S(2)}, u32[]{:S(2)}) collective-permute-start(f32[4,14,8,128]{3,2,1,0:T(8,128)S(1)} %pad_maximum_fusion), channel_id=1, source_target_pairs={{0,2},{1,3},{2,0},{3,1},{4,6},{5,7},{6,4},{7,5},{8,10},{9,11},{10,... | collective-permute-start | bytes 688136 | tf_op jit(solution)/shard_map/ppermute | solution.py:308
  43.3 6.9 %collective-permute-done.11 = f32[4,14,8,128]{3,2,1,0:T(8,128)S(1)} collective-permute-done((f32[4,14,8,128]{3,2,1,0:T(8,128)S(1)}, f32[4,14,8,128]{3,2,1,0:T(8,128)S(1)}, u32[]{:S(2)}, u32[]{:S(2)}) %collective-permute-start.11) | collective-permute-done | bytes 229408 | tf_op jit(solution)/shard_map/ppermute | solution.py:308
  50.2 0.0 copy-done.9
  50.3 0.0 copy-done.7
  50.3 0.0 copy-start.6
  50.3 1.6 %collective-permute-start.12 = (f32[8,14,8,128]{3,2,1,0:T(8,128)S(1)}, f32[8,14,8,128]{3,2,1,0:T(8,128)S(1)}, u32[]{:S(2)}, u32[]{:S(2)}) collective-permute-start(f32[8,14,8,128]{3,2,1,0:T(8,128)S(1)} %constant_dynamic-update-slice_fusion.refs_1_), channel_id=1, source_target_pairs={{0,1},{1,0},{2,3},{3,2},{4,5},{5,4},{6,7},{7,6},{8,9},{9,8},{10,11... | collective-permute-start | bytes 1376264 | tf_op jit(solution)/shard_map/ppermute | solution.py:308
  51.8 0.0 collective-permute-start.14
  51.8 1.6 %collective-permute-start.13 = (f32[8,2,8,128]{3,2,1,0:T(8,128)S(1)}, f32[8,2,8,128]{3,2,1,0:T(8,128)S(1)}, u32[]{:S(2)}, u32[]{:S(2)}) collective-permute-start(f32[8,2,8,128]{3,2,1,0:T(8,128)S(1)} %slice.62), channel_id=1, source_target_pairs={{0,16},{16,0},{1,17},{17,1},{2,18},{18,2},{3,19},{19,3},{4,20},{20... | collective-permute-start | bytes 196616 | tf_op jit(solution)/shard_map/ppermute | solution.py:304
  53.5 5.1 %collective-permute-done.14.refs_4_ = f32[8,2,8,128]{3,2,1,0:T(8,128)S(1)} collective-permute-done((f32[8,2,8,128]{3,2,1,0:T(8,128)S(1)}, f32[8,2,8,128]{3,2,1,0:T(8,128)S(1)}, u32[]{:S(2)}, u32[]{:S(2)}) %collective-permute-start.14) | collective-permute-done | bytes 65568 | tf_op jit(solution)/shard_map/ppermute | solution.py:312
  58.5 0.0 copy-start.10
  58.5 0.0 collective-permute-done.13.refs_3_
  58.5 0.3 collective-permute-done.12.refs_2_
  58.8 0.0 copy-done.6
  58.8 0.8 %copy-done.8 = f32[8,14,8,128]{3,2,1,0:T(8,128)} copy-done((f32[8,14,8,128]{3,2,1,0:T(8,128)}, f32[8,14,8,128]{3,2,1,0:T(8,128)S(1)}, u32[]{:S(2)}) %copy-start.8) | copy-done | bytes 458776
  59.6 8.8 %shard_map.104 = (f32[320,640]{1,0:T(8,128)}, f32[320,640]{1,0:T(8,128)}, f32[640,256]{1,0:T(8,128)}) custom-call(s32[3]{0:T(128)} %pad_add_fusion.refs_0_, f32[8,14,8,128]{3,2,1,0:T(8,128)} %copy-done.6, f32[8,14,8,128]{3,2,1,0:T(8,128)} %copy-done.8, f32[2,320,640]{2,1,0:T(8,128)} %refs_3_.1, f32[320,640]{1,0:T(8,128)} %copy-done.7, ...), custom_call_target="tpu_custom_call" | custom-call | flops 4089446400 | bytes 6651904 | tf_op jit(solution)/shard_map/pallas_call | solution.py:273
  68.4 0.0 copy-done.10
  68.4 0.0 copy-done.11
  68.4 0.0 copy-start
  68.5 0.6 collective-permute-start.16
  69.1 4.1 %shard_map.105 = (f32[256,256]{1,0:T(8,128)}, f32[320,256]{1,0:T(8,128)}, f32[320,256]{1,0:T(8,128)}) custom-call(s32[3]{0:T(128)} %pad_add_fusion.refs_0_, f32[8,14,8,128]{3,2,1,0:T(8,128)} %copy-done.6, f32[8,14,8,128]{3,2,1,0:T(8,128)} %copy-done.8, f32[8,2,8,128]{3,2,1,0:T(8,128)} %copy-done.11, f32[8,2,8,128]{3,2,1,0:T(8,128)} %copy-done.10, ...), custom_call_target="tpu_custom_call" | custom-call | flops 654311424 | bytes 2883584 | tf_op jit(solution)/shard_map/pallas_call | solution.py:273
  73.1 0.1 collective-permute-start.15
  73.2 0.0 collective-permute-done.16
  73.2 0.0 copy-done
  73.2 0.0 copy-start.1
  73.2 0.0 copy-start.2
  73.2 0.0 copy-start.4
  73.3 1.3 %broadcast_select_fusion = f32[2,320,640]{2,1,0:T(8,128)} fusion(f32[320,640]{1,0:T(8,128)S(1)} %collective-permute-done.16, f32[320,640]{1,0:T(8,128)S(1)} %copy-done, pred[2]{0:T(512)(128)(4,1)S(1)} %iota_compare_fusion), kind=kLoop, calls=%fused_computation | loop fusion | flops 409600 | bytes 3276802 | tf_op jit(solution)/shard_map/jit(_where)/select_n | solution.py:360
  74.6 0.4 collective-permute-done.15
  75.0 0.0 copy-done.1
  75.0 0.0 copy-done.2
  75.0 0.2 copy-done.4
  75.2 1.3 %multiply_subtract_fusion = (f32[2,320,256]{2,1,0:T(8,128)}, f32[2,320,256]{2,1,0:T(8,128)}) fusion(f32[2,320,256]{2,1,0:T(8,128)S(1)} %copy-done.1, f32[320,256]{1,0:T(8,128)S(1)} %collective-permute-done.15, f32[320,256]{1,0:T(8,128)S(1)} %copy-done.4, pred[2]{0:T(512)(128)(4,1)S(1)} %iota_compare_fusion, f32[2,320,256]{2,1,0:T(8,128)S(1)} %copy-done.2), kind=kLoop, calls=%fused_computation.2 | loop fusion | flops 819200 | bytes 3276802 | tf_op jit(solution)/shard_map/sub | solution.py:363
  (15 shorter events, 0.2 us)
Async XLA Ops:
  3.7 3.0 %collective-permute-start = (f32[16,14,8,128]{3,2,1,0:T(8,128)}, f32[16,14,8,128]{3,2,1,0:T(8,128)S(1)}, u32[]{:S(2)}, u32[]{:S(2)}) collective-permute-start(f32[16,14,8,128]{3,2,1,0:T(8,128)} %shard_map.103), channel_id=1, source_target_pairs={{0,16},{16,0},{1,17},{17,1},{2,18},{18,2},{3,19},{19,3},{4,20},{20... | collective-permute-start | bytes 2752520 | tf_op jit(solution)/shard_map/ppermute | solution.py:304
  6.7 1.7 %copy-start.3 = (f32[2,320,640]{2,1,0:T(8,128)S(1)}, f32[2,320,640]{2,1,0:T(8,128)}, u32[]{:S(2)}) copy-start(f32[2,320,640]{2,1,0:T(8,128)} %refs_3_.1) | copy-start | bytes 4915204
  6.7 4.8 %copy-start.5 = (f32[2,320,256]{2,1,0:T(8,128)S(1)}, f32[2,320,256]{2,1,0:T(8,128)}, u32[]{:S(2)}) copy-start(f32[2,320,256]{2,1,0:T(8,128)} %refs_5_.2) | copy-start | bytes 1966084
  8.5 9.5 %collective-permute-start.2 = (f32[320,640]{1,0:T(8,128)S(1)}, f32[320,640]{1,0:T(8,128)S(1)}, u32[]{:S(2)}, u32[]{:S(2)}) collective-permute-start(f32[320,640]{1,0:T(8,128)S(1)} %dynamic-slice_bitcast_fusion), channel_id=1, source_target_pairs={{0,16},{16,0},{1,17},{17,1},{2,18},{18,2},{3,19},{19,3},{4,20},{20... | collective-permute-start | bytes 2457608 | tf_op jit(solution)/shard_map/ppermute | solution.py:304
  8.6 9.4 %collective-permute-start.1 = (f32[8,14,8,128]{3,2,1,0:T(8,128)S(1)}, f32[8,14,8,128]{3,2,1,0:T(8,128)S(1)}, u32[]{:S(2)}, u32[]{:S(2)}) collective-permute-start(f32[8,14,8,128]{3,2,1,0:T(8,128)S(1)} %get-tuple-element.38), channel_id=1, source_target_pairs={{0,1},{1,0},{2,3},{3,2},{4,5},{5,4},{6,7},{7,6},{8,9},{9,8},{10,11... | collective-permute-start | bytes 1376264 | tf_op jit(solution)/shard_map/ppermute | solution.py:308
  11.6 1.7 %collective-permute-start.3 = (f32[320,256]{1,0:T(8,128)S(1)}, f32[320,256]{1,0:T(8,128)S(1)}, u32[]{:S(2)}, u32[]{:S(2)}) collective-permute-start(f32[320,256]{1,0:T(8,128)S(1)} %dynamic-slice_bitcast_fusion.1), channel_id=1, source_target_pairs={{0,16},{16,0},{1,17},{17,1},{2,18},{18,2},{3,19},{19,3},{4,20},{20... | collective-permute-start | bytes 983048 | tf_op jit(solution)/shard_map/ppermute | solution.py:304
  13.2 37.0 %copy-start.9 = (f32[320,256]{1,0:T(8,128)}, f32[320,256]{1,0:T(8,128)S(1)}, u32[]{:S(2)}) copy-start(f32[320,256]{1,0:T(8,128)S(1)} %collective-permute-done.3.refs_6_) | copy-start | bytes 983044
  18.0 32.3 %copy-start.7 = (f32[320,640]{1,0:T(8,128)}, f32[320,640]{1,0:T(8,128)S(1)}, u32[]{:S(2)}) copy-start(f32[320,640]{1,0:T(8,128)S(1)} %collective-permute-done.2.refs_4_) | copy-start | bytes 2457604
  18.0 6.1 %collective-permute-start.4 = (f32[4,14,8,128]{3,2,1,0:T(8,128)S(1)}, f32[4,14,8,128]{3,2,1,0:T(8,128)S(1)}, u32[]{:S(2)}, u32[]{:S(2)}) collective-permute-start(f32[4,14,8,128]{3,2,1,0:T(8,128)S(1)} %slice_add_fusion.3), channel_id=1, source_target_pairs={{0,2},{1,3},{2,0},{3,1},{4,6},{5,7},{6,4},{7,5},{8,10},{9,11},{10,... | collective-permute-start | bytes 688136 | tf_op jit(solution)/shard_map/ppermute | solution.py:308
  24.2 6.4 %collective-permute-start.5 = (f32[1,14,8,128]{3,2,1,0:T(8,128)S(1)}, f32[1,14,8,128]{3,2,1,0:T(8,128)S(1)}, u32[]{:S(2)}, u32[]{:S(2)}) collective-permute-start(f32[1,14,8,128]{3,2,1,0:T(8,128)S(1)} %get-tuple-element.40), channel_id=1, source_target_pairs={{0,12},{1,13},{2,14},{3,15},{4,8},{5,9},{6,10},{7,11},{8,4},{9,5},... | collective-permute-start | bytes 172040 | tf_op jit(solution)/shard_map/ppermute | solution.py:308
  28.4 4.2 %collective-permute-start.7 = (f32[1,14,8,128]{3,2,1,0:T(8,128)S(1)}, f32[1,14,8,128]{3,2,1,0:T(8,128)S(1)}, u32[]{:S(2)}, u32[]{:S(2)}) collective-permute-start(f32[1,14,8,128]{3,2,1,0:T(8,128)S(1)} %get-tuple-element.41), channel_id=1, source_target_pairs={{0,4},{1,5},{2,6},{3,7},{4,0},{5,1},{6,2},{7,3},{8,12},{9,13},{10,... | collective-permute-start | bytes 172040 | tf_op jit(solution)/shard_map/ppermute | solution.py:308
  28.4 5.1 %collective-permute-start.6 = (f32[1,14,8,128]{3,2,1,0:T(8,128)S(1)}, f32[1,14,8,128]{3,2,1,0:T(8,128)S(1)}, u32[]{:S(2)}, u32[]{:S(2)}) collective-permute-start(f32[1,14,8,128]{3,2,1,0:T(8,128)S(1)} %get-tuple-element.42), channel_id=1, source_target_pairs={{0,8},{1,9},{2,10},{3,11},{4,12},{5,13},{6,14},{7,15},{8,0},{9,1},... | collective-permute-start | bytes 172040 | tf_op jit(solution)/shard_map/ppermute | solution.py:308
  33.5 6.1 %collective-permute-start.10 = (f32[1,14,8,128]{3,2,1,0:T(8,128)S(1)}, f32[1,14,8,128]{3,2,1,0:T(8,128)S(1)}, u32[]{:S(2)}, u32[]{:S(2)}) collective-permute-start(f32[1,14,8,128]{3,2,1,0:T(8,128)S(1)} %get-tuple-element.37), channel_id=1, source_target_pairs={{0,12},{1,13},{2,14},{3,15},{4,8},{5,9},{6,10},{7,11},{8,4},{9,5},... | collective-permute-start | bytes 172040 | tf_op jit(solution)/shard_map/ppermute | solution.py:308
  35.0 6.1 %collective-permute-start.9 = (f32[1,14,8,128]{3,2,1,0:T(8,128)S(1)}, f32[1,14,8,128]{3,2,1,0:T(8,128)S(1)}, u32[]{:S(2)}, u32[]{:S(2)}) collective-permute-start(f32[1,14,8,128]{3,2,1,0:T(8,128)S(1)} %get-tuple-element.37), channel_id=1, source_target_pairs={{0,8},{1,9},{2,10},{3,11},{4,12},{5,13},{6,14},{7,15},{8,0},{9,1},... | collective-permute-start | bytes 172040 | tf_op jit(solution)/shard_map/ppermute | solution.py:308
  37.1 4.6 %collective-permute-start.8 = (f32[1,14,8,128]{3,2,1,0:T(8,128)S(1)}, f32[1,14,8,128]{3,2,1,0:T(8,128)S(1)}, u32[]{:S(2)}, u32[]{:S(2)}) collective-permute-start(f32[1,14,8,128]{3,2,1,0:T(8,128)S(1)} %get-tuple-element.37), channel_id=1, source_target_pairs={{0,4},{1,5},{2,6},{3,7},{4,0},{5,1},{6,2},{7,3},{8,12},{9,13},{10,... | collective-permute-start | bytes 172040 | tf_op jit(solution)/shard_map/ppermute | solution.py:308
  41.7 8.5 %collective-permute-start.11 = (f32[4,14,8,128]{3,2,1,0:T(8,128)S(1)}, f32[4,14,8,128]{3,2,1,0:T(8,128)S(1)}, u32[]{:S(2)}, u32[]{:S(2)}) collective-permute-start(f32[4,14,8,128]{3,2,1,0:T(8,128)S(1)} %pad_maximum_fusion), channel_id=1, source_target_pairs={{0,2},{1,3},{2,0},{3,1},{4,6},{5,7},{6,4},{7,5},{8,10},{9,11},{10,... | collective-permute-start | bytes 688136 | tf_op jit(solution)/shard_map/ppermute | solution.py:308
  50.3 8.6 %copy-start.6 = (f32[8,14,8,128]{3,2,1,0:T(8,128)}, f32[8,14,8,128]{3,2,1,0:T(8,128)S(1)}, u32[]{:S(2)}) copy-start(f32[8,14,8,128]{3,2,1,0:T(8,128)S(1)} %constant_dynamic-update-slice_fusion.refs_1_) | copy-start | bytes 1376260
  50.3 8.5 %collective-permute-start.12 = (f32[8,14,8,128]{3,2,1,0:T(8,128)S(1)}, f32[8,14,8,128]{3,2,1,0:T(8,128)S(1)}, u32[]{:S(2)}, u32[]{:S(2)}) collective-permute-start(f32[8,14,8,128]{3,2,1,0:T(8,128)S(1)} %constant_dynamic-update-slice_fusion.refs_1_), channel_id=1, source_target_pairs={{0,1},{1,0},{2,3},{3,2},{4,5},{5,4},{6,7},{7,6},{8,9},{9,8},{10,11... | collective-permute-start | bytes 1376264 | tf_op jit(solution)/shard_map/ppermute | solution.py:308
  51.8 6.7 %collective-permute-start.14 = (f32[8,2,8,128]{3,2,1,0:T(8,128)S(1)}, f32[8,2,8,128]{3,2,1,0:T(8,128)S(1)}, u32[]{:S(2)}, u32[]{:S(2)}) collective-permute-start(f32[8,2,8,128]{3,2,1,0:T(8,128)S(1)} %slice.62), channel_id=1, source_target_pairs={{0,17},{1,16},{2,19},{3,18},{4,21},{5,20},{6,23},{7,22},{8,25},{9,... | collective-permute-start | bytes 196616 | tf_op jit(solution)/shard_map/ppermute | solution.py:312
  51.8 6.7 %collective-permute-start.13 = (f32[8,2,8,128]{3,2,1,0:T(8,128)S(1)}, f32[8,2,8,128]{3,2,1,0:T(8,128)S(1)}, u32[]{:S(2)}, u32[]{:S(2)}) collective-permute-start(f32[8,2,8,128]{3,2,1,0:T(8,128)S(1)} %slice.62), channel_id=1, source_target_pairs={{0,16},{16,0},{1,17},{17,1},{2,18},{18,2},{3,19},{19,3},{4,20},{20... | collective-permute-start | bytes 196616 | tf_op jit(solution)/shard_map/ppermute | solution.py:304
  58.5 9.9 %copy-start.10 = (f32[8,2,8,128]{3,2,1,0:T(8,128)}, f32[8,2,8,128]{3,2,1,0:T(8,128)S(1)}, u32[]{:S(2)}) copy-start(f32[8,2,8,128]{3,2,1,0:T(8,128)S(1)} %collective-permute-done.14.refs_4_) | copy-start | bytes 196612
  58.5 9.9 %copy-start.11 = (f32[8,2,8,128]{3,2,1,0:T(8,128)}, f32[8,2,8,128]{3,2,1,0:T(8,128)S(1)}, u32[]{:S(2)}) copy-start(f32[8,2,8,128]{3,2,1,0:T(8,128)S(1)} %collective-permute-done.13.refs_3_) | copy-start | bytes 196612
  58.8 0.8 %copy-start.8 = (f32[8,14,8,128]{3,2,1,0:T(8,128)}, f32[8,14,8,128]{3,2,1,0:T(8,128)S(1)}, u32[]{:S(2)}) copy-start(f32[8,14,8,128]{3,2,1,0:T(8,128)S(1)} %collective-permute-done.12.refs_2_) | copy-start | bytes 1376260
  68.4 4.8 %copy-start = (f32[320,640]{1,0:T(8,128)S(1)}, f32[320,640]{1,0:T(8,128)}, u32[]{:S(2)}) copy-start(f32[320,640]{1,0:T(8,128)} %get-tuple-element.30) | copy-start | bytes 2457604
  68.5 4.8 %collective-permute-start.16 = (f32[320,640]{1,0:T(8,128)}, f32[320,640]{1,0:T(8,128)S(1)}, u32[]{:S(2)}, u32[]{:S(2)}) collective-permute-start(f32[320,640]{1,0:T(8,128)} %get-tuple-element.31), channel_id=1, source_target_pairs={{0,16},{16,0},{1,17},{17,1},{2,18},{18,2},{3,19},{19,3},{4,20},{20... | collective-permute-start | bytes 2457608 | tf_op jit(solution)/shard_map/ppermute | solution.py:304
  73.1 1.8 %collective-permute-start.15 = (f32[320,256]{1,0:T(8,128)}, f32[320,256]{1,0:T(8,128)S(1)}, u32[]{:S(2)}, u32[]{:S(2)}) collective-permute-start(f32[320,256]{1,0:T(8,128)} %get-tuple-element.29), channel_id=1, source_target_pairs={{0,16},{16,0},{1,17},{17,1},{2,18},{18,2},{3,19},{19,3},{4,20},{20... | collective-permute-start | bytes 983048 | tf_op jit(solution)/shard_map/ppermute | solution.py:304
  73.2 1.8 %copy-start.1 = (f32[2,320,256]{2,1,0:T(8,128)S(1)}, f32[2,320,256]{2,1,0:T(8,128)}, u32[]{:S(2)}) copy-start(f32[2,320,256]{2,1,0:T(8,128)} %param.12) | copy-start | bytes 1966084
  73.2 1.7 %copy-start.2 = (f32[2,320,256]{2,1,0:T(8,128)S(1)}, f32[2,320,256]{2,1,0:T(8,128)}, u32[]{:S(2)}) copy-start(f32[2,320,256]{2,1,0:T(8,128)} %param.13) | copy-start | bytes 1966084
  73.2 1.9 %copy-start.4 = (f32[320,256]{1,0:T(8,128)S(1)}, f32[320,256]{1,0:T(8,128)}, u32[]{:S(2)}) copy-start(f32[320,256]{1,0:T(8,128)} %get-tuple-element.28) | copy-start | bytes 983044

commit v4 on v3

--- a/solution.py
+++ b/solution.py
@@ -1,5 +1,3 @@
-import math
-
 import jax
 import jax.numpy as jnp
 from jax import lax
@@ -226,7 +224,7 @@
     left_ref[...] = (grad + once - apply3(twice, once)) * over
 
 
-def output_kernel(where_ref, near_ref, far_ref, other_near_ref, other_far_ref, fac_ref, left_ref, new_ref, mine_ref, theirs_ref,
+def output_kernel(where_ref, near_ref, far_ref, other_near_ref, other_far_ref, fac_ref, left_ref, _, new_ref, mine_ref, theirs_ref,
                   tile_scr, half_scr, *, scale):
     block = where_ref[0]
     few = SUBS // 2
@@ -269,14 +267,15 @@
 
 
 def call(kernel, where, args, outs, scratch=(), flops=0):
-    size = sum(arg.size * arg.dtype.itemsize for arg in args) + sum(4 * math.prod(shape) for shape in outs)
+    outs = [jax.ShapeDtypeStruct(shape, jnp.float32) for shape in outs]
+    size = sum(array.size * array.dtype.itemsize for array in (*args, *outs))
     return pl.pallas_call(
         kernel,
-        out_shape=[jax.ShapeDtypeStruct(shape, jnp.float32) for shape in outs],
-        in_specs=[pl.BlockSpec(memory_space=pltpu.SMEM)]
-        + [pl.BlockSpec(memory_space=pltpu.VMEM)] * len(args),
+        out_shape=outs,
+        in_specs=[pl.BlockSpec(memory_space=pltpu.SMEM)] + [pl.BlockSpec(memory_space=pltpu.VMEM)] * len(args),
         out_specs=[pl.BlockSpec(memory_space=pltpu.VMEM)] * len(outs),
         scratch_shapes=[pltpu.VMEM(shape, jnp.float32) for shape in scratch],
+        compiler_params=pltpu.CompilerParams(vmem_limit_bytes=24 << 20),
         cost_estimate=pl.CostEstimate(flops=flops, bytes_accessed=size, transcendentals=0),
     )(where, *args)
 
@@ -311,26 +310,27 @@
         pairs = [(g * peers + o, (1 - g) * peers + (o ^ flips[g])) for g in range(2) for o in range(peers)]
         return lax.ppermute(value, ("grp", "own"), pairs)
 
-    def stats(far):
-        return call(lambda *refs: stats_kernel(*refs, far=far), where, (activations, cotangents), packed,
-                    flops=2 * activations.shape[0] * order * order)[0]
-
-    arrived = swap(stats(True))
-    held = stats(False)
-    going = held[8:] + arrived[8:]
+    samples_in = (activations, cotangents)
+    work = 2 * activations.shape[0] * order * order
+    (theirs,) = call(lambda *refs: stats_kernel(*refs, far=True), where, samples_in, packed, (), work)
+    arrived = swap(theirs[8:]), swap(theirs[:8])
+    (held,) = call(lambda *refs: stats_kernel(*refs, far=False), where, samples_in, packed, (), work)
+    going = held[8:] + arrived[0]
+    kept = held[:8] + arrived[1]
     came = send(going, (1, 2))
-    fac_rows, grad_rows, _ = fence((input_factor, gradient, going))
+    fac_rows, grad_rows, kept = fence((input_factor, gradient, kept))
     fac_far = swap(lax.dynamic_index_in_dim(fac_rows, 1 - group, 0, False))
     grad_far = swap(lax.dynamic_index_in_dim(grad_rows, 1 - group, 0, False))
     came, fac_far, grad_far = fence((came, fac_far, grad_far))
-    kept = held[:8] + arrived[:8]
     came = send(kept[4:] + came[4:], (2, 1)), kept[:4] + came[:4]
     kept = came[0] + came[1]
     ways = (3, 2, 1)
     pieces = {d: send(kept[d : d + 1], (4 * d, 4 * d)) for d in ways}
     kept = kept[:1] + pieces[3] + pieces[2] + pieces[1]
     pieces = {d: send(kept, (4 * d, 4 * d)) for d in ways}
+    pace = swap(pieces[3][:, :1])
     kept = jnp.concatenate([kept, pieces[1], pieces[2], pieces[3]], 0)
+    kept, pace = fence((kept, pace))
     near = jnp.concatenate([kept, send(kept, (2, 1))], 0)
     far = send(near, (1, 2))
 
@@ -349,7 +349,7 @@
     new_output, update, update_far = call(
         lambda *refs: output_kernel(*refs, scale=scale),
         where,
-        (near, far, beside, across, output_factor, left),
+        (near, far, beside, across, output_factor, left, pace),
         [(rank, rank), (slab, rank), (slab, rank)],
         [(2, LANES, LANES), (2, SHARDS, SUBS, LANES)],
         24 * rank * rank * rank + 6 * order * rank * rank,

time: 76.7 us -> 67.5 us (0.88)
  Pallas kernels: 17.8 us -> 10.5 us
  other arithmetic: 4.69 us -> 2.89 us
  waiting for transfers between devices: 31.2 us -> 29.6 us
  local copies, waits for them, and re-layouts: 1.43 us -> 2.65 us
    pallas_call x4, Pallas kernels: 17.8 us -> 10.5 us  [call(): pl.pallas_call(kernel, out_shape=outs, in_specs=[pl.BlockSpec(memory_spac...]
    ppermute x10, waiting for transfers between devices: 24.1 us -> 21.9 us  [send(): return lax.ppermute(value, ('grp', 'own'), pairs)]
    add x1 -> x2, other arithmetic: 1.4 us -> 0.11 us  [the longest x1 0.1 us: on_chip_pairs(): kept = held[:8] + arrived[1]]
    unnamed x27 -> x19, local copies, waits for them, and re-layouts: 1.32 us -> 2.48 us
    ppermute x6 -> x8, starting transfers between devices: 2.97 us -> 3.69 us  [swap(): return lax.ppermute(value, 'grp', [(0, 1), (1, 0)])]
    ppermute x6 -> x8, waiting for transfers between devices: 2.01 us -> 2.71 us  [swap(): return lax.ppermute(value, 'grp', [(0, 1), (1, 0)])]
  transfers between devices with their start and end apart: 17 -> 19, of which waited for: 13 -> 15; matrix products, arithmetic and copies ran while one was open for 2% -> 2% of each run, Pallas kernels for 9% -> 5%
where the time goes in v4:
time: 67.5 us; the launch traced here: 67.3 us
  waiting for transfers between devices  29.6 us (44%)
  starting transfers between devices  20.8 us (31%)
  Pallas kernels  10.5 us (16%)
  other arithmetic  2.89 us (4%)
  local copies, waits for them, and re-layouts  2.65 us (4%)
  between operations  0.84 us (1%)
    ppermute x10, waiting for transfers between devices, send(): return lax.ppermute(value, ('grp', 'own'), pairs)  21.9 us
    ppermute x10, starting transfers between devices, send(): return lax.ppermute(value, ('grp', 'own'), pairs)  17.1 us
    pallas_call x4, Pallas kernels, call(): pl.pallas_call(kernel, out_shape=outs, in_specs=[pl.BlockSpec(memory_spac...  10.5 us
    ppermute x1, waiting for transfers between devices, cross(): return lax.ppermute(value, ('grp', 'own'), pairs)  5.01 us
    ppermute x8, starting transfers between devices, swap(): return lax.ppermute(value, 'grp', [(0, 1), (1, 0)])  3.69 us
    ppermute x8, waiting for transfers between devices, swap(): return lax.ppermute(value, 'grp', [(0, 1), (1, 0)])  2.71 us
    unnamed x19, local copies, waits for them, and re-layouts  2.48 us
  transfers between devices with their start and end apart: 19, of which 15 were waited for; matrix products, arithmetic and copies ran while one was open for 2% of the time, Pallas kernels for 5%

profile of v4, /device:TPU:0, one launch (start us, length us, event | category | flops | bytes accessed | tf_op | source)
XLA Modules:
  0.0 67.3 jit_solution(3483272310656676804)
XLA Ops:
  0.7 0.1 pad_add_fusion.refs_0_
  0.8 0.0 copy-start
  0.8 1.1 %copy-done = bf16[256,1280]{1,0:T(8,128)(2,1)S(1)} copy-done((bf16[256,1280]{1,0:T(8,128)(2,1)S(1)}, bf16[256,1280]{1,0:T(8,128)(2,1)}, u32[]{:S(2)}) %copy-start) | copy-done | bytes 655384
  1.8 0.0 copy-start.2
  1.9 0.9 %copy-done.2 = bf16[256,256]{1,0:T(8,128)(2,1)S(1)} copy-done((bf16[256,256]{1,0:T(8,128)(2,1)S(1)}, bf16[256,256]{1,0:T(8,128)(2,1)}, u32[]{:S(2)}) %copy-start.2) | copy-done | bytes 131096
  2.8 0.0 copy-start.1
  2.8 1.0 %shard_map.103 = f32[16,14,8,128]{3,2,1,0:T(8,128)S(1)} custom-call(s32[3]{0:T(128)S(1)} %pad_add_fusion.refs_0_, bf16[256,1280]{1,0:T(8,128)(2,1)S(1)} %copy-done, bf16[256,256]{1,0:T(8,128)(2,1)S(1)} %copy-done.2), custom_call_target="tpu_custom_call" | custom-call | flops 209715200 | bytes 1703936 | tf_op jit(solution)/shard_map/pallas_call | solution.py:272
  3.7 0.1 fusion.2
  3.8 0.6 collective-permute-start
  4.4 0.1 collective-permute-start.1
  4.4 0.0 copy-done.1
  4.4 0.0 copy-done.3
  4.4 1.0 %shard_map.102 = f32[16,14,8,128]{3,2,1,0:T(8,128)S(1)} custom-call(s32[3]{0:T(128)S(1)} %pad_add_fusion.refs_0_, bf16[256,1280]{1,0:T(8,128)(2,1)S(1)} %copy-done.1, bf16[256,256]{1,0:T(8,128)(2,1)S(1)} %copy-done.3), custom_call_target="tpu_custom_call" | custom-call | flops 209715200 | bytes 1703936 | tf_op jit(solution)/shard_map/pallas_call | solution.py:272
  5.4 0.0 copy-start.4
  5.4 0.0 copy-start.5
  5.4 0.4 collective-permute-done
  5.8 0.7 collective-permute-done.1
  6.5 0.1 slice_add_fusion.1
  6.6 0.3 copy-done.4
  6.8 0.1 dynamic-slice_bitcast_fusion
  6.9 0.5 collective-permute-start.3
  7.4 2.6 %collective-permute-start.2 = (f32[8,14,8,128]{3,2,1,0:T(8,128)S(1)}, f32[8,14,8,128]{3,2,1,0:T(8,128)S(1)}, u32[]{:S(2)}, u32[]{:S(2)}) collective-permute-start(f32[8,14,8,128]{3,2,1,0:T(8,128)S(1)} %get-tuple-element.43), channel_id=1, source_target_pairs={{0,1},{1,0},{2,3},{3,2},{4,5},{5,4},{6,7},{7,6},{8,9},{9,8},{10,11... | collective-permute-start | bytes 1376264 | tf_op jit(solution)/shard_map/ppermute | solution.py:307
  10.0 0.0 copy-done.5
  10.0 0.2 collective-permute-start.4
  10.2 1.5 %collective-permute-done.4.refs_6_ = f32[320,256]{1,0:T(8,128)S(1)} collective-permute-done((f32[320,256]{1,0:T(8,128)S(1)}, f32[320,256]{1,0:T(8,128)S(1)}, u32[]{:S(2)}, u32[]{:S(2)}) %collective-permute-start.4) | collective-permute-done | bytes 327712 | tf_op jit(solution)/shard_map/ppermute | solution.py:303
  11.7 4.7 %collective-permute-done.2 = f32[8,14,8,128]{3,2,1,0:T(8,128)S(1)} collective-permute-done((f32[8,14,8,128]{3,2,1,0:T(8,128)S(1)}, f32[8,14,8,128]{3,2,1,0:T(8,128)S(1)}, u32[]{:S(2)}, u32[]{:S(2)}) %collective-permute-start.2) | collective-permute-done | bytes 458784 | tf_op jit(solution)/shard_map/ppermute | solution.py:307
  16.4 0.0 collective-permute-done.3.refs_4_
  16.4 2.1 %collective-permute-start.5 = (f32[4,14,8,128]{3,2,1,0:T(8,128)S(1)}, f32[4,14,8,128]{3,2,1,0:T(8,128)S(1)}, u32[]{:S(2)}, u32[]{:S(2)}) collective-permute-start(f32[4,14,8,128]{3,2,1,0:T(8,128)S(1)} %slice_add_fusion.2), channel_id=1, source_target_pairs={{0,2},{1,3},{2,0},{3,1},{4,6},{5,7},{6,4},{7,5},{8,10},{9,11},{10,... | collective-permute-start | bytes 688136 | tf_op jit(solution)/shard_map/ppermute | solution.py:307
  18.6 4.0 %collective-permute-done.5 = f32[4,14,8,128]{3,2,1,0:T(8,128)S(1)} collective-permute-done((f32[4,14,8,128]{3,2,1,0:T(8,128)S(1)}, f32[4,14,8,128]{3,2,1,0:T(8,128)S(1)}, u32[]{:S(2)}, u32[]{:S(2)}) %collective-permute-start.5) | collective-permute-done | bytes 229408 | tf_op jit(solution)/shard_map/ppermute | solution.py:307
  22.6 4.2 %collective-permute-start.6 = (f32[1,14,8,128]{3,2,1,0:T(8,128)S(1)}, f32[1,14,8,128]{3,2,1,0:T(8,128)S(1)}, u32[]{:S(2)}, u32[]{:S(2)}) collective-permute-start(f32[1,14,8,128]{3,2,1,0:T(8,128)S(1)} %get-tuple-element.46), channel_id=1, source_target_pairs={{0,12},{1,13},{2,14},{3,15},{4,8},{5,9},{6,10},{7,11},{8,4},{9,5},... | collective-permute-start | bytes 172040 | tf_op jit(solution)/shard_map/ppermute | solution.py:307
  26.8 0.0 collective-permute-start.8
  26.8 0.6 collective-permute-start.7
  27.4 1.6 %collective-permute-done.6 = f32[1,14,8,128]{3,2,1,0:T(8,128)S(1)} collective-permute-done((f32[1,14,8,128]{3,2,1,0:T(8,128)S(1)}, f32[1,14,8,128]{3,2,1,0:T(8,128)S(1)}, u32[]{:S(2)}, u32[]{:S(2)}) %collective-permute-start.6) | collective-permute-done | bytes 57376 | tf_op jit(solution)/shard_map/ppermute | solution.py:307
  29.1 1.9 %collective-permute-done.8 = f32[1,14,8,128]{3,2,1,0:T(8,128)S(1)} collective-permute-done((f32[1,14,8,128]{3,2,1,0:T(8,128)S(1)}, f32[1,14,8,128]{3,2,1,0:T(8,128)S(1)}, u32[]{:S(2)}, u32[]{:S(2)}) %collective-permute-start.8) | collective-permute-done | bytes 57376 | tf_op jit(solution)/shard_map/ppermute | solution.py:307
  31.0 0.9 %collective-permute-done.7 = f32[1,14,8,128]{3,2,1,0:T(8,128)S(1)} collective-permute-done((f32[1,14,8,128]{3,2,1,0:T(8,128)S(1)}, f32[1,14,8,128]{3,2,1,0:T(8,128)S(1)}, u32[]{:S(2)}, u32[]{:S(2)}) %collective-permute-start.7) | collective-permute-done | bytes 57376 | tf_op jit(solution)/shard_map/ppermute | solution.py:307
  31.9 2.4 %collective-permute-start.11 = (f32[1,14,8,128]{3,2,1,0:T(8,128)S(1)}, f32[1,14,8,128]{3,2,1,0:T(8,128)S(1)}, u32[]{:S(2)}, u32[]{:S(2)}) collective-permute-start(f32[1,14,8,128]{3,2,1,0:T(8,128)S(1)} %fusion.1), channel_id=1, source_target_pairs={{0,12},{1,13},{2,14},{3,15},{4,8},{5,9},{6,10},{7,11},{8,4},{9,5},... | collective-permute-start | bytes 172040 | tf_op jit(solution)/shard_map/ppermute | solution.py:307
  34.3 1.2 %collective-permute-start.10 = (f32[1,14,8,128]{3,2,1,0:T(8,128)S(1)}, f32[1,14,8,128]{3,2,1,0:T(8,128)S(1)}, u32[]{:S(2)}, u32[]{:S(2)}) collective-permute-start(f32[1,14,8,128]{3,2,1,0:T(8,128)S(1)} %fusion.1), channel_id=1, source_target_pairs={{0,8},{1,9},{2,10},{3,11},{4,12},{5,13},{6,14},{7,15},{8,0},{9,1},... | collective-permute-start | bytes 172040 | tf_op jit(solution)/shard_map/ppermute | solution.py:307
  35.5 0.9 %collective-permute-start.9 = (f32[1,14,8,128]{3,2,1,0:T(8,128)S(1)}, f32[1,14,8,128]{3,2,1,0:T(8,128)S(1)}, u32[]{:S(2)}, u32[]{:S(2)}) collective-permute-start(f32[1,14,8,128]{3,2,1,0:T(8,128)S(1)} %fusion.1), channel_id=1, source_target_pairs={{0,4},{1,5},{2,6},{3,7},{4,0},{5,1},{6,2},{7,3},{8,12},{9,13},{10,... | collective-permute-start | bytes 172040 | tf_op jit(solution)/shard_map/ppermute | solution.py:307
  36.4 2.2 %collective-permute-done.11 = f32[1,14,8,128]{3,2,1,0:T(8,128)S(1)} collective-permute-done((f32[1,14,8,128]{3,2,1,0:T(8,128)S(1)}, f32[1,14,8,128]{3,2,1,0:T(8,128)S(1)}, u32[]{:S(2)}, u32[]{:S(2)}) %collective-permute-start.11) | collective-permute-done | bytes 57376 | tf_op jit(solution)/shard_map/ppermute | solution.py:307
  38.5 0.0 collective-permute-start.12
  38.5 1.4 %collective-permute-done.10 = f32[1,14,8,128]{3,2,1,0:T(8,128)S(1)} collective-permute-done((f32[1,14,8,128]{3,2,1,0:T(8,128)S(1)}, f32[1,14,8,128]{3,2,1,0:T(8,128)S(1)}, u32[]{:S(2)}, u32[]{:S(2)}) %collective-permute-start.10) | collective-permute-done | bytes 57376 | tf_op jit(solution)/shard_map/ppermute | solution.py:307
  39.9 0.4 collective-permute-done.9
  40.3 0.0 collective-permute-done.12.refs_7_
  40.3 1.6 %collective-permute-start.13 = (f32[4,14,8,128]{3,2,1,0:T(8,128)S(1)}, f32[4,14,8,128]{3,2,1,0:T(8,128)S(1)}, u32[]{:S(2)}, u32[]{:S(2)}) collective-permute-start(f32[4,14,8,128]{3,2,1,0:T(8,128)S(1)} %pad_maximum_fusion), channel_id=1, source_target_pairs={{0,2},{1,3},{2,0},{3,1},{4,6},{5,7},{6,4},{7,5},{8,10},{9,11},{10,... | collective-permute-start | bytes 688136 | tf_op jit(solution)/shard_map/ppermute | solution.py:307
  41.9 4.5 %collective-permute-done.13 = f32[4,14,8,128]{3,2,1,0:T(8,128)S(1)} collective-permute-done((f32[4,14,8,128]{3,2,1,0:T(8,128)S(1)}, f32[4,14,8,128]{3,2,1,0:T(8,128)S(1)}, u32[]{:S(2)}, u32[]{:S(2)}) %collective-permute-start.13) | collective-permute-done | bytes 229408 | tf_op jit(solution)/shard_map/ppermute | solution.py:307
  46.4 1.6 %collective-permute-start.14 = (f32[8,14,8,128]{3,2,1,0:T(8,128)S(1)}, f32[8,14,8,128]{3,2,1,0:T(8,128)S(1)}, u32[]{:S(2)}, u32[]{:S(2)}) collective-permute-start(f32[8,14,8,128]{3,2,1,0:T(8,128)S(1)} %constant_dynamic-update-slice_fusion.refs_1_), channel_id=1, source_target_pairs={{0,1},{1,0},{2,3},{3,2},{4,5},{5,4},{6,7},{7,6},{8,9},{9,8},{10,11... | collective-permute-start | bytes 1376264 | tf_op jit(solution)/shard_map/ppermute | solution.py:307
  48.0 0.1 collective-permute-start.16
  48.0 1.6 %collective-permute-start.15 = (f32[8,2,8,128]{3,2,1,0:T(8,128)S(1)}, f32[8,2,8,128]{3,2,1,0:T(8,128)S(1)}, u32[]{:S(2)}, u32[]{:S(2)}) collective-permute-start(f32[8,2,8,128]{3,2,1,0:T(8,128)S(1)} %slice.65), channel_id=1, source_target_pairs={{0,16},{16,0},{1,17},{17,1},{2,18},{18,2},{3,19},{19,3},{4,20},{20... | collective-permute-start | bytes 196616 | tf_op jit(solution)/shard_map/ppermute | solution.py:303
  49.7 5.0 %collective-permute-done.16.refs_4_ = f32[8,2,8,128]{3,2,1,0:T(8,128)S(1)} collective-permute-done((f32[8,2,8,128]{3,2,1,0:T(8,128)S(1)}, f32[8,2,8,128]{3,2,1,0:T(8,128)S(1)}, u32[]{:S(2)}, u32[]{:S(2)}) %collective-permute-start.16) | collective-permute-done | bytes 65568 | tf_op jit(solution)/shard_map/ppermute | solution.py:311
  54.7 0.0 collective-permute-done.15.refs_3_
  54.7 0.3 collective-permute-done.14.refs_2_
  55.0 6.4 %shard_map.104 = (f32[320,640]{1,0:T(8,128)S(1)}, f32[320,640]{1,0:T(8,128)S(1)}, f32[640,256]{1,0:T(8,128)S(1)}) custom-call(s32[3]{0:T(128)S(1)} %pad_add_fusion.refs_0_, f32[8,14,8,128]{3,2,1,0:T(8,128)S(1)} %constant_dynamic-update-slice_fusion.refs_1_, f32[8,14,8,128]{3,2,1,0:T(8,128)S(1)} %collective-permute-done.14.refs_2_, ...), custom_call_target="tpu_custom_call" | custom-call | flops 4089446400 | bytes 6651904 | tf_op jit(solution)/shard_map/pallas_call | solution.py:272
  61.3 0.6 collective-permute-start.18
  61.9 0.0 copy-done.6
  61.9 2.2 %shard_map.105 = (f32[256,256]{1,0:T(8,128)}, f32[320,256]{1,0:T(8,128)S(1)}, f32[320,256]{1,0:T(8,128)S(1)}) custom-call(s32[3]{0:T(128)S(1)} %pad_add_fusion.refs_0_, f32[8,14,8,128]{3,2,1,0:T(8,128)S(1)} %constant_dynamic-update-slice_fusion.refs_1_, f32[8,14,8,128]{3,2,1,0:T(8,128)S(1)} %collective-permute-done.14.refs_2_, ...), custom_call_target="tpu_custom_call" | custom-call | flops 654311424 | bytes 2887680 | tf_op jit(solution)/shard_map/pallas_call | solution.py:272
  64.2 0.1 collective-permute-start.17
  64.3 0.0 collective-permute-done.18
  64.3 0.0 copy-start.7
  64.3 0.0 copy-start.8
  64.3 1.3 %broadcast_select_fusion = f32[2,320,640]{2,1,0:T(8,128)} fusion(f32[320,640]{1,0:T(8,128)S(1)} %collective-permute-done.18, f32[320,640]{1,0:T(8,128)S(1)} %get-tuple-element.36, pred[2]{0:T(512)(128)(4,1)S(1)} %iota_compare_fusion), kind=kLoop, calls=%fused_computation | loop fusion | flops 409600 | bytes 3276802 | tf_op jit(solution)/shard_map/jit(_where)/select_n | solution.py:360
  65.6 0.2 collective-permute-done.17
  65.9 0.0 copy-done.7
  65.9 0.1 copy-done.8
  66.0 1.3 %multiply_subtract_fusion = (f32[2,320,256]{2,1,0:T(8,128)}, f32[2,320,256]{2,1,0:T(8,128)}) fusion(f32[2,320,256]{2,1,0:T(8,128)S(1)} %copy-done.7, f32[320,256]{1,0:T(8,128)S(1)} %collective-permute-done.17, f32[320,256]{1,0:T(8,128)S(1)} %get-tuple-element.34, pred[2]{0:T(512)(128)(4,1)S(1)} %iota_compare_fusion, f32[2,320,256]{2,1,0:T(8,128)S(1)} %copy-done.8), kind=kLoop, calls=%fused_computation.2 | loop fusion | flops 819200 | bytes 3276802 | tf_op jit(solution)/shard_map/sub | solution.py:363
  (13 shorter events, 0.2 us)
Async XLA Ops:
  0.8 1.1 %copy-start = (bf16[256,1280]{1,0:T(8,128)(2,1)S(1)}, bf16[256,1280]{1,0:T(8,128)(2,1)}, u32[]{:S(2)}) copy-start(bf16[256,1280]{1,0:T(8,128)(2,1)} %refs_1_.3) | copy-start | bytes 1966084
  1.8 0.9 %copy-start.2 = (bf16[256,256]{1,0:T(8,128)(2,1)S(1)}, bf16[256,256]{1,0:T(8,128)(2,1)}, u32[]{:S(2)}) copy-start(bf16[256,256]{1,0:T(8,128)(2,1)} %refs_2_.3) | copy-start | bytes 393220
  2.8 1.7 %copy-start.1 = (bf16[256,1280]{1,0:T(8,128)(2,1)S(1)}, bf16[256,1280]{1,0:T(8,128)(2,1)}, u32[]{:S(2)}) copy-start(bf16[256,1280]{1,0:T(8,128)(2,1)} %refs_1_.3) | copy-start | bytes 1966084
  2.8 1.7 %copy-start.3 = (bf16[256,256]{1,0:T(8,128)(2,1)S(1)}, bf16[256,256]{1,0:T(8,128)(2,1)}, u32[]{:S(2)}) copy-start(bf16[256,256]{1,0:T(8,128)(2,1)} %refs_2_.3) | copy-start | bytes 393220
  3.8 2.0 %collective-permute-start = (f32[8,14,8,128]{3,2,1,0:T(8,128)S(1)}, f32[8,14,8,128]{3,2,1,0:T(8,128)S(1)}, u32[]{:S(2)}, u32[]{:S(2)}) collective-permute-start(f32[8,14,8,128]{3,2,1,0:T(8,128)S(1)} %get-tuple-element.44), channel_id=1, source_target_pairs={{0,16},{16,0},{1,17},{17,1},{2,18},{18,2},{3,19},{19,3},{4,20},{20... | collective-permute-start | bytes 1376264 | tf_op jit(solution)/shard_map/ppermute | solution.py:303
  4.4 2.1 %collective-permute-start.1 = (f32[8,14,8,128]{3,2,1,0:T(8,128)S(1)}, f32[8,14,8,128]{3,2,1,0:T(8,128)S(1)}, u32[]{:S(2)}, u32[]{:S(2)}) collective-permute-start(f32[8,14,8,128]{3,2,1,0:T(8,128)S(1)} %get-tuple-element.45), channel_id=1, source_target_pairs={{0,16},{16,0},{1,17},{17,1},{2,18},{18,2},{3,19},{19,3},{4,20},{20... | collective-permute-start | bytes 1376264 | tf_op jit(solution)/shard_map/ppermute | solution.py:303
  5.4 1.4 %copy-start.4 = (f32[2,320,640]{2,1,0:T(8,128)S(1)}, f32[2,320,640]{2,1,0:T(8,128)}, u32[]{:S(2)}) copy-start(f32[2,320,640]{2,1,0:T(8,128)} %refs_3_.1) | copy-start | bytes 4915204
  5.4 4.5 %copy-start.5 = (f32[2,320,256]{2,1,0:T(8,128)S(1)}, f32[2,320,256]{2,1,0:T(8,128)}, u32[]{:S(2)}) copy-start(f32[2,320,256]{2,1,0:T(8,128)} %refs_5_.2) | copy-start | bytes 1966084
  6.9 9.5 %collective-permute-start.3 = (f32[320,640]{1,0:T(8,128)S(1)}, f32[320,640]{1,0:T(8,128)S(1)}, u32[]{:S(2)}, u32[]{:S(2)}) collective-permute-start(f32[320,640]{1,0:T(8,128)S(1)} %dynamic-slice_bitcast_fusion), channel_id=1, source_target_pairs={{0,16},{16,0},{1,17},{17,1},{2,18},{18,2},{3,19},{19,3},{4,20},{20... | collective-permute-start | bytes 2457608 | tf_op jit(solution)/shard_map/ppermute | solution.py:303
  7.4 9.0 %collective-permute-start.2 = (f32[8,14,8,128]{3,2,1,0:T(8,128)S(1)}, f32[8,14,8,128]{3,2,1,0:T(8,128)S(1)}, u32[]{:S(2)}, u32[]{:S(2)}) collective-permute-start(f32[8,14,8,128]{3,2,1,0:T(8,128)S(1)} %get-tuple-element.43), channel_id=1, source_target_pairs={{0,1},{1,0},{2,3},{3,2},{4,5},{5,4},{6,7},{7,6},{8,9},{9,8},{10,11... | collective-permute-start | bytes 1376264 | tf_op jit(solution)/shard_map/ppermute | solution.py:307
  10.0 1.7 %collective-permute-start.4 = (f32[320,256]{1,0:T(8,128)S(1)}, f32[320,256]{1,0:T(8,128)S(1)}, u32[]{:S(2)}, u32[]{:S(2)}) collective-permute-start(f32[320,256]{1,0:T(8,128)S(1)} %dynamic-slice_bitcast_fusion.1), channel_id=1, source_target_pairs={{0,16},{16,0},{1,17},{17,1},{2,18},{18,2},{3,19},{19,3},{4,20},{20... | collective-permute-start | bytes 983048 | tf_op jit(solution)/shard_map/ppermute | solution.py:303
  16.4 6.1 %collective-permute-start.5 = (f32[4,14,8,128]{3,2,1,0:T(8,128)S(1)}, f32[4,14,8,128]{3,2,1,0:T(8,128)S(1)}, u32[]{:S(2)}, u32[]{:S(2)}) collective-permute-start(f32[4,14,8,128]{3,2,1,0:T(8,128)S(1)} %slice_add_fusion.2), channel_id=1, source_target_pairs={{0,2},{1,3},{2,0},{3,1},{4,6},{5,7},{6,4},{7,5},{8,10},{9,11},{10,... | collective-permute-start | bytes 688136 | tf_op jit(solution)/shard_map/ppermute | solution.py:307
  22.6 6.5 %collective-permute-start.6 = (f32[1,14,8,128]{3,2,1,0:T(8,128)S(1)}, f32[1,14,8,128]{3,2,1,0:T(8,128)S(1)}, u32[]{:S(2)}, u32[]{:S(2)}) collective-permute-start(f32[1,14,8,128]{3,2,1,0:T(8,128)S(1)} %get-tuple-element.46), channel_id=1, source_target_pairs={{0,12},{1,13},{2,14},{3,15},{4,8},{5,9},{6,10},{7,11},{8,4},{9,5},... | collective-permute-start | bytes 172040 | tf_op jit(solution)/shard_map/ppermute | solution.py:307
  26.8 4.2 %collective-permute-start.8 = (f32[1,14,8,128]{3,2,1,0:T(8,128)S(1)}, f32[1,14,8,128]{3,2,1,0:T(8,128)S(1)}, u32[]{:S(2)}, u32[]{:S(2)}) collective-permute-start(f32[1,14,8,128]{3,2,1,0:T(8,128)S(1)} %get-tuple-element.47), channel_id=1, source_target_pairs={{0,4},{1,5},{2,6},{3,7},{4,0},{5,1},{6,2},{7,3},{8,12},{9,13},{10,... | collective-permute-start | bytes 172040 | tf_op jit(solution)/shard_map/ppermute | solution.py:307
  26.8 5.1 %collective-permute-start.7 = (f32[1,14,8,128]{3,2,1,0:T(8,128)S(1)}, f32[1,14,8,128]{3,2,1,0:T(8,128)S(1)}, u32[]{:S(2)}, u32[]{:S(2)}) collective-permute-start(f32[1,14,8,128]{3,2,1,0:T(8,128)S(1)} %get-tuple-element.48), channel_id=1, source_target_pairs={{0,8},{1,9},{2,10},{3,11},{4,12},{5,13},{6,14},{7,15},{8,0},{9,1},... | collective-permute-start | bytes 172040 | tf_op jit(solution)/shard_map/ppermute | solution.py:307
  31.9 6.6 %collective-permute-start.11 = (f32[1,14,8,128]{3,2,1,0:T(8,128)S(1)}, f32[1,14,8,128]{3,2,1,0:T(8,128)S(1)}, u32[]{:S(2)}, u32[]{:S(2)}) collective-permute-start(f32[1,14,8,128]{3,2,1,0:T(8,128)S(1)} %fusion.1), channel_id=1, source_target_pairs={{0,12},{1,13},{2,14},{3,15},{4,8},{5,9},{6,10},{7,11},{8,4},{9,5},... | collective-permute-start | bytes 172040 | tf_op jit(solution)/shard_map/ppermute | solution.py:307
  34.3 5.6 %collective-permute-start.10 = (f32[1,14,8,128]{3,2,1,0:T(8,128)S(1)}, f32[1,14,8,128]{3,2,1,0:T(8,128)S(1)}, u32[]{:S(2)}, u32[]{:S(2)}) collective-permute-start(f32[1,14,8,128]{3,2,1,0:T(8,128)S(1)} %fusion.1), channel_id=1, source_target_pairs={{0,8},{1,9},{2,10},{3,11},{4,12},{5,13},{6,14},{7,15},{8,0},{9,1},... | collective-permute-start | bytes 172040 | tf_op jit(solution)/shard_map/ppermute | solution.py:307
  35.5 4.8 %collective-permute-start.9 = (f32[1,14,8,128]{3,2,1,0:T(8,128)S(1)}, f32[1,14,8,128]{3,2,1,0:T(8,128)S(1)}, u32[]{:S(2)}, u32[]{:S(2)}) collective-permute-start(f32[1,14,8,128]{3,2,1,0:T(8,128)S(1)} %fusion.1), channel_id=1, source_target_pairs={{0,4},{1,5},{2,6},{3,7},{4,0},{5,1},{6,2},{7,3},{8,12},{9,13},{10,... | collective-permute-start | bytes 172040 | tf_op jit(solution)/shard_map/ppermute | solution.py:307
  38.5 1.8 %collective-permute-start.12 = (f32[1,1,8,128]{3,2,1,0:T(8,128)S(1)}, f32[1,1,8,128]{3,2,1,0:T(8,128)S(1)}, u32[]{:S(2)}, u32[]{:S(2)}) collective-permute-start(f32[1,1,8,128]{3,2,1,0:T(8,128)S(1)} %slice.64), channel_id=1, source_target_pairs={{0,16},{16,0},{1,17},{17,1},{2,18},{18,2},{3,19},{19,3},{4,20},{20... | collective-permute-start | bytes 12296 | tf_op jit(solution)/shard_map/ppermute | solution.py:303
  40.3 6.1 %collective-permute-start.13 = (f32[4,14,8,128]{3,2,1,0:T(8,128)S(1)}, f32[4,14,8,128]{3,2,1,0:T(8,128)S(1)}, u32[]{:S(2)}, u32[]{:S(2)}) collective-permute-start(f32[4,14,8,128]{3,2,1,0:T(8,128)S(1)} %pad_maximum_fusion), channel_id=1, source_target_pairs={{0,2},{1,3},{2,0},{3,1},{4,6},{5,7},{6,4},{7,5},{8,10},{9,11},{10,... | collective-permute-start | bytes 688136 | tf_op jit(solution)/shard_map/ppermute | solution.py:307
  46.4 8.5 %collective-permute-start.14 = (f32[8,14,8,128]{3,2,1,0:T(8,128)S(1)}, f32[8,14,8,128]{3,2,1,0:T(8,128)S(1)}, u32[]{:S(2)}, u32[]{:S(2)}) collective-permute-start(f32[8,14,8,128]{3,2,1,0:T(8,128)S(1)} %constant_dynamic-update-slice_fusion.refs_1_), channel_id=1, source_target_pairs={{0,1},{1,0},{2,3},{3,2},{4,5},{5,4},{6,7},{7,6},{8,9},{9,8},{10,11... | collective-permute-start | bytes 1376264 | tf_op jit(solution)/shard_map/ppermute | solution.py:307
  48.0 14.0 %copy-start.6 = (f32[256,256]{1,0:T(8,128)S(1)}, f32[256,256]{1,0:T(8,128)}, u32[]{:S(2)}) copy-start(f32[256,256]{1,0:T(8,128)} %refs_5_.3) | copy-start | bytes 786436
  48.0 6.7 %collective-permute-start.16 = (f32[8,2,8,128]{3,2,1,0:T(8,128)S(1)}, f32[8,2,8,128]{3,2,1,0:T(8,128)S(1)}, u32[]{:S(2)}, u32[]{:S(2)}) collective-permute-start(f32[8,2,8,128]{3,2,1,0:T(8,128)S(1)} %slice.65), channel_id=1, source_target_pairs={{0,17},{1,16},{2,19},{3,18},{4,21},{5,20},{6,23},{7,22},{8,25},{9,... | collective-permute-start | bytes 196616 | tf_op jit(solution)/shard_map/ppermute | solution.py:311
  48.0 6.6 %collective-permute-start.15 = (f32[8,2,8,128]{3,2,1,0:T(8,128)S(1)}, f32[8,2,8,128]{3,2,1,0:T(8,128)S(1)}, u32[]{:S(2)}, u32[]{:S(2)}) collective-permute-start(f32[8,2,8,128]{3,2,1,0:T(8,128)S(1)} %slice.65), channel_id=1, source_target_pairs={{0,16},{16,0},{1,17},{17,1},{2,18},{18,2},{3,19},{19,3},{4,20},{20... | collective-permute-start | bytes 196616 | tf_op jit(solution)/shard_map/ppermute | solution.py:303
  61.3 2.9 %collective-permute-start.18 = (f32[320,640]{1,0:T(8,128)S(1)}, f32[320,640]{1,0:T(8,128)S(1)}, u32[]{:S(2)}, u32[]{:S(2)}) collective-permute-start(f32[320,640]{1,0:T(8,128)S(1)} %get-tuple-element.37), channel_id=1, source_target_pairs={{0,16},{16,0},{1,17},{17,1},{2,18},{18,2},{3,19},{19,3},{4,20},{20... | collective-permute-start | bytes 2457608 | tf_op jit(solution)/shard_map/ppermute | solution.py:303
  64.2 1.7 %collective-permute-start.17 = (f32[320,256]{1,0:T(8,128)S(1)}, f32[320,256]{1,0:T(8,128)S(1)}, u32[]{:S(2)}, u32[]{:S(2)}) collective-permute-start(f32[320,256]{1,0:T(8,128)S(1)} %get-tuple-element.35), channel_id=1, source_target_pairs={{0,16},{16,0},{1,17},{17,1},{2,18},{18,2},{3,19},{19,3},{4,20},{20... | collective-permute-start | bytes 983048 | tf_op jit(solution)/shard_map/ppermute | solution.py:303
  64.3 1.6 %copy-start.7 = (f32[2,320,256]{2,1,0:T(8,128)S(1)}, f32[2,320,256]{2,1,0:T(8,128)}, u32[]{:S(2)}) copy-start(f32[2,320,256]{2,1,0:T(8,128)} %param.12) | copy-start | bytes 1966084
  64.3 1.7 %copy-start.8 = (f32[2,320,256]{2,1,0:T(8,128)S(1)}, f32[2,320,256]{2,1,0:T(8,128)}, u32[]{:S(2)}) copy-start(f32[2,320,256]{2,1,0:T(8,128)} %param.13) | copy-start | bytes 1966084

commit v5 on v4

--- a/solution.py
+++ b/solution.py
@@ -90,10 +90,14 @@
     return mul(a[0], b[0]) + (mul(a[0], b[1]) + mul(a[1], b[0]))
 
 
+def long3(a, b):
+    return mul(jnp.concatenate([a[0], a[1], a[0]], 1), jnp.concatenate([b[0], b[0], b[1]], 0))
+
+
 def apply3(a, b):
     b = split(b)
     half = a[0].shape[0] // 2
-    return jnp.concatenate([mul3([v[:half] for v in a], b), mul3([v[half:] for v in a], b)], 0)
+    return jnp.concatenate([long3([v[:half] for v in a], b), long3([v[half:] for v in a], b)], 0)
 
 
 def twice_less_square(value, halves):
@@ -102,7 +106,7 @@
     strips = []
     for end in ends:
         cols = slice(max(end - 2 * LANES, 0), end)
-        square = mul3([v[:end] for v in halves], [v[:, cols] for v in halves])
+        square = long3([v[:end] for v in halves], [v[:, cols] for v in halves])
         strips.append(split(2.0 * value[:end, cols] - square))
     parts = []
     for part in range(2):
@@ -126,7 +130,7 @@
     return rows, cols
 
 
-def stats_kernel(where_ref, act_ref, cot_ref, packed_ref, *, far):
+def stats_kernel(where_ref, act_ref, out_ref, packed_ref, *, far):
     block = 1 - where_ref[0] if far else where_ref[0]
     me = where_ref[2] if far else where_ref[1]
     order = act_ref.shape[1] // 2
@@ -147,11 +151,10 @@
         for j in range(1, tiles - i):
             put(index, strip[:, j * LANES : (j + 1) * LANES])
             index += 1
-    cot = cot_ref[:, pl.ds(pl.multiple_of(block * LANES, LANES), LANES)]
-    diagonal.append(mul(cot.T, cot))
-    upper = mul(cot_ref[:, :LANES].T, cot_ref[:, LANES:])
+    here = pl.ds(pl.multiple_of(block * LANES, LANES), LANES)
+    diagonal.append(out_ref[here, here])
     half = LANES // 2
-    upper = jnp.where(block == 0, upper[:half], upper[half:])
+    upper = out_ref[pl.ds(pl.multiple_of(block * half, SUBS), half), LANES:]
     rows, cols = places_in((LANES, LANES))
     npairs = len(diagonal) // 2
     lines = []
@@ -173,10 +176,10 @@
         put(pl.multiple_of(jnp.bitwise_xor(me, place) * SUBS, SUBS), half[place % half.shape[0]])
 
 
-def input_kernel(where_ref, near_ref, far_ref, fac_ref, fac_far_ref, grad_ref, grad_far_ref,
+def input_kernel(where_ref, near_ref, far_ref, fac_ref, fac_top_ref, fac_low_ref, grad_ref, grad_far_ref,
                  mine_ref, theirs_ref, left_ref, stat_ref, fac_scr, grad_scr, *, scale):
     block, me = where_ref[0], where_ref[1]
-    slab, order = fac_far_ref.shape
+    slab, order = fac_ref.shape[1:]
     tiles = order // LANES
     own_rows = pl.ds(pl.multiple_of(block * slab, SUBS), slab)
     far_rows = pl.ds(pl.multiple_of((1 - block) * slab, SUBS), slab)
@@ -185,7 +188,9 @@
 
     spread(me, (near_ref, far_ref), put)
     fac_scr[own_rows, :] = 0.5 * fac_ref[block]
-    fac_scr[far_rows, :] = 0.5 * fac_far_ref[...]
+    for part, ref in enumerate((fac_top_ref, fac_low_ref)):
+        first = (1 - block) * slab + part * (slab // 2)
+        fac_scr[pl.ds(pl.multiple_of(first, SUBS), slab // 2), :] = 0.5 * ref[...]
     grad_scr[own_rows, :] = grad_ref[block]
     grad_scr[far_rows, :] = grad_far_ref[...]
     at = lambda n: slice(n * LANES, (n + 1) * LANES)
@@ -310,7 +315,8 @@
         pairs = [(g * peers + o, (1 - g) * peers + (o ^ flips[g])) for g in range(2) for o in range(peers)]
         return lax.ppermute(value, ("grp", "own"), pairs)
 
-    samples_in = (activations, cotangents)
+    stat_out = jnp.einsum("ti,tj->ij", cotangents, cotangents, preferred_element_type=jnp.float32)
+    samples_in = (activations, stat_out)
     work = 2 * activations.shape[0] * order * order
     (theirs,) = call(lambda *refs: stats_kernel(*refs, far=True), where, samples_in, packed, (), work)
     arrived = swap(theirs[8:]), swap(theirs[:8])
@@ -318,9 +324,10 @@
     going = held[8:] + arrived[0]
     kept = held[:8] + arrived[1]
     came = send(going, (1, 2))
-    fac_rows, grad_rows, kept = fence((input_factor, gradient, kept))
-    fac_far = swap(lax.dynamic_index_in_dim(fac_rows, 1 - group, 0, False))
-    grad_far = swap(lax.dynamic_index_in_dim(grad_rows, 1 - group, 0, False))
+    fac_rows = lax.dynamic_index_in_dim(input_factor, 1 - group, 0, False)
+    grad_rows = lax.dynamic_index_in_dim(gradient, 1 - group, 0, False)
+    fac_far = swap(fac_rows[: slab // 2]), swap(fac_rows[slab // 2 :])
+    grad_far = swap(grad_rows)
     came, fac_far, grad_far = fence((came, fac_far, grad_far))
     came = send(kept[4:] + came[4:], (2, 1)), kept[:4] + came[:4]
     kept = came[0] + came[1]
@@ -333,7 +340,6 @@
     kept, pace = fence((kept, pace))
     near = jnp.concatenate([kept, send(kept, (2, 1))], 0)
     far = send(near, (1, 2))
-
     share = near[:, :2]
     beside = swap(share)
     across = cross(share, (1, 2))
@@ -341,7 +347,7 @@
     mine, theirs, left = call(
         lambda *refs: input_kernel(*refs, scale=scale),
         where,
-        (near, far, input_factor, fac_far, gradient, grad_far),
+        (near, far, input_factor, *fac_far, gradient, grad_far),
         [(slab, order), (slab, order), (order, rank)],
         [(packed[0][1], LANES, LANES), (order, order), (order, rank)],
         heavy,
@@ -378,7 +384,7 @@
     def on_device(*args):
         nblocks, slab, order = args[2].shape
         rank = args[3].shape[0]
-        fits = nblocks == 2 and order % LANES == 0 and slab % SUBS == 0 and rank == 2 * LANES and order // LANES in (1, 3, 5, 7)
+        fits = nblocks == 2 and order % LANES == 0 and slab % (2 * SUBS) == 0 and rank == 2 * LANES and order // LANES in (1, 3, 5, 7)
         paired = mesh.shape["grp"] == 2 and mesh.shape["own"] == SHARDS
         return (on_chip_pairs if fits and paired else any_mesh)(*args)
 

time: 67.5 us -> 66.5 us (0.985)
  waiting for transfers between devices: 29.6 us -> 28.9 us
    ppermute x10, waiting for transfers between devices: 21.9 us -> 20.5 us  [send(): return lax.ppermute(value, ('grp', 'own'), pairs)]
    ppermute x8 -> x9, waiting for transfers between devices: 2.71 us -> 3.4 us  [swap(): return lax.ppermute(value, 'grp', [(0, 1), (1, 0)])]
    unnamed x19 -> x17, local copies, waits for them, and re-layouts: 2.48 us -> 2.13 us
    ppermute x8 -> x9, starting transfers between devices: 3.69 us -> 3.66 us  [swap(): return lax.ppermute(value, 'grp', [(0, 1), (1, 0)])]
  transfers between devices with their start and end apart: 19 -> 20, of which waited for: 15 -> 15; matrix products, arithmetic and copies ran while one was open for 2% -> 2% of each run, Pallas kernels for 5% -> 5%
where the time goes in v5:
time: 66.5 us; the launch traced here: 66.3 us
  waiting for transfers between devices  28.9 us (43%)
  starting transfers between devices  21.1 us (32%)
  Pallas kernels  10 us (15%)
  other arithmetic  2.93 us (4%)
  local copies, waits for them, and re-layouts  2.3 us (3%)
  between operations  0.85 us (1%)
    ppermute x10, waiting for transfers between devices, send(): return lax.ppermute(value, ('grp', 'own'), pairs)  20.5 us
    ppermute x10, starting transfers between devices, send(): return lax.ppermute(value, ('grp', 'own'), pairs)  17.4 us
    pallas_call x4, Pallas kernels, call(): pl.pallas_call(kernel, out_shape=outs, in_specs=[pl.BlockSpec(memory_spac...  10 us
    ppermute x1, waiting for transfers between devices, cross(): return lax.ppermute(value, ('grp', 'own'), pairs)  5.01 us
    ppermute x9, starting transfers between devices, swap(): return lax.ppermute(value, 'grp', [(0, 1), (1, 0)])  3.66 us
    ppermute x9, waiting for transfers between devices, swap(): return lax.ppermute(value, 'grp', [(0, 1), (1, 0)])  3.4 us
    unnamed x17, local copies, waits for them, and re-layouts  2.13 us
    select_n x1, other arithmetic, on_chip_pairs(): new_input = jnp.where(own_block, mine[None], rows_far[None])  1.34 us
  transfers between devices with their start and end apart: 20, of which 15 were waited for; matrix products, arithmetic and copies ran while one was open for 2% of the time, Pallas kernels for 5%

profile of v5, /device:TPU:0, one launch (start us, length us, event | category | flops | bytes accessed | tf_op | source)
XLA Modules:
  0.0 66.3 jit_solution(8785262608159709629)
XLA Ops:
  0.6 0.0 copy-start
  0.7 0.8 %copy-done = bf16[256,256]{1,0:T(8,128)(2,1)S(1)} copy-done((bf16[256,256]{1,0:T(8,128)(2,1)S(1)}, bf16[256,256]{1,0:T(8,128)(2,1)}, u32[]{:S(2)}) %copy-start) | copy-done | bytes 131096
  1.5 0.2 fusion.5.refs_2_
  1.8 0.1 pad_add_fusion.refs_0_
  1.8 1.1 %copy-done.1 = bf16[256,1280]{1,0:T(8,128)(2,1)S(1)} copy-done((bf16[256,1280]{1,0:T(8,128)(2,1)S(1)}, bf16[256,1280]{1,0:T(8,128)(2,1)}, u32[]{:S(2)}) %copy-start.1) | copy-done | bytes 655384
  2.9 0.9 %shard_map.103 = f32[16,14,8,128]{3,2,1,0:T(8,128)S(1)} custom-call(s32[3]{0:T(128)S(1)} %pad_add_fusion.refs_0_, bf16[256,1280]{1,0:T(8,128)(2,1)S(1)} %copy-done.1, f32[256,256]{1,0:T(8,128)S(1)} %fusion.5.refs_2_), custom_call_target="tpu_custom_call" | custom-call | flops 209715200 | bytes 1835008 | tf_op jit(solution)/shard_map/pallas_call | solution.py:277
  3.9 0.1 fusion.3
  4.0 0.6 collective-permute-start.1
  4.5 0.1 collective-permute-start
  4.6 0.0 copy-done.2
  4.6 0.9 %shard_map.102 = f32[16,14,8,128]{3,2,1,0:T(8,128)S(1)} custom-call(s32[3]{0:T(128)S(1)} %pad_add_fusion.refs_0_, bf16[256,1280]{1,0:T(8,128)(2,1)S(1)} %copy-done.2, f32[256,256]{1,0:T(8,128)S(1)} %fusion.5.refs_2_), custom_call_target="tpu_custom_call" | custom-call | flops 209715200 | bytes 1835008 | tf_op jit(solution)/shard_map/pallas_call | solution.py:277
  5.5 0.0 copy-start.3
  5.6 0.0 copy-start.4
  5.6 0.4 collective-permute-done.1
  6.0 0.7 collective-permute-done
  6.6 0.1 slice_add_fusion
  6.7 2.9 %collective-permute-start.2 = (f32[8,14,8,128]{3,2,1,0:T(8,128)S(1)}, f32[8,14,8,128]{3,2,1,0:T(8,128)S(1)}, u32[]{:S(2)}, u32[]{:S(2)}) collective-permute-start(f32[8,14,8,128]{3,2,1,0:T(8,128)S(1)} %get-tuple-element.40), channel_id=1, source_target_pairs={{0,1},{1,0},{2,3},{3,2},{4,5},{5,4},{6,7},{7,6},{8,9},{9,8},{10,11... | collective-permute-start | bytes 1376264 | tf_op jit(solution)/shard_map/ppermute | solution.py:312
  9.6 0.0 copy-done.3
  9.6 0.1 dynamic-slice_bitcast_fusion
  9.7 0.1 collective-permute-start.4
  9.8 0.5 collective-permute-start.3
  10.3 0.0 copy-done.4
  10.3 0.1 collective-permute-start.5
  10.4 2.1 %collective-permute-done.5.refs_7_ = f32[320,256]{1,0:T(8,128)S(1)} collective-permute-done((f32[320,256]{1,0:T(8,128)S(1)}, f32[320,256]{1,0:T(8,128)S(1)}, u32[]{:S(2)}, u32[]{:S(2)}) %collective-permute-start.5) | collective-permute-done | bytes 327712 | tf_op jit(solution)/shard_map/ppermute | solution.py:308
  12.6 0.0 collective-permute-done.4.refs_5_
  12.6 0.0 collective-permute-done.3.refs_4_
  12.6 3.5 %collective-permute-done.2 = f32[8,14,8,128]{3,2,1,0:T(8,128)S(1)} collective-permute-done((f32[8,14,8,128]{3,2,1,0:T(8,128)S(1)}, f32[8,14,8,128]{3,2,1,0:T(8,128)S(1)}, u32[]{:S(2)}, u32[]{:S(2)}) %collective-permute-start.2) | collective-permute-done | bytes 458784 | tf_op jit(solution)/shard_map/ppermute | solution.py:312
  16.1 2.1 %collective-permute-start.6 = (f32[4,14,8,128]{3,2,1,0:T(8,128)S(1)}, f32[4,14,8,128]{3,2,1,0:T(8,128)S(1)}, u32[]{:S(2)}, u32[]{:S(2)}) collective-permute-start(f32[4,14,8,128]{3,2,1,0:T(8,128)S(1)} %slice_add_fusion.3), channel_id=1, source_target_pairs={{0,2},{1,3},{2,0},{3,1},{4,6},{5,7},{6,4},{7,5},{8,10},{9,11},{10,... | collective-permute-start | bytes 688136 | tf_op jit(solution)/shard_map/ppermute | solution.py:312
  18.2 4.0 %collective-permute-done.6 = f32[4,14,8,128]{3,2,1,0:T(8,128)S(1)} collective-permute-done((f32[4,14,8,128]{3,2,1,0:T(8,128)S(1)}, f32[4,14,8,128]{3,2,1,0:T(8,128)S(1)}, u32[]{:S(2)}, u32[]{:S(2)}) %collective-permute-start.6) | collective-permute-done | bytes 229408 | tf_op jit(solution)/shard_map/ppermute | solution.py:312
  22.2 0.1 fusion
  22.3 4.2 %collective-permute-start.7 = (f32[1,14,8,128]{3,2,1,0:T(8,128)S(1)}, f32[1,14,8,128]{3,2,1,0:T(8,128)S(1)}, u32[]{:S(2)}, u32[]{:S(2)}) collective-permute-start(f32[1,14,8,128]{3,2,1,0:T(8,128)S(1)} %get-tuple-element.44), channel_id=1, source_target_pairs={{0,12},{1,13},{2,14},{3,15},{4,8},{5,9},{6,10},{7,11},{8,4},{9,5},... | collective-permute-start | bytes 172040 | tf_op jit(solution)/shard_map/ppermute | solution.py:312
  26.5 0.0 collective-permute-start.9
  26.5 0.6 collective-permute-start.8
  27.1 1.6 %collective-permute-done.7 = f32[1,14,8,128]{3,2,1,0:T(8,128)S(1)} collective-permute-done((f32[1,14,8,128]{3,2,1,0:T(8,128)S(1)}, f32[1,14,8,128]{3,2,1,0:T(8,128)S(1)}, u32[]{:S(2)}, u32[]{:S(2)}) %collective-permute-start.7) | collective-permute-done | bytes 57376 | tf_op jit(solution)/shard_map/ppermute | solution.py:312
  28.7 1.9 %collective-permute-done.9 = f32[1,14,8,128]{3,2,1,0:T(8,128)S(1)} collective-permute-done((f32[1,14,8,128]{3,2,1,0:T(8,128)S(1)}, f32[1,14,8,128]{3,2,1,0:T(8,128)S(1)}, u32[]{:S(2)}, u32[]{:S(2)}) %collective-permute-start.9) | collective-permute-done | bytes 57376 | tf_op jit(solution)/shard_map/ppermute | solution.py:312
  30.7 0.9 %collective-permute-done.8 = f32[1,14,8,128]{3,2,1,0:T(8,128)S(1)} collective-permute-done((f32[1,14,8,128]{3,2,1,0:T(8,128)S(1)}, f32[1,14,8,128]{3,2,1,0:T(8,128)S(1)}, u32[]{:S(2)}, u32[]{:S(2)}) %collective-permute-start.8) | collective-permute-done | bytes 57376 | tf_op jit(solution)/shard_map/ppermute | solution.py:312
  31.6 1.6 %collective-permute-start.12 = (f32[1,14,8,128]{3,2,1,0:T(8,128)S(1)}, f32[1,14,8,128]{3,2,1,0:T(8,128)S(1)}, u32[]{:S(2)}, u32[]{:S(2)}) collective-permute-start(f32[1,14,8,128]{3,2,1,0:T(8,128)S(1)} %fusion.2), channel_id=1, source_target_pairs={{0,12},{1,13},{2,14},{3,15},{4,8},{5,9},{6,10},{7,11},{8,4},{9,5},... | collective-permute-start | bytes 172040 | tf_op jit(solution)/shard_map/ppermute | solution.py:312
  33.2 2.0 %collective-permute-start.11 = (f32[1,14,8,128]{3,2,1,0:T(8,128)S(1)}, f32[1,14,8,128]{3,2,1,0:T(8,128)S(1)}, u32[]{:S(2)}, u32[]{:S(2)}) collective-permute-start(f32[1,14,8,128]{3,2,1,0:T(8,128)S(1)} %fusion.2), channel_id=1, source_target_pairs={{0,8},{1,9},{2,10},{3,11},{4,12},{5,13},{6,14},{7,15},{8,0},{9,1},... | collective-permute-start | bytes 172040 | tf_op jit(solution)/shard_map/ppermute | solution.py:312
  35.2 0.9 %collective-permute-start.10 = (f32[1,14,8,128]{3,2,1,0:T(8,128)S(1)}, f32[1,14,8,128]{3,2,1,0:T(8,128)S(1)}, u32[]{:S(2)}, u32[]{:S(2)}) collective-permute-start(f32[1,14,8,128]{3,2,1,0:T(8,128)S(1)} %fusion.2), channel_id=1, source_target_pairs={{0,4},{1,5},{2,6},{3,7},{4,0},{5,1},{6,2},{7,3},{8,12},{9,13},{10,... | collective-permute-start | bytes 172040 | tf_op jit(solution)/shard_map/ppermute | solution.py:312
  36.0 1.7 %collective-permute-done.12 = f32[1,14,8,128]{3,2,1,0:T(8,128)S(1)} collective-permute-done((f32[1,14,8,128]{3,2,1,0:T(8,128)S(1)}, f32[1,14,8,128]{3,2,1,0:T(8,128)S(1)}, u32[]{:S(2)}, u32[]{:S(2)}) %collective-permute-start.12) | collective-permute-done | bytes 57376 | tf_op jit(solution)/shard_map/ppermute | solution.py:312
  37.7 0.0 collective-permute-start.13
  37.7 1.5 %collective-permute-done.11 = f32[1,14,8,128]{3,2,1,0:T(8,128)S(1)} collective-permute-done((f32[1,14,8,128]{3,2,1,0:T(8,128)S(1)}, f32[1,14,8,128]{3,2,1,0:T(8,128)S(1)}, u32[]{:S(2)}, u32[]{:S(2)}) %collective-permute-start.11) | collective-permute-done | bytes 57376 | tf_op jit(solution)/shard_map/ppermute | solution.py:312
  39.2 0.6 collective-permute-done.10
  39.8 0.0 collective-permute-done.13.refs_7_
  39.8 1.6 %collective-permute-start.14 = (f32[4,14,8,128]{3,2,1,0:T(8,128)S(1)}, f32[4,14,8,128]{3,2,1,0:T(8,128)S(1)}, u32[]{:S(2)}, u32[]{:S(2)}) collective-permute-start(f32[4,14,8,128]{3,2,1,0:T(8,128)S(1)} %pad_maximum_fusion), channel_id=1, source_target_pairs={{0,2},{1,3},{2,0},{3,1},{4,6},{5,7},{6,4},{7,5},{8,10},{9,11},{10,... | collective-permute-start | bytes 688136 | tf_op jit(solution)/shard_map/ppermute | solution.py:312
  41.4 4.5 %collective-permute-done.14 = f32[4,14,8,128]{3,2,1,0:T(8,128)S(1)} collective-permute-done((f32[4,14,8,128]{3,2,1,0:T(8,128)S(1)}, f32[4,14,8,128]{3,2,1,0:T(8,128)S(1)}, u32[]{:S(2)}, u32[]{:S(2)}) %collective-permute-start.14) | collective-permute-done | bytes 229408 | tf_op jit(solution)/shard_map/ppermute | solution.py:312
  45.9 1.6 %collective-permute-start.15 = (f32[8,14,8,128]{3,2,1,0:T(8,128)S(1)}, f32[8,14,8,128]{3,2,1,0:T(8,128)S(1)}, u32[]{:S(2)}, u32[]{:S(2)}) collective-permute-start(f32[8,14,8,128]{3,2,1,0:T(8,128)S(1)} %constant_dynamic-update-slice_fusion.refs_1_), channel_id=1, source_target_pairs={{0,1},{1,0},{2,3},{3,2},{4,5},{5,4},{6,7},{7,6},{8,9},{9,8},{10,11... | collective-permute-start | bytes 1376264 | tf_op jit(solution)/shard_map/ppermute | solution.py:312
  47.5 0.1 collective-permute-start.17
  47.5 1.6 %collective-permute-start.16 = (f32[8,2,8,128]{3,2,1,0:T(8,128)S(1)}, f32[8,2,8,128]{3,2,1,0:T(8,128)S(1)}, u32[]{:S(2)}, u32[]{:S(2)}) collective-permute-start(f32[8,2,8,128]{3,2,1,0:T(8,128)S(1)} %slice.83), channel_id=1, source_target_pairs={{0,16},{16,0},{1,17},{17,1},{2,18},{18,2},{3,19},{19,3},{4,20},{20... | collective-permute-start | bytes 196616 | tf_op jit(solution)/shard_map/ppermute | solution.py:308
  49.2 5.0 %collective-permute-done.17.refs_4_ = f32[8,2,8,128]{3,2,1,0:T(8,128)S(1)} collective-permute-done((f32[8,2,8,128]{3,2,1,0:T(8,128)S(1)}, f32[8,2,8,128]{3,2,1,0:T(8,128)S(1)}, u32[]{:S(2)}, u32[]{:S(2)}) %collective-permute-start.17) | collective-permute-done | bytes 65568 | tf_op jit(solution)/shard_map/ppermute | solution.py:316
  54.2 0.0 collective-permute-done.16.refs_3_
  54.2 0.3 collective-permute-done.15.refs_2_
  54.5 5.9 %shard_map.104 = (f32[320,640]{1,0:T(8,128)S(1)}, f32[320,640]{1,0:T(8,128)S(1)}, f32[640,256]{1,0:T(8,128)S(1)}) custom-call(s32[3]{0:T(128)S(1)} %pad_add_fusion.refs_0_, f32[8,14,8,128]{3,2,1,0:T(8,128)S(1)} %constant_dynamic-update-slice_fusion.refs_1_, f32[8,14,8,128]{3,2,1,0:T(8,128)S(1)} %collective-permute-done.15.refs_2_, ...), custom_call_target="tpu_custom_call" | custom-call | flops 4089446400 | bytes 6651904 | tf_op jit(solution)/shard_map/pallas_call | solution.py:277
  60.4 0.6 collective-permute-start.19
  61.0 0.0 copy-done.5
  61.0 2.2 %shard_map.105 = (f32[256,256]{1,0:T(8,128)}, f32[320,256]{1,0:T(8,128)S(1)}, f32[320,256]{1,0:T(8,128)S(1)}) custom-call(s32[3]{0:T(128)S(1)} %pad_add_fusion.refs_0_, f32[8,14,8,128]{3,2,1,0:T(8,128)S(1)} %constant_dynamic-update-slice_fusion.refs_1_, f32[8,14,8,128]{3,2,1,0:T(8,128)S(1)} %collective-permute-done.15.refs_2_, ...), custom_call_target="tpu_custom_call" | custom-call | flops 654311424 | bytes 2887680 | tf_op jit(solution)/shard_map/pallas_call | solution.py:277
  63.2 0.1 collective-permute-start.18
  63.3 0.0 collective-permute-done.19
  63.3 0.0 copy-start.6
  63.3 0.0 copy-start.7
  63.3 1.3 %broadcast_select_fusion = f32[2,320,640]{2,1,0:T(8,128)} fusion(f32[320,640]{1,0:T(8,128)S(1)} %collective-permute-done.19, f32[320,640]{1,0:T(8,128)S(1)} %get-tuple-element.32, pred[2]{0:T(512)(128)(4,1)S(1)} %iota_compare_fusion), kind=kLoop, calls=%fused_computation | loop fusion | flops 409600 | bytes 3276802 | tf_op jit(solution)/shard_map/jit(_where)/select_n | solution.py:366
  64.7 0.2 collective-permute-done.18
  64.9 0.1 copy-done.7
  65.0 1.3 %multiply_subtract_fusion = (f32[2,320,256]{2,1,0:T(8,128)}, f32[2,320,256]{2,1,0:T(8,128)}) fusion(f32[2,320,256]{2,1,0:T(8,128)S(1)} %copy-done.6, f32[320,256]{1,0:T(8,128)S(1)} %collective-permute-done.18, f32[320,256]{1,0:T(8,128)S(1)} %get-tuple-element.30, pred[2]{0:T(512)(128)(4,1)S(1)} %iota_compare_fusion, f32[2,320,256]{2,1,0:T(8,128)S(1)} %copy-done.7), kind=kLoop, calls=%fused_computation.1 | loop fusion | flops 819200 | bytes 3276802 | tf_op jit(solution)/shard_map/sub | solution.py:369
  (14 shorter events, 0.2 us)
Async XLA Ops:
  0.6 0.9 %copy-start = (bf16[256,256]{1,0:T(8,128)(2,1)S(1)}, bf16[256,256]{1,0:T(8,128)(2,1)}, u32[]{:S(2)}) copy-start(bf16[256,256]{1,0:T(8,128)(2,1)} %param.8) | copy-start | bytes 393220
  1.8 1.1 %copy-start.1 = (bf16[256,1280]{1,0:T(8,128)(2,1)S(1)}, bf16[256,1280]{1,0:T(8,128)(2,1)}, u32[]{:S(2)}) copy-start(bf16[256,1280]{1,0:T(8,128)(2,1)} %refs_1_.3) | copy-start | bytes 1966084
  2.9 1.7 %copy-start.2 = (bf16[256,1280]{1,0:T(8,128)(2,1)S(1)}, bf16[256,1280]{1,0:T(8,128)(2,1)}, u32[]{:S(2)}) copy-start(bf16[256,1280]{1,0:T(8,128)(2,1)} %refs_1_.3) | copy-start | bytes 1966084
  4.0 2.0 %collective-permute-start.1 = (f32[8,14,8,128]{3,2,1,0:T(8,128)S(1)}, f32[8,14,8,128]{3,2,1,0:T(8,128)S(1)}, u32[]{:S(2)}, u32[]{:S(2)}) collective-permute-start(f32[8,14,8,128]{3,2,1,0:T(8,128)S(1)} %get-tuple-element.42), channel_id=1, source_target_pairs={{0,16},{16,0},{1,17},{17,1},{2,18},{18,2},{3,19},{19,3},{4,20},{20... | collective-permute-start | bytes 1376264 | tf_op jit(solution)/shard_map/ppermute | solution.py:308
  4.5 2.1 %collective-permute-start = (f32[8,14,8,128]{3,2,1,0:T(8,128)S(1)}, f32[8,14,8,128]{3,2,1,0:T(8,128)S(1)}, u32[]{:S(2)}, u32[]{:S(2)}) collective-permute-start(f32[8,14,8,128]{3,2,1,0:T(8,128)S(1)} %get-tuple-element.43), channel_id=1, source_target_pairs={{0,16},{16,0},{1,17},{17,1},{2,18},{18,2},{3,19},{19,3},{4,20},{20... | collective-permute-start | bytes 1376264 | tf_op jit(solution)/shard_map/ppermute | solution.py:308
  5.5 4.1 %copy-start.3 = (f32[2,320,640]{2,1,0:T(8,128)S(1)}, f32[2,320,640]{2,1,0:T(8,128)}, u32[]{:S(2)}) copy-start(f32[2,320,640]{2,1,0:T(8,128)} %refs_3_.1) | copy-start | bytes 4915204
  5.6 4.7 %copy-start.4 = (f32[2,320,256]{2,1,0:T(8,128)S(1)}, f32[2,320,256]{2,1,0:T(8,128)}, u32[]{:S(2)}) copy-start(f32[2,320,256]{2,1,0:T(8,128)} %refs_6_.1) | copy-start | bytes 1966084
  6.7 9.4 %collective-permute-start.2 = (f32[8,14,8,128]{3,2,1,0:T(8,128)S(1)}, f32[8,14,8,128]{3,2,1,0:T(8,128)S(1)}, u32[]{:S(2)}, u32[]{:S(2)}) collective-permute-start(f32[8,14,8,128]{3,2,1,0:T(8,128)S(1)} %get-tuple-element.40), channel_id=1, source_target_pairs={{0,1},{1,0},{2,3},{3,2},{4,5},{5,4},{6,7},{7,6},{8,9},{9,8},{10,11... | collective-permute-start | bytes 1376264 | tf_op jit(solution)/shard_map/ppermute | solution.py:312
  9.7 2.9 %collective-permute-start.4 = (f32[160,640]{1,0:T(8,128)S(1)}, f32[160,640]{1,0:T(8,128)S(1)}, u32[]{:S(2)}, u32[]{:S(2)}) collective-permute-start(f32[160,640]{1,0:T(8,128)S(1)} %get-tuple-element.38), channel_id=1, source_target_pairs={{0,16},{16,0},{1,17},{17,1},{2,18},{18,2},{3,19},{19,3},{4,20},{20... | collective-permute-start | bytes 1228808 | tf_op jit(solution)/shard_map/ppermute | solution.py:308
  9.8 2.8 %collective-permute-start.3 = (f32[160,640]{1,0:T(8,128)S(1)}, f32[160,640]{1,0:T(8,128)S(1)}, u32[]{:S(2)}, u32[]{:S(2)}) collective-permute-start(f32[160,640]{1,0:T(8,128)S(1)} %get-tuple-element.39), channel_id=1, source_target_pairs={{0,16},{16,0},{1,17},{17,1},{2,18},{18,2},{3,19},{19,3},{4,20},{20... | collective-permute-start | bytes 1228808 | tf_op jit(solution)/shard_map/ppermute | solution.py:308
  10.3 2.3 %collective-permute-start.5 = (f32[320,256]{1,0:T(8,128)S(1)}, f32[320,256]{1,0:T(8,128)S(1)}, u32[]{:S(2)}, u32[]{:S(2)}) collective-permute-start(f32[320,256]{1,0:T(8,128)S(1)} %dynamic-slice_bitcast_fusion.2), channel_id=1, source_target_pairs={{0,16},{16,0},{1,17},{17,1},{2,18},{18,2},{3,19},{19,3},{4,20},{20... | collective-permute-start | bytes 983048 | tf_op jit(solution)/shard_map/ppermute | solution.py:308
  16.1 6.1 %collective-permute-start.6 = (f32[4,14,8,128]{3,2,1,0:T(8,128)S(1)}, f32[4,14,8,128]{3,2,1,0:T(8,128)S(1)}, u32[]{:S(2)}, u32[]{:S(2)}) collective-permute-start(f32[4,14,8,128]{3,2,1,0:T(8,128)S(1)} %slice_add_fusion.3), channel_id=1, source_target_pairs={{0,2},{1,3},{2,0},{3,1},{4,6},{5,7},{6,4},{7,5},{8,10},{9,11},{10,... | collective-permute-start | bytes 688136 | tf_op jit(solution)/shard_map/ppermute | solution.py:312
  22.3 6.4 %collective-permute-start.7 = (f32[1,14,8,128]{3,2,1,0:T(8,128)S(1)}, f32[1,14,8,128]{3,2,1,0:T(8,128)S(1)}, u32[]{:S(2)}, u32[]{:S(2)}) collective-permute-start(f32[1,14,8,128]{3,2,1,0:T(8,128)S(1)} %get-tuple-element.44), channel_id=1, source_target_pairs={{0,12},{1,13},{2,14},{3,15},{4,8},{5,9},{6,10},{7,11},{8,4},{9,5},... | collective-permute-start | bytes 172040 | tf_op jit(solution)/shard_map/ppermute | solution.py:312
  26.5 4.2 %collective-permute-start.9 = (f32[1,14,8,128]{3,2,1,0:T(8,128)S(1)}, f32[1,14,8,128]{3,2,1,0:T(8,128)S(1)}, u32[]{:S(2)}, u32[]{:S(2)}) collective-permute-start(f32[1,14,8,128]{3,2,1,0:T(8,128)S(1)} %get-tuple-element.45), channel_id=1, source_target_pairs={{0,4},{1,5},{2,6},{3,7},{4,0},{5,1},{6,2},{7,3},{8,12},{9,13},{10,... | collective-permute-start | bytes 172040 | tf_op jit(solution)/shard_map/ppermute | solution.py:312
  26.5 5.1 %collective-permute-start.8 = (f32[1,14,8,128]{3,2,1,0:T(8,128)S(1)}, f32[1,14,8,128]{3,2,1,0:T(8,128)S(1)}, u32[]{:S(2)}, u32[]{:S(2)}) collective-permute-start(f32[1,14,8,128]{3,2,1,0:T(8,128)S(1)} %get-tuple-element.46), channel_id=1, source_target_pairs={{0,8},{1,9},{2,10},{3,11},{4,12},{5,13},{6,14},{7,15},{8,0},{9,1},... | collective-permute-start | bytes 172040 | tf_op jit(solution)/shard_map/ppermute | solution.py:312
  31.6 6.1 %collective-permute-start.12 = (f32[1,14,8,128]{3,2,1,0:T(8,128)S(1)}, f32[1,14,8,128]{3,2,1,0:T(8,128)S(1)}, u32[]{:S(2)}, u32[]{:S(2)}) collective-permute-start(f32[1,14,8,128]{3,2,1,0:T(8,128)S(1)} %fusion.2), channel_id=1, source_target_pairs={{0,12},{1,13},{2,14},{3,15},{4,8},{5,9},{6,10},{7,11},{8,4},{9,5},... | collective-permute-start | bytes 172040 | tf_op jit(solution)/shard_map/ppermute | solution.py:312
  33.2 6.1 %collective-permute-start.11 = (f32[1,14,8,128]{3,2,1,0:T(8,128)S(1)}, f32[1,14,8,128]{3,2,1,0:T(8,128)S(1)}, u32[]{:S(2)}, u32[]{:S(2)}) collective-permute-start(f32[1,14,8,128]{3,2,1,0:T(8,128)S(1)} %fusion.2), channel_id=1, source_target_pairs={{0,8},{1,9},{2,10},{3,11},{4,12},{5,13},{6,14},{7,15},{8,0},{9,1},... | collective-permute-start | bytes 172040 | tf_op jit(solution)/shard_map/ppermute | solution.py:312
  35.2 4.6 %collective-permute-start.10 = (f32[1,14,8,128]{3,2,1,0:T(8,128)S(1)}, f32[1,14,8,128]{3,2,1,0:T(8,128)S(1)}, u32[]{:S(2)}, u32[]{:S(2)}) collective-permute-start(f32[1,14,8,128]{3,2,1,0:T(8,128)S(1)} %fusion.2), channel_id=1, source_target_pairs={{0,4},{1,5},{2,6},{3,7},{4,0},{5,1},{6,2},{7,3},{8,12},{9,13},{10,... | collective-permute-start | bytes 172040 | tf_op jit(solution)/shard_map/ppermute | solution.py:312
  37.7 2.1 %collective-permute-start.13 = (f32[1,1,8,128]{3,2,1,0:T(8,128)S(1)}, f32[1,1,8,128]{3,2,1,0:T(8,128)S(1)}, u32[]{:S(2)}, u32[]{:S(2)}) collective-permute-start(f32[1,1,8,128]{3,2,1,0:T(8,128)S(1)} %slice.82), channel_id=1, source_target_pairs={{0,16},{16,0},{1,17},{17,1},{2,18},{18,2},{3,19},{19,3},{4,20},{20... | collective-permute-start | bytes 12296 | tf_op jit(solution)/shard_map/ppermute | solution.py:308
  39.8 6.1 %collective-permute-start.14 = (f32[4,14,8,128]{3,2,1,0:T(8,128)S(1)}, f32[4,14,8,128]{3,2,1,0:T(8,128)S(1)}, u32[]{:S(2)}, u32[]{:S(2)}) collective-permute-start(f32[4,14,8,128]{3,2,1,0:T(8,128)S(1)} %pad_maximum_fusion), channel_id=1, source_target_pairs={{0,2},{1,3},{2,0},{3,1},{4,6},{5,7},{6,4},{7,5},{8,10},{9,11},{10,... | collective-permute-start | bytes 688136 | tf_op jit(solution)/shard_map/ppermute | solution.py:312
  45.9 8.5 %collective-permute-start.15 = (f32[8,14,8,128]{3,2,1,0:T(8,128)S(1)}, f32[8,14,8,128]{3,2,1,0:T(8,128)S(1)}, u32[]{:S(2)}, u32[]{:S(2)}) collective-permute-start(f32[8,14,8,128]{3,2,1,0:T(8,128)S(1)} %constant_dynamic-update-slice_fusion.refs_1_), channel_id=1, source_target_pairs={{0,1},{1,0},{2,3},{3,2},{4,5},{5,4},{6,7},{7,6},{8,9},{9,8},{10,11... | collective-permute-start | bytes 1376264 | tf_op jit(solution)/shard_map/ppermute | solution.py:312
  47.5 13.5 %copy-start.5 = (f32[256,256]{1,0:T(8,128)S(1)}, f32[256,256]{1,0:T(8,128)}, u32[]{:S(2)}) copy-start(f32[256,256]{1,0:T(8,128)} %refs_5_.1) | copy-start | bytes 786436
  47.5 6.7 %collective-permute-start.17 = (f32[8,2,8,128]{3,2,1,0:T(8,128)S(1)}, f32[8,2,8,128]{3,2,1,0:T(8,128)S(1)}, u32[]{:S(2)}, u32[]{:S(2)}) collective-permute-start(f32[8,2,8,128]{3,2,1,0:T(8,128)S(1)} %slice.83), channel_id=1, source_target_pairs={{0,17},{1,16},{2,19},{3,18},{4,21},{5,20},{6,23},{7,22},{8,25},{9,... | collective-permute-start | bytes 196616 | tf_op jit(solution)/shard_map/ppermute | solution.py:316
  47.5 6.6 %collective-permute-start.16 = (f32[8,2,8,128]{3,2,1,0:T(8,128)S(1)}, f32[8,2,8,128]{3,2,1,0:T(8,128)S(1)}, u32[]{:S(2)}, u32[]{:S(2)}) collective-permute-start(f32[8,2,8,128]{3,2,1,0:T(8,128)S(1)} %slice.83), channel_id=1, source_target_pairs={{0,16},{16,0},{1,17},{17,1},{2,18},{18,2},{3,19},{19,3},{4,20},{20... | collective-permute-start | bytes 196616 | tf_op jit(solution)/shard_map/ppermute | solution.py:308
  60.4 2.9 %collective-permute-start.19 = (f32[320,640]{1,0:T(8,128)S(1)}, f32[320,640]{1,0:T(8,128)S(1)}, u32[]{:S(2)}, u32[]{:S(2)}) collective-permute-start(f32[320,640]{1,0:T(8,128)S(1)} %get-tuple-element.33), channel_id=1, source_target_pairs={{0,16},{16,0},{1,17},{17,1},{2,18},{18,2},{3,19},{19,3},{4,20},{20... | collective-permute-start | bytes 2457608 | tf_op jit(solution)/shard_map/ppermute | solution.py:308
  63.2 1.7 %collective-permute-start.18 = (f32[320,256]{1,0:T(8,128)S(1)}, f32[320,256]{1,0:T(8,128)S(1)}, u32[]{:S(2)}, u32[]{:S(2)}) collective-permute-start(f32[320,256]{1,0:T(8,128)S(1)} %get-tuple-element.31), channel_id=1, source_target_pairs={{0,16},{16,0},{1,17},{17,1},{2,18},{18,2},{3,19},{19,3},{4,20},{20... | collective-permute-start | bytes 983048 | tf_op jit(solution)/shard_map/ppermute | solution.py:308
  63.3 1.6 %copy-start.6 = (f32[2,320,256]{2,1,0:T(8,128)S(1)}, f32[2,320,256]{2,1,0:T(8,128)}, u32[]{:S(2)}) copy-start(f32[2,320,256]{2,1,0:T(8,128)} %param.12) | copy-start | bytes 1966084
  63.3 1.7 %copy-start.7 = (f32[2,320,256]{2,1,0:T(8,128)S(1)}, f32[2,320,256]{2,1,0:T(8,128)}, u32[]{:S(2)}) copy-start(f32[2,320,256]{2,1,0:T(8,128)} %param.13) | copy-start | bytes 1966084

commit v6 on v5

--- a/solution.py
+++ b/solution.py
@@ -322,8 +322,9 @@
     arrived = swap(theirs[8:]), swap(theirs[:8])
     (held,) = call(lambda *refs: stats_kernel(*refs, far=False), where, samples_in, packed, (), work)
     going = held[8:] + arrived[0]
-    kept = held[:8] + arrived[1]
+    low, going = fence((held[:8], going))
     came = send(going, (1, 2))
+    kept = low + arrived[1]
     fac_rows = lax.dynamic_index_in_dim(input_factor, 1 - group, 0, False)
     grad_rows = lax.dynamic_index_in_dim(gradient, 1 - group, 0, False)
     fac_far = swap(fac_rows[: slab // 2]), swap(fac_rows[slab // 2 :])

time: 66.5 us -> 65.9 us (level)
  waiting for transfers between devices: 28.9 us -> 28.2 us
    ppermute x9, waiting for transfers between devices: 3.4 us -> 2.7 us  [swap(): return lax.ppermute(value, 'grp', [(0, 1), (1, 0)])]
  transfers between devices with their start and end apart: 20 -> 20, of which waited for: 15 -> 14; matrix products, arithmetic and copies ran while one was open for 2% -> 2% of each run, Pallas kernels for 5% -> 5%
where the time goes in v6:
time: 65.9 us; the launch traced here: 65.6 us
  waiting for transfers between devices  28.2 us (43%)
  starting transfers between devices  21.1 us (32%)
  Pallas kernels  10 us (15%)
  other arithmetic  2.96 us (4%)
  local copies, waits for them, and re-layouts  2.3 us (3%)
  between operations  0.85 us (1%)
    ppermute x10, waiting for transfers between devices, send(): return lax.ppermute(value, ('grp', 'own'), pairs)  20.5 us
    ppermute x10, starting transfers between devices, send(): return lax.ppermute(value, ('grp', 'own'), pairs)  17.4 us
    pallas_call x4, Pallas kernels, call(): pl.pallas_call(kernel, out_shape=outs, in_specs=[pl.BlockSpec(memory_spac...  10 us
    ppermute x1, waiting for transfers between devices, cross(): return lax.ppermute(value, ('grp', 'own'), pairs)  5.01 us
    ppermute x9, starting transfers between devices, swap(): return lax.ppermute(value, 'grp', [(0, 1), (1, 0)])  3.66 us
    ppermute x9, waiting for transfers between devices, swap(): return lax.ppermute(value, 'grp', [(0, 1), (1, 0)])  2.7 us
    unnamed x17, local copies, waits for them, and re-layouts  2.13 us
    select_n x1, other arithmetic, on_chip_pairs(): new_input = jnp.where(own_block, mine[None], rows_far[None])  1.34 us
  transfers between devices with their start and end apart: 20, of which 14 were waited for; matrix products, arithmetic and copies ran while one was open for 2% of the time, Pallas kernels for 5%

profile of v6, /device:TPU:0, one launch (start us, length us, event | category | flops | bytes accessed | tf_op | source)
XLA Modules:
  0.0 65.6 jit_solution(15748234392061765299)
XLA Ops:
  0.6 0.0 copy-start
  0.7 0.8 %copy-done = bf16[256,256]{1,0:T(8,128)(2,1)S(1)} copy-done((bf16[256,256]{1,0:T(8,128)(2,1)S(1)}, bf16[256,256]{1,0:T(8,128)(2,1)}, u32[]{:S(2)}) %copy-start) | copy-done | bytes 131096
  1.5 0.2 fusion.5.refs_2_
  1.8 0.1 pad_add_fusion.refs_0_
  1.8 1.1 %copy-done.1 = bf16[256,1280]{1,0:T(8,128)(2,1)S(1)} copy-done((bf16[256,1280]{1,0:T(8,128)(2,1)S(1)}, bf16[256,1280]{1,0:T(8,128)(2,1)}, u32[]{:S(2)}) %copy-start.1) | copy-done | bytes 655384
  2.9 0.9 %shard_map.103 = f32[16,14,8,128]{3,2,1,0:T(8,128)S(1)} custom-call(s32[3]{0:T(128)S(1)} %pad_add_fusion.refs_0_, bf16[256,1280]{1,0:T(8,128)(2,1)S(1)} %copy-done.1, f32[256,256]{1,0:T(8,128)S(1)} %fusion.5.refs_2_), custom_call_target="tpu_custom_call" | custom-call | flops 209715200 | bytes 1835008 | tf_op jit(solution)/shard_map/pallas_call | solution.py:277
  3.9 0.1 fusion.3
  4.0 0.6 collective-permute-start
  4.5 0.1 collective-permute-start.1
  4.6 0.0 copy-done.2
  4.6 0.9 %shard_map.102 = f32[16,14,8,128]{3,2,1,0:T(8,128)S(1)} custom-call(s32[3]{0:T(128)S(1)} %pad_add_fusion.refs_0_, bf16[256,1280]{1,0:T(8,128)(2,1)S(1)} %copy-done.2, f32[256,256]{1,0:T(8,128)S(1)} %fusion.5.refs_2_), custom_call_target="tpu_custom_call" | custom-call | flops 209715200 | bytes 1835008 | tf_op jit(solution)/shard_map/pallas_call | solution.py:277
  5.5 0.0 copy-start.4
  5.6 0.4 collective-permute-done
  6.0 0.1 slice_add_fusion
  6.0 2.9 %collective-permute-start.2 = (f32[8,14,8,128]{3,2,1,0:T(8,128)S(1)}, f32[8,14,8,128]{3,2,1,0:T(8,128)S(1)}, u32[]{:S(2)}, u32[]{:S(2)}) collective-permute-start(f32[8,14,8,128]{3,2,1,0:T(8,128)S(1)} %get-tuple-element.23), channel_id=1, source_target_pairs={{0,1},{1,0},{2,3},{3,2},{4,5},{5,4},{6,7},{7,6},{8,9},{9,8},{10,11... | collective-permute-start | bytes 1376264 | tf_op jit(solution)/shard_map/ppermute | solution.py:312
  9.0 0.0 copy-done.3
  9.0 0.1 dynamic-slice_bitcast_fusion
  9.0 0.1 collective-permute-start.4
  9.1 0.5 collective-permute-start.3
  9.6 0.0 copy-done.4
  9.6 0.1 collective-permute-start.5
  9.8 0.0 collective-permute-done.1
  9.8 2.1 %collective-permute-done.5.refs_7_ = f32[320,256]{1,0:T(8,128)S(1)} collective-permute-done((f32[320,256]{1,0:T(8,128)S(1)}, f32[320,256]{1,0:T(8,128)S(1)}, u32[]{:S(2)}, u32[]{:S(2)}) %collective-permute-start.5) | collective-permute-done | bytes 327712 | tf_op jit(solution)/shard_map/ppermute | solution.py:308
  11.9 0.0 collective-permute-done.4.refs_5_
  11.9 0.0 collective-permute-done.3.refs_4_
  11.9 3.5 %collective-permute-done.2 = f32[8,14,8,128]{3,2,1,0:T(8,128)S(1)} collective-permute-done((f32[8,14,8,128]{3,2,1,0:T(8,128)S(1)}, f32[8,14,8,128]{3,2,1,0:T(8,128)S(1)}, u32[]{:S(2)}, u32[]{:S(2)}) %collective-permute-start.2) | collective-permute-done | bytes 458784 | tf_op jit(solution)/shard_map/ppermute | solution.py:312
  15.4 2.1 %collective-permute-start.6 = (f32[4,14,8,128]{3,2,1,0:T(8,128)S(1)}, f32[4,14,8,128]{3,2,1,0:T(8,128)S(1)}, u32[]{:S(2)}, u32[]{:S(2)}) collective-permute-start(f32[4,14,8,128]{3,2,1,0:T(8,128)S(1)} %slice_add_fusion.2), channel_id=1, source_target_pairs={{0,2},{1,3},{2,0},{3,1},{4,6},{5,7},{6,4},{7,5},{8,10},{9,11},{10,... | collective-permute-start | bytes 688136 | tf_op jit(solution)/shard_map/ppermute | solution.py:312
  17.6 4.0 %collective-permute-done.6 = f32[4,14,8,128]{3,2,1,0:T(8,128)S(1)} collective-permute-done((f32[4,14,8,128]{3,2,1,0:T(8,128)S(1)}, f32[4,14,8,128]{3,2,1,0:T(8,128)S(1)}, u32[]{:S(2)}, u32[]{:S(2)}) %collective-permute-start.6) | collective-permute-done | bytes 229408 | tf_op jit(solution)/shard_map/ppermute | solution.py:312
  21.6 0.1 fusion
  21.6 4.2 %collective-permute-start.7 = (f32[1,14,8,128]{3,2,1,0:T(8,128)S(1)}, f32[1,14,8,128]{3,2,1,0:T(8,128)S(1)}, u32[]{:S(2)}, u32[]{:S(2)}) collective-permute-start(f32[1,14,8,128]{3,2,1,0:T(8,128)S(1)} %get-tuple-element.48), channel_id=1, source_target_pairs={{0,12},{1,13},{2,14},{3,15},{4,8},{5,9},{6,10},{7,11},{8,4},{9,5},... | collective-permute-start | bytes 172040 | tf_op jit(solution)/shard_map/ppermute | solution.py:312
  25.8 0.0 collective-permute-start.9
  25.8 0.6 collective-permute-start.8
  26.4 1.6 %collective-permute-done.7 = f32[1,14,8,128]{3,2,1,0:T(8,128)S(1)} collective-permute-done((f32[1,14,8,128]{3,2,1,0:T(8,128)S(1)}, f32[1,14,8,128]{3,2,1,0:T(8,128)S(1)}, u32[]{:S(2)}, u32[]{:S(2)}) %collective-permute-start.7) | collective-permute-done | bytes 57376 | tf_op jit(solution)/shard_map/ppermute | solution.py:312
  28.1 1.9 %collective-permute-done.9 = f32[1,14,8,128]{3,2,1,0:T(8,128)S(1)} collective-permute-done((f32[1,14,8,128]{3,2,1,0:T(8,128)S(1)}, f32[1,14,8,128]{3,2,1,0:T(8,128)S(1)}, u32[]{:S(2)}, u32[]{:S(2)}) %collective-permute-start.9) | collective-permute-done | bytes 57376 | tf_op jit(solution)/shard_map/ppermute | solution.py:312
  30.0 0.9 %collective-permute-done.8 = f32[1,14,8,128]{3,2,1,0:T(8,128)S(1)} collective-permute-done((f32[1,14,8,128]{3,2,1,0:T(8,128)S(1)}, f32[1,14,8,128]{3,2,1,0:T(8,128)S(1)}, u32[]{:S(2)}, u32[]{:S(2)}) %collective-permute-start.8) | collective-permute-done | bytes 57376 | tf_op jit(solution)/shard_map/ppermute | solution.py:312
  30.9 1.6 %collective-permute-start.12 = (f32[1,14,8,128]{3,2,1,0:T(8,128)S(1)}, f32[1,14,8,128]{3,2,1,0:T(8,128)S(1)}, u32[]{:S(2)}, u32[]{:S(2)}) collective-permute-start(f32[1,14,8,128]{3,2,1,0:T(8,128)S(1)} %fusion.2), channel_id=1, source_target_pairs={{0,12},{1,13},{2,14},{3,15},{4,8},{5,9},{6,10},{7,11},{8,4},{9,5},... | collective-permute-start | bytes 172040 | tf_op jit(solution)/shard_map/ppermute | solution.py:312
  32.5 2.0 %collective-permute-start.11 = (f32[1,14,8,128]{3,2,1,0:T(8,128)S(1)}, f32[1,14,8,128]{3,2,1,0:T(8,128)S(1)}, u32[]{:S(2)}, u32[]{:S(2)}) collective-permute-start(f32[1,14,8,128]{3,2,1,0:T(8,128)S(1)} %fusion.2), channel_id=1, source_target_pairs={{0,8},{1,9},{2,10},{3,11},{4,12},{5,13},{6,14},{7,15},{8,0},{9,1},... | collective-permute-start | bytes 172040 | tf_op jit(solution)/shard_map/ppermute | solution.py:312
  34.5 0.9 %collective-permute-start.10 = (f32[1,14,8,128]{3,2,1,0:T(8,128)S(1)}, f32[1,14,8,128]{3,2,1,0:T(8,128)S(1)}, u32[]{:S(2)}, u32[]{:S(2)}) collective-permute-start(f32[1,14,8,128]{3,2,1,0:T(8,128)S(1)} %fusion.2), channel_id=1, source_target_pairs={{0,4},{1,5},{2,6},{3,7},{4,0},{5,1},{6,2},{7,3},{8,12},{9,13},{10,... | collective-permute-start | bytes 172040 | tf_op jit(solution)/shard_map/ppermute | solution.py:312
  35.4 1.7 %collective-permute-done.12 = f32[1,14,8,128]{3,2,1,0:T(8,128)S(1)} collective-permute-done((f32[1,14,8,128]{3,2,1,0:T(8,128)S(1)}, f32[1,14,8,128]{3,2,1,0:T(8,128)S(1)}, u32[]{:S(2)}, u32[]{:S(2)}) %collective-permute-start.12) | collective-permute-done | bytes 57376 | tf_op jit(solution)/shard_map/ppermute | solution.py:312
  37.0 0.0 collective-permute-start.13
  37.0 1.5 %collective-permute-done.11 = f32[1,14,8,128]{3,2,1,0:T(8,128)S(1)} collective-permute-done((f32[1,14,8,128]{3,2,1,0:T(8,128)S(1)}, f32[1,14,8,128]{3,2,1,0:T(8,128)S(1)}, u32[]{:S(2)}, u32[]{:S(2)}) %collective-permute-start.11) | collective-permute-done | bytes 57376 | tf_op jit(solution)/shard_map/ppermute | solution.py:312
  38.5 0.6 collective-permute-done.10
  39.1 0.0 collective-permute-done.13.refs_7_
  39.1 1.6 %collective-permute-start.14 = (f32[4,14,8,128]{3,2,1,0:T(8,128)S(1)}, f32[4,14,8,128]{3,2,1,0:T(8,128)S(1)}, u32[]{:S(2)}, u32[]{:S(2)}) collective-permute-start(f32[4,14,8,128]{3,2,1,0:T(8,128)S(1)} %pad_maximum_fusion), channel_id=1, source_target_pairs={{0,2},{1,3},{2,0},{3,1},{4,6},{5,7},{6,4},{7,5},{8,10},{9,11},{10,... | collective-permute-start | bytes 688136 | tf_op jit(solution)/shard_map/ppermute | solution.py:312
  40.7 4.5 %collective-permute-done.14 = f32[4,14,8,128]{3,2,1,0:T(8,128)S(1)} collective-permute-done((f32[4,14,8,128]{3,2,1,0:T(8,128)S(1)}, f32[4,14,8,128]{3,2,1,0:T(8,128)S(1)}, u32[]{:S(2)}, u32[]{:S(2)}) %collective-permute-start.14) | collective-permute-done | bytes 229408 | tf_op jit(solution)/shard_map/ppermute | solution.py:312
  45.2 1.6 %collective-permute-start.15 = (f32[8,14,8,128]{3,2,1,0:T(8,128)S(1)}, f32[8,14,8,128]{3,2,1,0:T(8,128)S(1)}, u32[]{:S(2)}, u32[]{:S(2)}) collective-permute-start(f32[8,14,8,128]{3,2,1,0:T(8,128)S(1)} %constant_dynamic-update-slice_fusion.refs_1_), channel_id=1, source_target_pairs={{0,1},{1,0},{2,3},{3,2},{4,5},{5,4},{6,7},{7,6},{8,9},{9,8},{10,11... | collective-permute-start | bytes 1376264 | tf_op jit(solution)/shard_map/ppermute | solution.py:312
  46.8 0.1 collective-permute-start.17
  46.9 1.6 %collective-permute-start.16 = (f32[8,2,8,128]{3,2,1,0:T(8,128)S(1)}, f32[8,2,8,128]{3,2,1,0:T(8,128)S(1)}, u32[]{:S(2)}, u32[]{:S(2)}) collective-permute-start(f32[8,2,8,128]{3,2,1,0:T(8,128)S(1)} %slice.83), channel_id=1, source_target_pairs={{0,16},{16,0},{1,17},{17,1},{2,18},{18,2},{3,19},{19,3},{4,20},{20... | collective-permute-start | bytes 196616 | tf_op jit(solution)/shard_map/ppermute | solution.py:308
  48.5 5.0 %collective-permute-done.17.refs_4_ = f32[8,2,8,128]{3,2,1,0:T(8,128)S(1)} collective-permute-done((f32[8,2,8,128]{3,2,1,0:T(8,128)S(1)}, f32[8,2,8,128]{3,2,1,0:T(8,128)S(1)}, u32[]{:S(2)}, u32[]{:S(2)}) %collective-permute-start.17) | collective-permute-done | bytes 65568 | tf_op jit(solution)/shard_map/ppermute | solution.py:316
  53.5 0.0 collective-permute-done.16.refs_3_
  53.5 0.3 collective-permute-done.15.refs_2_
  53.8 5.9 %shard_map.104 = (f32[320,640]{1,0:T(8,128)S(1)}, f32[320,640]{1,0:T(8,128)S(1)}, f32[640,256]{1,0:T(8,128)S(1)}) custom-call(s32[3]{0:T(128)S(1)} %pad_add_fusion.refs_0_, f32[8,14,8,128]{3,2,1,0:T(8,128)S(1)} %constant_dynamic-update-slice_fusion.refs_1_, f32[8,14,8,128]{3,2,1,0:T(8,128)S(1)} %collective-permute-done.15.refs_2_, ...), custom_call_target="tpu_custom_call" | custom-call | flops 4089446400 | bytes 6651904 | tf_op jit(solution)/shard_map/pallas_call | solution.py:277
  59.7 0.6 collective-permute-start.19
  60.3 0.0 copy-done.5
  60.3 2.2 %shard_map.105 = (f32[256,256]{1,0:T(8,128)}, f32[320,256]{1,0:T(8,128)S(1)}, f32[320,256]{1,0:T(8,128)S(1)}) custom-call(s32[3]{0:T(128)S(1)} %pad_add_fusion.refs_0_, f32[8,14,8,128]{3,2,1,0:T(8,128)S(1)} %constant_dynamic-update-slice_fusion.refs_1_, f32[8,14,8,128]{3,2,1,0:T(8,128)S(1)} %collective-permute-done.15.refs_2_, ...), custom_call_target="tpu_custom_call" | custom-call | flops 654311424 | bytes 2887680 | tf_op jit(solution)/shard_map/pallas_call | solution.py:277
  62.5 0.1 collective-permute-start.18
  62.6 0.0 collective-permute-done.19
  62.6 0.0 copy-start.6
  62.6 0.0 copy-start.7
  62.6 1.3 %broadcast_select_fusion = f32[2,320,640]{2,1,0:T(8,128)} fusion(f32[320,640]{1,0:T(8,128)S(1)} %collective-permute-done.19, f32[320,640]{1,0:T(8,128)S(1)} %get-tuple-element.36, pred[2]{0:T(512)(128)(4,1)S(1)} %iota_compare_fusion), kind=kLoop, calls=%fused_computation | loop fusion | flops 409600 | bytes 3276802 | tf_op jit(solution)/shard_map/jit(_where)/select_n | solution.py:367
  64.0 0.2 collective-permute-done.18
  64.2 0.0 copy-done.6
  64.2 0.1 copy-done.7
  64.4 1.3 %multiply_subtract_fusion = (f32[2,320,256]{2,1,0:T(8,128)}, f32[2,320,256]{2,1,0:T(8,128)}) fusion(f32[2,320,256]{2,1,0:T(8,128)S(1)} %copy-done.6, f32[320,256]{1,0:T(8,128)S(1)} %collective-permute-done.18, f32[320,256]{1,0:T(8,128)S(1)} %get-tuple-element.34, pred[2]{0:T(512)(128)(4,1)S(1)} %iota_compare_fusion, f32[2,320,256]{2,1,0:T(8,128)S(1)} %copy-done.7), kind=kLoop, calls=%fused_computation.1 | loop fusion | flops 819200 | bytes 3276802 | tf_op jit(solution)/shard_map/sub | solution.py:370
  (15 shorter events, 0.2 us)
Async XLA Ops:
  0.6 0.9 %copy-start = (bf16[256,256]{1,0:T(8,128)(2,1)S(1)}, bf16[256,256]{1,0:T(8,128)(2,1)}, u32[]{:S(2)}) copy-start(bf16[256,256]{1,0:T(8,128)(2,1)} %param.8) | copy-start | bytes 393220
  1.8 1.1 %copy-start.1 = (bf16[256,1280]{1,0:T(8,128)(2,1)S(1)}, bf16[256,1280]{1,0:T(8,128)(2,1)}, u32[]{:S(2)}) copy-start(bf16[256,1280]{1,0:T(8,128)(2,1)} %refs_1_.3) | copy-start | bytes 1966084
  2.9 1.7 %copy-start.2 = (bf16[256,1280]{1,0:T(8,128)(2,1)S(1)}, bf16[256,1280]{1,0:T(8,128)(2,1)}, u32[]{:S(2)}) copy-start(bf16[256,1280]{1,0:T(8,128)(2,1)} %refs_1_.3) | copy-start | bytes 1966084
  4.0 2.0 %collective-permute-start = (f32[8,14,8,128]{3,2,1,0:T(8,128)S(1)}, f32[8,14,8,128]{3,2,1,0:T(8,128)S(1)}, u32[]{:S(2)}, u32[]{:S(2)}) collective-permute-start(f32[8,14,8,128]{3,2,1,0:T(8,128)S(1)} %get-tuple-element.45), channel_id=1, source_target_pairs={{0,16},{16,0},{1,17},{17,1},{2,18},{18,2},{3,19},{19,3},{4,20},{20... | collective-permute-start | bytes 1376264 | tf_op jit(solution)/shard_map/ppermute | solution.py:308
  4.5 5.3 %collective-permute-start.1 = (f32[8,14,8,128]{3,2,1,0:T(8,128)S(1)}, f32[8,14,8,128]{3,2,1,0:T(8,128)S(1)}, u32[]{:S(2)}, u32[]{:S(2)}) collective-permute-start(f32[8,14,8,128]{3,2,1,0:T(8,128)S(1)} %get-tuple-element.44), channel_id=1, source_target_pairs={{0,16},{16,0},{1,17},{17,1},{2,18},{18,2},{3,19},{19,3},{4,20},{20... | collective-permute-start | bytes 1376264 | tf_op jit(solution)/shard_map/ppermute | solution.py:308
  4.6 4.4 %copy-start.3 = (f32[2,320,640]{2,1,0:T(8,128)S(1)}, f32[2,320,640]{2,1,0:T(8,128)}, u32[]{:S(2)}) copy-start(f32[2,320,640]{2,1,0:T(8,128)} %refs_3_.1) | copy-start | bytes 4915204
  5.5 4.0 %copy-start.4 = (f32[2,320,256]{2,1,0:T(8,128)S(1)}, f32[2,320,256]{2,1,0:T(8,128)}, u32[]{:S(2)}) copy-start(f32[2,320,256]{2,1,0:T(8,128)} %refs_6_.1) | copy-start | bytes 1966084
  6.0 9.4 %collective-permute-start.2 = (f32[8,14,8,128]{3,2,1,0:T(8,128)S(1)}, f32[8,14,8,128]{3,2,1,0:T(8,128)S(1)}, u32[]{:S(2)}, u32[]{:S(2)}) collective-permute-start(f32[8,14,8,128]{3,2,1,0:T(8,128)S(1)} %get-tuple-element.23), channel_id=1, source_target_pairs={{0,1},{1,0},{2,3},{3,2},{4,5},{5,4},{6,7},{7,6},{8,9},{9,8},{10,11... | collective-permute-start | bytes 1376264 | tf_op jit(solution)/shard_map/ppermute | solution.py:312
  9.0 2.9 %collective-permute-start.4 = (f32[160,640]{1,0:T(8,128)S(1)}, f32[160,640]{1,0:T(8,128)S(1)}, u32[]{:S(2)}, u32[]{:S(2)}) collective-permute-start(f32[160,640]{1,0:T(8,128)S(1)} %get-tuple-element.42), channel_id=1, source_target_pairs={{0,16},{16,0},{1,17},{17,1},{2,18},{18,2},{3,19},{19,3},{4,20},{20... | collective-permute-start | bytes 1228808 | tf_op jit(solution)/shard_map/ppermute | solution.py:308
  9.1 2.8 %collective-permute-start.3 = (f32[160,640]{1,0:T(8,128)S(1)}, f32[160,640]{1,0:T(8,128)S(1)}, u32[]{:S(2)}, u32[]{:S(2)}) collective-permute-start(f32[160,640]{1,0:T(8,128)S(1)} %get-tuple-element.43), channel_id=1, source_target_pairs={{0,16},{16,0},{1,17},{17,1},{2,18},{18,2},{3,19},{19,3},{4,20},{20... | collective-permute-start | bytes 1228808 | tf_op jit(solution)/shard_map/ppermute | solution.py:308
  9.6 2.3 %collective-permute-start.5 = (f32[320,256]{1,0:T(8,128)S(1)}, f32[320,256]{1,0:T(8,128)S(1)}, u32[]{:S(2)}, u32[]{:S(2)}) collective-permute-start(f32[320,256]{1,0:T(8,128)S(1)} %dynamic-slice_bitcast_fusion.2), channel_id=1, source_target_pairs={{0,16},{16,0},{1,17},{17,1},{2,18},{18,2},{3,19},{19,3},{4,20},{20... | collective-permute-start | bytes 983048 | tf_op jit(solution)/shard_map/ppermute | solution.py:308
  15.4 6.1 %collective-permute-start.6 = (f32[4,14,8,128]{3,2,1,0:T(8,128)S(1)}, f32[4,14,8,128]{3,2,1,0:T(8,128)S(1)}, u32[]{:S(2)}, u32[]{:S(2)}) collective-permute-start(f32[4,14,8,128]{3,2,1,0:T(8,128)S(1)} %slice_add_fusion.2), channel_id=1, source_target_pairs={{0,2},{1,3},{2,0},{3,1},{4,6},{5,7},{6,4},{7,5},{8,10},{9,11},{10,... | collective-permute-start | bytes 688136 | tf_op jit(solution)/shard_map/ppermute | solution.py:312
  21.6 6.4 %collective-permute-start.7 = (f32[1,14,8,128]{3,2,1,0:T(8,128)S(1)}, f32[1,14,8,128]{3,2,1,0:T(8,128)S(1)}, u32[]{:S(2)}, u32[]{:S(2)}) collective-permute-start(f32[1,14,8,128]{3,2,1,0:T(8,128)S(1)} %get-tuple-element.48), channel_id=1, source_target_pairs={{0,12},{1,13},{2,14},{3,15},{4,8},{5,9},{6,10},{7,11},{8,4},{9,5},... | collective-permute-start | bytes 172040 | tf_op jit(solution)/shard_map/ppermute | solution.py:312
  25.8 4.2 %collective-permute-start.9 = (f32[1,14,8,128]{3,2,1,0:T(8,128)S(1)}, f32[1,14,8,128]{3,2,1,0:T(8,128)S(1)}, u32[]{:S(2)}, u32[]{:S(2)}) collective-permute-start(f32[1,14,8,128]{3,2,1,0:T(8,128)S(1)} %get-tuple-element.49), channel_id=1, source_target_pairs={{0,4},{1,5},{2,6},{3,7},{4,0},{5,1},{6,2},{7,3},{8,12},{9,13},{10,... | collective-permute-start | bytes 172040 | tf_op jit(solution)/shard_map/ppermute | solution.py:312
  25.8 5.1 %collective-permute-start.8 = (f32[1,14,8,128]{3,2,1,0:T(8,128)S(1)}, f32[1,14,8,128]{3,2,1,0:T(8,128)S(1)}, u32[]{:S(2)}, u32[]{:S(2)}) collective-permute-start(f32[1,14,8,128]{3,2,1,0:T(8,128)S(1)} %get-tuple-element.50), channel_id=1, source_target_pairs={{0,8},{1,9},{2,10},{3,11},{4,12},{5,13},{6,14},{7,15},{8,0},{9,1},... | collective-permute-start | bytes 172040 | tf_op jit(solution)/shard_map/ppermute | solution.py:312
  30.9 6.1 %collective-permute-start.12 = (f32[1,14,8,128]{3,2,1,0:T(8,128)S(1)}, f32[1,14,8,128]{3,2,1,0:T(8,128)S(1)}, u32[]{:S(2)}, u32[]{:S(2)}) collective-permute-start(f32[1,14,8,128]{3,2,1,0:T(8,128)S(1)} %fusion.2), channel_id=1, source_target_pairs={{0,12},{1,13},{2,14},{3,15},{4,8},{5,9},{6,10},{7,11},{8,4},{9,5},... | collective-permute-start | bytes 172040 | tf_op jit(solution)/shard_map/ppermute | solution.py:312
  32.5 6.1 %collective-permute-start.11 = (f32[1,14,8,128]{3,2,1,0:T(8,128)S(1)}, f32[1,14,8,128]{3,2,1,0:T(8,128)S(1)}, u32[]{:S(2)}, u32[]{:S(2)}) collective-permute-start(f32[1,14,8,128]{3,2,1,0:T(8,128)S(1)} %fusion.2), channel_id=1, source_target_pairs={{0,8},{1,9},{2,10},{3,11},{4,12},{5,13},{6,14},{7,15},{8,0},{9,1},... | collective-permute-start | bytes 172040 | tf_op jit(solution)/shard_map/ppermute | solution.py:312
  34.5 4.6 %collective-permute-start.10 = (f32[1,14,8,128]{3,2,1,0:T(8,128)S(1)}, f32[1,14,8,128]{3,2,1,0:T(8,128)S(1)}, u32[]{:S(2)}, u32[]{:S(2)}) collective-permute-start(f32[1,14,8,128]{3,2,1,0:T(8,128)S(1)} %fusion.2), channel_id=1, source_target_pairs={{0,4},{1,5},{2,6},{3,7},{4,0},{5,1},{6,2},{7,3},{8,12},{9,13},{10,... | collective-permute-start | bytes 172040 | tf_op jit(solution)/shard_map/ppermute | solution.py:312
  37.0 2.1 %collective-permute-start.13 = (f32[1,1,8,128]{3,2,1,0:T(8,128)S(1)}, f32[1,1,8,128]{3,2,1,0:T(8,128)S(1)}, u32[]{:S(2)}, u32[]{:S(2)}) collective-permute-start(f32[1,1,8,128]{3,2,1,0:T(8,128)S(1)} %slice.82), channel_id=1, source_target_pairs={{0,16},{16,0},{1,17},{17,1},{2,18},{18,2},{3,19},{19,3},{4,20},{20... | collective-permute-start | bytes 12296 | tf_op jit(solution)/shard_map/ppermute | solution.py:308
  39.1 6.1 %collective-permute-start.14 = (f32[4,14,8,128]{3,2,1,0:T(8,128)S(1)}, f32[4,14,8,128]{3,2,1,0:T(8,128)S(1)}, u32[]{:S(2)}, u32[]{:S(2)}) collective-permute-start(f32[4,14,8,128]{3,2,1,0:T(8,128)S(1)} %pad_maximum_fusion), channel_id=1, source_target_pairs={{0,2},{1,3},{2,0},{3,1},{4,6},{5,7},{6,4},{7,5},{8,10},{9,11},{10,... | collective-permute-start | bytes 688136 | tf_op jit(solution)/shard_map/ppermute | solution.py:312
  45.2 8.5 %collective-permute-start.15 = (f32[8,14,8,128]{3,2,1,0:T(8,128)S(1)}, f32[8,14,8,128]{3,2,1,0:T(8,128)S(1)}, u32[]{:S(2)}, u32[]{:S(2)}) collective-permute-start(f32[8,14,8,128]{3,2,1,0:T(8,128)S(1)} %constant_dynamic-update-slice_fusion.refs_1_), channel_id=1, source_target_pairs={{0,1},{1,0},{2,3},{3,2},{4,5},{5,4},{6,7},{7,6},{8,9},{9,8},{10,11... | collective-permute-start | bytes 1376264 | tf_op jit(solution)/shard_map/ppermute | solution.py:312
  46.8 13.5 %copy-start.5 = (f32[256,256]{1,0:T(8,128)S(1)}, f32[256,256]{1,0:T(8,128)}, u32[]{:S(2)}) copy-start(f32[256,256]{1,0:T(8,128)} %refs_5_.1) | copy-start | bytes 786436
  46.8 6.7 %collective-permute-start.17 = (f32[8,2,8,128]{3,2,1,0:T(8,128)S(1)}, f32[8,2,8,128]{3,2,1,0:T(8,128)S(1)}, u32[]{:S(2)}, u32[]{:S(2)}) collective-permute-start(f32[8,2,8,128]{3,2,1,0:T(8,128)S(1)} %slice.83), channel_id=1, source_target_pairs={{0,17},{1,16},{2,19},{3,18},{4,21},{5,20},{6,23},{7,22},{8,25},{9,... | collective-permute-start | bytes 196616 | tf_op jit(solution)/shard_map/ppermute | solution.py:316
  46.9 6.6 %collective-permute-start.16 = (f32[8,2,8,128]{3,2,1,0:T(8,128)S(1)}, f32[8,2,8,128]{3,2,1,0:T(8,128)S(1)}, u32[]{:S(2)}, u32[]{:S(2)}) collective-permute-start(f32[8,2,8,128]{3,2,1,0:T(8,128)S(1)} %slice.83), channel_id=1, source_target_pairs={{0,16},{16,0},{1,17},{17,1},{2,18},{18,2},{3,19},{19,3},{4,20},{20... | collective-permute-start | bytes 196616 | tf_op jit(solution)/shard_map/ppermute | solution.py:308
  59.7 2.9 %collective-permute-start.19 = (f32[320,640]{1,0:T(8,128)S(1)}, f32[320,640]{1,0:T(8,128)S(1)}, u32[]{:S(2)}, u32[]{:S(2)}) collective-permute-start(f32[320,640]{1,0:T(8,128)S(1)} %get-tuple-element.37), channel_id=1, source_target_pairs={{0,16},{16,0},{1,17},{17,1},{2,18},{18,2},{3,19},{19,3},{4,20},{20... | collective-permute-start | bytes 2457608 | tf_op jit(solution)/shard_map/ppermute | solution.py:308
  62.5 1.7 %collective-permute-start.18 = (f32[320,256]{1,0:T(8,128)S(1)}, f32[320,256]{1,0:T(8,128)S(1)}, u32[]{:S(2)}, u32[]{:S(2)}) collective-permute-start(f32[320,256]{1,0:T(8,128)S(1)} %get-tuple-element.35), channel_id=1, source_target_pairs={{0,16},{16,0},{1,17},{17,1},{2,18},{18,2},{3,19},{19,3},{4,20},{20... | collective-permute-start | bytes 983048 | tf_op jit(solution)/shard_map/ppermute | solution.py:308
  62.6 1.6 %copy-start.6 = (f32[2,320,256]{2,1,0:T(8,128)S(1)}, f32[2,320,256]{2,1,0:T(8,128)}, u32[]{:S(2)}) copy-start(f32[2,320,256]{2,1,0:T(8,128)} %param.12) | copy-start | bytes 1966084
  62.6 1.7 %copy-start.7 = (f32[2,320,256]{2,1,0:T(8,128)S(1)}, f32[2,320,256]{2,1,0:T(8,128)}, u32[]{:S(2)}) copy-start(f32[2,320,256]{2,1,0:T(8,128)} %param.13) | copy-start | bytes 1966084

commit v7 on v6

--- a/solution.py
+++ b/solution.py
@@ -229,7 +229,7 @@
     left_ref[...] = (grad + once - apply3(twice, once)) * over
 
 
-def output_kernel(where_ref, near_ref, far_ref, other_near_ref, other_far_ref, fac_ref, left_ref, _, new_ref, mine_ref, theirs_ref,
+def output_kernel(where_ref, near_ref, far_ref, other_near_ref, other_far_ref, fac_ref, left_ref, _pace, _early, new_ref, mine_ref, theirs_ref,
                   tile_scr, half_scr, *, scale):
     block = where_ref[0]
     few = SUBS // 2
@@ -330,6 +330,8 @@
     fac_far = swap(fac_rows[: slab // 2]), swap(fac_rows[slab // 2 :])
     grad_far = swap(grad_rows)
     came, fac_far, grad_far = fence((came, fac_far, grad_far))
+    early = swap(fac_far[0][:SUBS, :LANES])
+    came, early = fence((came, early))
     came = send(kept[4:] + came[4:], (2, 1)), kept[:4] + came[:4]
     kept = came[0] + came[1]
     ways = (3, 2, 1)
@@ -356,7 +358,7 @@
     new_output, update, update_far = call(
         lambda *refs: output_kernel(*refs, scale=scale),
         where,
-        (near, far, beside, across, output_factor, left, pace),
+        (near, far, beside, across, output_factor, left, pace, early),
         [(rank, rank), (slab, rank), (slab, rank)],
         [(2, LANES, LANES), (2, SHARDS, SUBS, LANES)],
         24 * rank * rank * rank + 6 * order * rank * rank,

time: 65.9 us -> 67.3 us (1.021)
  waiting for transfers between devices: 28.2 us -> 29.7 us
    ppermute x9 -> x10, waiting for transfers between devices: 2.7 us -> 3.86 us  [swap(): return lax.ppermute(value, 'grp', [(0, 1), (1, 0)])]
    ppermute x9 -> x10, starting transfers between devices: 3.66 us -> 3.65 us  [swap(): return lax.ppermute(value, 'grp', [(0, 1), (1, 0)])]
  transfers between devices with their start and end apart: 20 -> 21, of which waited for: 14 -> 15; matrix products, arithmetic and copies ran while one was open for 2% -> 2% of each run, Pallas kernels for 5% -> 5%
where the time goes in v7:
time: 67.3 us; the launch traced here: 67.1 us
  waiting for transfers between devices  29.7 us (44%)
  starting transfers between devices  21.1 us (31%)
  Pallas kernels  10 us (15%)
  other arithmetic  2.91 us (4%)
  local copies, waits for them, and re-layouts  2.3 us (3%)
  between operations  0.87 us (1%)
    ppermute x10, waiting for transfers between devices, send(): return lax.ppermute(value, ('grp', 'own'), pairs)  20.8 us
    ppermute x10, starting transfers between devices, send(): return lax.ppermute(value, ('grp', 'own'), pairs)  17.4 us
    pallas_call x4, Pallas kernels, call(): pl.pallas_call(kernel, out_shape=outs, in_specs=[pl.BlockSpec(memory_spac...  10 us
    ppermute x1, waiting for transfers between devices, cross(): return lax.ppermute(value, ('grp', 'own'), pairs)  5.02 us
    ppermute x10, waiting for transfers between devices, swap(): return lax.ppermute(value, 'grp', [(0, 1), (1, 0)])  3.86 us
    ppermute x10, starting transfers between devices, swap(): return lax.ppermute(value, 'grp', [(0, 1), (1, 0)])  3.65 us
    unnamed x17, local copies, waits for them, and re-layouts  2.13 us
  transfers between devices with their start and end apart: 21, of which 15 were waited for; matrix products, arithmetic and copies ran while one was open for 2% of the time, Pallas kernels for 5%

profile of v7, /device:TPU:0, one launch (start us, length us, event | category | flops | bytes accessed | tf_op | source)
XLA Modules:
  0.0 67.1 jit_solution(7727901769616310363)
XLA Ops:
  0.6 0.0 copy-start
  0.7 0.8 %copy-done = bf16[256,256]{1,0:T(8,128)(2,1)S(1)} copy-done((bf16[256,256]{1,0:T(8,128)(2,1)S(1)}, bf16[256,256]{1,0:T(8,128)(2,1)}, u32[]{:S(2)}) %copy-start) | copy-done | bytes 131096
  1.5 0.2 fusion.5.refs_2_
  1.8 0.1 pad_add_fusion.refs_0_
  1.8 1.1 %copy-done.1 = bf16[256,1280]{1,0:T(8,128)(2,1)S(1)} copy-done((bf16[256,1280]{1,0:T(8,128)(2,1)S(1)}, bf16[256,1280]{1,0:T(8,128)(2,1)}, u32[]{:S(2)}) %copy-start.1) | copy-done | bytes 655384
  2.9 0.9 %shard_map.103 = f32[16,14,8,128]{3,2,1,0:T(8,128)S(1)} custom-call(s32[3]{0:T(128)S(1)} %pad_add_fusion.refs_0_, bf16[256,1280]{1,0:T(8,128)(2,1)S(1)} %copy-done.1, f32[256,256]{1,0:T(8,128)S(1)} %fusion.5.refs_2_), custom_call_target="tpu_custom_call" | custom-call | flops 209715200 | bytes 1835008 | tf_op jit(solution)/shard_map/pallas_call | solution.py:277
  3.9 0.1 fusion.3
  4.0 0.6 collective-permute-start
  4.5 0.1 collective-permute-start.1
  4.6 0.0 copy-done.2
  4.6 0.9 %shard_map.102 = f32[16,14,8,128]{3,2,1,0:T(8,128)S(1)} custom-call(s32[3]{0:T(128)S(1)} %pad_add_fusion.refs_0_, bf16[256,1280]{1,0:T(8,128)(2,1)S(1)} %copy-done.2, f32[256,256]{1,0:T(8,128)S(1)} %fusion.5.refs_2_), custom_call_target="tpu_custom_call" | custom-call | flops 209715200 | bytes 1835008 | tf_op jit(solution)/shard_map/pallas_call | solution.py:277
  5.5 0.0 copy-start.4
  5.6 0.4 collective-permute-done
  6.0 0.1 slice_add_fusion
  6.0 2.9 %collective-permute-start.2 = (f32[8,14,8,128]{3,2,1,0:T(8,128)S(1)}, f32[8,14,8,128]{3,2,1,0:T(8,128)S(1)}, u32[]{:S(2)}, u32[]{:S(2)}) collective-permute-start(f32[8,14,8,128]{3,2,1,0:T(8,128)S(1)} %get-tuple-element.25), channel_id=1, source_target_pairs={{0,1},{1,0},{2,3},{3,2},{4,5},{5,4},{6,7},{7,6},{8,9},{9,8},{10,11... | collective-permute-start | bytes 1376264 | tf_op jit(solution)/shard_map/ppermute | solution.py:312
  9.0 0.1 dynamic-slice_bitcast_fusion
  9.0 0.1 collective-permute-start.4
  9.1 0.5 collective-permute-start.3
  9.6 0.0 copy-done.4
  9.6 0.1 collective-permute-start.5
  9.8 2.1 %collective-permute-done.5.refs_7_ = f32[320,256]{1,0:T(8,128)S(1)} collective-permute-done((f32[320,256]{1,0:T(8,128)S(1)}, f32[320,256]{1,0:T(8,128)S(1)}, u32[]{:S(2)}, u32[]{:S(2)}) %collective-permute-start.5) | collective-permute-done | bytes 327712 | tf_op jit(solution)/shard_map/ppermute | solution.py:308
  11.9 0.0 collective-permute-done.4.refs_5_
  11.9 0.0 collective-permute-done.3.refs_4_
  11.9 3.5 %collective-permute-done.2 = f32[8,14,8,128]{3,2,1,0:T(8,128)S(1)} collective-permute-done((f32[8,14,8,128]{3,2,1,0:T(8,128)S(1)}, f32[8,14,8,128]{3,2,1,0:T(8,128)S(1)}, u32[]{:S(2)}, u32[]{:S(2)}) %collective-permute-start.2) | collective-permute-done | bytes 458784 | tf_op jit(solution)/shard_map/ppermute | solution.py:312
  15.4 0.0 collective-permute-start.6
  15.4 0.0 collective-permute-done.1
  15.4 0.1 add.62
  15.5 1.1 %collective-permute-done.6.refs_8_ = f32[8,128]{1,0:T(8,128)S(1)} collective-permute-done((f32[8,128]{1,0:T(8,128)S(1)}, f32[8,128]{1,0:T(8,128)S(1)}, u32[]{:S(2)}, u32[]{:S(2)}) %collective-permute-start.6) | collective-permute-done | bytes 4128 | tf_op jit(solution)/shard_map/ppermute | solution.py:308
  16.6 2.1 %collective-permute-start.7 = (f32[4,14,8,128]{3,2,1,0:T(8,128)S(1)}, f32[4,14,8,128]{3,2,1,0:T(8,128)S(1)}, u32[]{:S(2)}, u32[]{:S(2)}) collective-permute-start(f32[4,14,8,128]{3,2,1,0:T(8,128)S(1)} %slice_add_fusion.2), channel_id=1, source_target_pairs={{0,2},{1,3},{2,0},{3,1},{4,6},{5,7},{6,4},{7,5},{8,10},{9,11},{10,... | collective-permute-start | bytes 688136 | tf_op jit(solution)/shard_map/ppermute | solution.py:312
  18.7 4.0 %collective-permute-done.7 = f32[4,14,8,128]{3,2,1,0:T(8,128)S(1)} collective-permute-done((f32[4,14,8,128]{3,2,1,0:T(8,128)S(1)}, f32[4,14,8,128]{3,2,1,0:T(8,128)S(1)}, u32[]{:S(2)}, u32[]{:S(2)}) %collective-permute-start.7) | collective-permute-done | bytes 229408 | tf_op jit(solution)/shard_map/ppermute | solution.py:312
  22.8 4.2 %collective-permute-start.8 = (f32[1,14,8,128]{3,2,1,0:T(8,128)S(1)}, f32[1,14,8,128]{3,2,1,0:T(8,128)S(1)}, u32[]{:S(2)}, u32[]{:S(2)}) collective-permute-start(f32[1,14,8,128]{3,2,1,0:T(8,128)S(1)} %get-tuple-element.52), channel_id=1, source_target_pairs={{0,12},{1,13},{2,14},{3,15},{4,8},{5,9},{6,10},{7,11},{8,4},{9,5},... | collective-permute-start | bytes 172040 | tf_op jit(solution)/shard_map/ppermute | solution.py:312
  27.0 0.0 collective-permute-start.10
  27.0 0.6 collective-permute-start.9
  27.6 1.6 %collective-permute-done.8 = f32[1,14,8,128]{3,2,1,0:T(8,128)S(1)} collective-permute-done((f32[1,14,8,128]{3,2,1,0:T(8,128)S(1)}, f32[1,14,8,128]{3,2,1,0:T(8,128)S(1)}, u32[]{:S(2)}, u32[]{:S(2)}) %collective-permute-start.8) | collective-permute-done | bytes 57376 | tf_op jit(solution)/shard_map/ppermute | solution.py:312
  29.2 1.9 %collective-permute-done.10 = f32[1,14,8,128]{3,2,1,0:T(8,128)S(1)} collective-permute-done((f32[1,14,8,128]{3,2,1,0:T(8,128)S(1)}, f32[1,14,8,128]{3,2,1,0:T(8,128)S(1)}, u32[]{:S(2)}, u32[]{:S(2)}) %collective-permute-start.10) | collective-permute-done | bytes 57376 | tf_op jit(solution)/shard_map/ppermute | solution.py:312
  31.1 0.9 %collective-permute-done.9 = f32[1,14,8,128]{3,2,1,0:T(8,128)S(1)} collective-permute-done((f32[1,14,8,128]{3,2,1,0:T(8,128)S(1)}, f32[1,14,8,128]{3,2,1,0:T(8,128)S(1)}, u32[]{:S(2)}, u32[]{:S(2)}) %collective-permute-start.9) | collective-permute-done | bytes 57376 | tf_op jit(solution)/shard_map/ppermute | solution.py:312
  32.1 2.7 %collective-permute-start.13 = (f32[1,14,8,128]{3,2,1,0:T(8,128)S(1)}, f32[1,14,8,128]{3,2,1,0:T(8,128)S(1)}, u32[]{:S(2)}, u32[]{:S(2)}) collective-permute-start(f32[1,14,8,128]{3,2,1,0:T(8,128)S(1)} %fusion.2), channel_id=1, source_target_pairs={{0,12},{1,13},{2,14},{3,15},{4,8},{5,9},{6,10},{7,11},{8,4},{9,5},... | collective-permute-start | bytes 172040 | tf_op jit(solution)/shard_map/ppermute | solution.py:312
  34.8 0.8 %collective-permute-start.12 = (f32[1,14,8,128]{3,2,1,0:T(8,128)S(1)}, f32[1,14,8,128]{3,2,1,0:T(8,128)S(1)}, u32[]{:S(2)}, u32[]{:S(2)}) collective-permute-start(f32[1,14,8,128]{3,2,1,0:T(8,128)S(1)} %fusion.2), channel_id=1, source_target_pairs={{0,8},{1,9},{2,10},{3,11},{4,12},{5,13},{6,14},{7,15},{8,0},{9,1},... | collective-permute-start | bytes 172040 | tf_op jit(solution)/shard_map/ppermute | solution.py:312
  35.6 0.9 %collective-permute-start.11 = (f32[1,14,8,128]{3,2,1,0:T(8,128)S(1)}, f32[1,14,8,128]{3,2,1,0:T(8,128)S(1)}, u32[]{:S(2)}, u32[]{:S(2)}) collective-permute-start(f32[1,14,8,128]{3,2,1,0:T(8,128)S(1)} %fusion.2), channel_id=1, source_target_pairs={{0,4},{1,5},{2,6},{3,7},{4,0},{5,1},{6,2},{7,3},{8,12},{9,13},{10,... | collective-permute-start | bytes 172040 | tf_op jit(solution)/shard_map/ppermute | solution.py:312
  36.5 1.7 %collective-permute-done.13 = f32[1,14,8,128]{3,2,1,0:T(8,128)S(1)} collective-permute-done((f32[1,14,8,128]{3,2,1,0:T(8,128)S(1)}, f32[1,14,8,128]{3,2,1,0:T(8,128)S(1)}, u32[]{:S(2)}, u32[]{:S(2)}) %collective-permute-start.13) | collective-permute-done | bytes 57376 | tf_op jit(solution)/shard_map/ppermute | solution.py:312
  38.2 0.0 collective-permute-start.14
  38.2 2.1 %collective-permute-done.12 = f32[1,14,8,128]{3,2,1,0:T(8,128)S(1)} collective-permute-done((f32[1,14,8,128]{3,2,1,0:T(8,128)S(1)}, f32[1,14,8,128]{3,2,1,0:T(8,128)S(1)}, u32[]{:S(2)}, u32[]{:S(2)}) %collective-permute-start.12) | collective-permute-done | bytes 57376 | tf_op jit(solution)/shard_map/ppermute | solution.py:312
  40.3 0.3 collective-permute-done.11
  40.6 0.0 collective-permute-done.14.refs_7_
  40.6 1.6 %collective-permute-start.15 = (f32[4,14,8,128]{3,2,1,0:T(8,128)S(1)}, f32[4,14,8,128]{3,2,1,0:T(8,128)S(1)}, u32[]{:S(2)}, u32[]{:S(2)}) collective-permute-start(f32[4,14,8,128]{3,2,1,0:T(8,128)S(1)} %pad_maximum_fusion), channel_id=1, source_target_pairs={{0,2},{1,3},{2,0},{3,1},{4,6},{5,7},{6,4},{7,5},{8,10},{9,11},{10,... | collective-permute-start | bytes 688136 | tf_op jit(solution)/shard_map/ppermute | solution.py:312
  42.2 4.5 %collective-permute-done.15 = f32[4,14,8,128]{3,2,1,0:T(8,128)S(1)} collective-permute-done((f32[4,14,8,128]{3,2,1,0:T(8,128)S(1)}, f32[4,14,8,128]{3,2,1,0:T(8,128)S(1)}, u32[]{:S(2)}, u32[]{:S(2)}) %collective-permute-start.15) | collective-permute-done | bytes 229408 | tf_op jit(solution)/shard_map/ppermute | solution.py:312
  46.7 1.6 %collective-permute-start.16 = (f32[8,14,8,128]{3,2,1,0:T(8,128)S(1)}, f32[8,14,8,128]{3,2,1,0:T(8,128)S(1)}, u32[]{:S(2)}, u32[]{:S(2)}) collective-permute-start(f32[8,14,8,128]{3,2,1,0:T(8,128)S(1)} %constant_dynamic-update-slice_fusion.refs_1_), channel_id=1, source_target_pairs={{0,1},{1,0},{2,3},{3,2},{4,5},{5,4},{6,7},{7,6},{8,9},{9,8},{10,11... | collective-permute-start | bytes 1376264 | tf_op jit(solution)/shard_map/ppermute | solution.py:312
  48.3 0.1 collective-permute-start.18
  48.4 1.6 %collective-permute-start.17 = (f32[8,2,8,128]{3,2,1,0:T(8,128)S(1)}, f32[8,2,8,128]{3,2,1,0:T(8,128)S(1)}, u32[]{:S(2)}, u32[]{:S(2)}) collective-permute-start(f32[8,2,8,128]{3,2,1,0:T(8,128)S(1)} %slice.87), channel_id=1, source_target_pairs={{0,16},{16,0},{1,17},{17,1},{2,18},{18,2},{3,19},{19,3},{4,20},{20... | collective-permute-start | bytes 196616 | tf_op jit(solution)/shard_map/ppermute | solution.py:308
  50.0 5.0 %collective-permute-done.18.refs_4_ = f32[8,2,8,128]{3,2,1,0:T(8,128)S(1)} collective-permute-done((f32[8,2,8,128]{3,2,1,0:T(8,128)S(1)}, f32[8,2,8,128]{3,2,1,0:T(8,128)S(1)}, u32[]{:S(2)}, u32[]{:S(2)}) %collective-permute-start.18) | collective-permute-done | bytes 65568 | tf_op jit(solution)/shard_map/ppermute | solution.py:316
  55.0 0.0 collective-permute-done.17.refs_3_
  55.0 0.3 collective-permute-done.16.refs_2_
  55.3 5.9 %shard_map.104 = (f32[320,640]{1,0:T(8,128)S(1)}, f32[320,640]{1,0:T(8,128)S(1)}, f32[640,256]{1,0:T(8,128)S(1)}) custom-call(s32[3]{0:T(128)S(1)} %pad_add_fusion.refs_0_, f32[8,14,8,128]{3,2,1,0:T(8,128)S(1)} %constant_dynamic-update-slice_fusion.refs_1_, f32[8,14,8,128]{3,2,1,0:T(8,128)S(1)} %collective-permute-done.16.refs_2_, ...), custom_call_target="tpu_custom_call" | custom-call | flops 4089446400 | bytes 6651904 | tf_op jit(solution)/shard_map/pallas_call | solution.py:277
  61.2 0.6 collective-permute-start.20
  61.8 0.0 copy-done.5
  61.8 2.2 %shard_map.105 = (f32[256,256]{1,0:T(8,128)}, f32[320,256]{1,0:T(8,128)S(1)}, f32[320,256]{1,0:T(8,128)S(1)}) custom-call(s32[3]{0:T(128)S(1)} %pad_add_fusion.refs_0_, f32[8,14,8,128]{3,2,1,0:T(8,128)S(1)} %constant_dynamic-update-slice_fusion.refs_1_, f32[8,14,8,128]{3,2,1,0:T(8,128)S(1)} %collective-permute-done.16.refs_2_, ...), custom_call_target="tpu_custom_call" | custom-call | flops 654311424 | bytes 2891776 | tf_op jit(solution)/shard_map/pallas_call | solution.py:277
  64.0 0.1 collective-permute-start.19
  64.1 0.0 collective-permute-done.20
  64.1 0.0 copy-start.6
  64.1 0.0 copy-start.7
  64.2 1.3 %broadcast_select_fusion = f32[2,320,640]{2,1,0:T(8,128)} fusion(f32[320,640]{1,0:T(8,128)S(1)} %collective-permute-done.20, f32[320,640]{1,0:T(8,128)S(1)} %get-tuple-element.40, pred[2]{0:T(512)(128)(4,1)S(1)} %iota_compare_fusion), kind=kLoop, calls=%fused_computation | loop fusion | flops 409600 | bytes 3276802 | tf_op jit(solution)/shard_map/jit(_where)/select_n | solution.py:369
  65.5 0.2 collective-permute-done.19
  65.7 0.1 copy-done.7
  65.9 1.3 %multiply_subtract_fusion = (f32[2,320,256]{2,1,0:T(8,128)}, f32[2,320,256]{2,1,0:T(8,128)}) fusion(f32[2,320,256]{2,1,0:T(8,128)S(1)} %copy-done.6, f32[320,256]{1,0:T(8,128)S(1)} %collective-permute-done.19, f32[320,256]{1,0:T(8,128)S(1)} %get-tuple-element.38, pred[2]{0:T(512)(128)(4,1)S(1)} %iota_compare_fusion, f32[2,320,256]{2,1,0:T(8,128)S(1)} %copy-done.7), kind=kLoop, calls=%fused_computation.1 | loop fusion | flops 819200 | bytes 3276802 | tf_op jit(solution)/shard_map/sub | solution.py:372
  (18 shorter events, 0.2 us)
Async XLA Ops:
  0.6 0.9 %copy-start = (bf16[256,256]{1,0:T(8,128)(2,1)S(1)}, bf16[256,256]{1,0:T(8,128)(2,1)}, u32[]{:S(2)}) copy-start(bf16[256,256]{1,0:T(8,128)(2,1)} %param.8) | copy-start | bytes 393220
  1.8 1.1 %copy-start.1 = (bf16[256,1280]{1,0:T(8,128)(2,1)S(1)}, bf16[256,1280]{1,0:T(8,128)(2,1)}, u32[]{:S(2)}) copy-start(bf16[256,1280]{1,0:T(8,128)(2,1)} %refs_1_.3) | copy-start | bytes 1966084
  2.9 1.7 %copy-start.2 = (bf16[256,1280]{1,0:T(8,128)(2,1)S(1)}, bf16[256,1280]{1,0:T(8,128)(2,1)}, u32[]{:S(2)}) copy-start(bf16[256,1280]{1,0:T(8,128)(2,1)} %refs_1_.3) | copy-start | bytes 1966084
  4.0 2.0 %collective-permute-start = (f32[8,14,8,128]{3,2,1,0:T(8,128)S(1)}, f32[8,14,8,128]{3,2,1,0:T(8,128)S(1)}, u32[]{:S(2)}, u32[]{:S(2)}) collective-permute-start(f32[8,14,8,128]{3,2,1,0:T(8,128)S(1)} %get-tuple-element.49), channel_id=1, source_target_pairs={{0,16},{16,0},{1,17},{17,1},{2,18},{18,2},{3,19},{19,3},{4,20},{20... | collective-permute-start | bytes 1376264 | tf_op jit(solution)/shard_map/ppermute | solution.py:308
  4.5 10.9 %collective-permute-start.1 = (f32[8,14,8,128]{3,2,1,0:T(8,128)S(1)}, f32[8,14,8,128]{3,2,1,0:T(8,128)S(1)}, u32[]{:S(2)}, u32[]{:S(2)}) collective-permute-start(f32[8,14,8,128]{3,2,1,0:T(8,128)S(1)} %get-tuple-element.48), channel_id=1, source_target_pairs={{0,16},{16,0},{1,17},{17,1},{2,18},{18,2},{3,19},{19,3},{4,20},{20... | collective-permute-start | bytes 1376264 | tf_op jit(solution)/shard_map/ppermute | solution.py:308
  4.6 4.4 %copy-start.3 = (f32[2,320,640]{2,1,0:T(8,128)S(1)}, f32[2,320,640]{2,1,0:T(8,128)}, u32[]{:S(2)}) copy-start(f32[2,320,640]{2,1,0:T(8,128)} %refs_3_.1) | copy-start | bytes 4915204
  5.5 4.0 %copy-start.4 = (f32[2,320,256]{2,1,0:T(8,128)S(1)}, f32[2,320,256]{2,1,0:T(8,128)}, u32[]{:S(2)}) copy-start(f32[2,320,256]{2,1,0:T(8,128)} %refs_6_.1) | copy-start | bytes 1966084
  6.0 9.4 %collective-permute-start.2 = (f32[8,14,8,128]{3,2,1,0:T(8,128)S(1)}, f32[8,14,8,128]{3,2,1,0:T(8,128)S(1)}, u32[]{:S(2)}, u32[]{:S(2)}) collective-permute-start(f32[8,14,8,128]{3,2,1,0:T(8,128)S(1)} %get-tuple-element.25), channel_id=1, source_target_pairs={{0,1},{1,0},{2,3},{3,2},{4,5},{5,4},{6,7},{7,6},{8,9},{9,8},{10,11... | collective-permute-start | bytes 1376264 | tf_op jit(solution)/shard_map/ppermute | solution.py:312
  9.0 2.9 %collective-permute-start.4 = (f32[160,640]{1,0:T(8,128)S(1)}, f32[160,640]{1,0:T(8,128)S(1)}, u32[]{:S(2)}, u32[]{:S(2)}) collective-permute-start(f32[160,640]{1,0:T(8,128)S(1)} %get-tuple-element.46), channel_id=1, source_target_pairs={{0,16},{16,0},{1,17},{17,1},{2,18},{18,2},{3,19},{19,3},{4,20},{20... | collective-permute-start | bytes 1228808 | tf_op jit(solution)/shard_map/ppermute | solution.py:308
  9.1 2.8 %collective-permute-start.3 = (f32[160,640]{1,0:T(8,128)S(1)}, f32[160,640]{1,0:T(8,128)S(1)}, u32[]{:S(2)}, u32[]{:S(2)}) collective-permute-start(f32[160,640]{1,0:T(8,128)S(1)} %get-tuple-element.47), channel_id=1, source_target_pairs={{0,16},{16,0},{1,17},{17,1},{2,18},{18,2},{3,19},{19,3},{4,20},{20... | collective-permute-start | bytes 1228808 | tf_op jit(solution)/shard_map/ppermute | solution.py:308
  9.6 2.3 %collective-permute-start.5 = (f32[320,256]{1,0:T(8,128)S(1)}, f32[320,256]{1,0:T(8,128)S(1)}, u32[]{:S(2)}, u32[]{:S(2)}) collective-permute-start(f32[320,256]{1,0:T(8,128)S(1)} %dynamic-slice_bitcast_fusion.2), channel_id=1, source_target_pairs={{0,16},{16,0},{1,17},{17,1},{2,18},{18,2},{3,19},{19,3},{4,20},{20... | collective-permute-start | bytes 983048 | tf_op jit(solution)/shard_map/ppermute | solution.py:308
  15.4 1.2 %collective-permute-start.6 = (f32[8,128]{1,0:T(8,128)S(1)}, f32[8,128]{1,0:T(8,128)S(1)}, u32[]{:S(2)}, u32[]{:S(2)}) collective-permute-start(f32[8,128]{1,0:T(8,128)S(1)} %slice.66), channel_id=1, source_target_pairs={{0,16},{16,0},{1,17},{17,1},{2,18},{18,2},{3,19},{19,3},{4,20},{20... | collective-permute-start | bytes 12296 | tf_op jit(solution)/shard_map/ppermute | solution.py:308
  16.6 6.1 %collective-permute-start.7 = (f32[4,14,8,128]{3,2,1,0:T(8,128)S(1)}, f32[4,14,8,128]{3,2,1,0:T(8,128)S(1)}, u32[]{:S(2)}, u32[]{:S(2)}) collective-permute-start(f32[4,14,8,128]{3,2,1,0:T(8,128)S(1)} %slice_add_fusion.2), channel_id=1, source_target_pairs={{0,2},{1,3},{2,0},{3,1},{4,6},{5,7},{6,4},{7,5},{8,10},{9,11},{10,... | collective-permute-start | bytes 688136 | tf_op jit(solution)/shard_map/ppermute | solution.py:312
  22.8 6.4 %collective-permute-start.8 = (f32[1,14,8,128]{3,2,1,0:T(8,128)S(1)}, f32[1,14,8,128]{3,2,1,0:T(8,128)S(1)}, u32[]{:S(2)}, u32[]{:S(2)}) collective-permute-start(f32[1,14,8,128]{3,2,1,0:T(8,128)S(1)} %get-tuple-element.52), channel_id=1, source_target_pairs={{0,12},{1,13},{2,14},{3,15},{4,8},{5,9},{6,10},{7,11},{8,4},{9,5},... | collective-permute-start | bytes 172040 | tf_op jit(solution)/shard_map/ppermute | solution.py:312
  27.0 4.2 %collective-permute-start.10 = (f32[1,14,8,128]{3,2,1,0:T(8,128)S(1)}, f32[1,14,8,128]{3,2,1,0:T(8,128)S(1)}, u32[]{:S(2)}, u32[]{:S(2)}) collective-permute-start(f32[1,14,8,128]{3,2,1,0:T(8,128)S(1)} %get-tuple-element.53), channel_id=1, source_target_pairs={{0,4},{1,5},{2,6},{3,7},{4,0},{5,1},{6,2},{7,3},{8,12},{9,13},{10,... | collective-permute-start | bytes 172040 | tf_op jit(solution)/shard_map/ppermute | solution.py:312
  27.0 5.1 %collective-permute-start.9 = (f32[1,14,8,128]{3,2,1,0:T(8,128)S(1)}, f32[1,14,8,128]{3,2,1,0:T(8,128)S(1)}, u32[]{:S(2)}, u32[]{:S(2)}) collective-permute-start(f32[1,14,8,128]{3,2,1,0:T(8,128)S(1)} %get-tuple-element.54), channel_id=1, source_target_pairs={{0,8},{1,9},{2,10},{3,11},{4,12},{5,13},{6,14},{7,15},{8,0},{9,1},... | collective-permute-start | bytes 172040 | tf_op jit(solution)/shard_map/ppermute | solution.py:312
  32.1 6.1 %collective-permute-start.13 = (f32[1,14,8,128]{3,2,1,0:T(8,128)S(1)}, f32[1,14,8,128]{3,2,1,0:T(8,128)S(1)}, u32[]{:S(2)}, u32[]{:S(2)}) collective-permute-start(f32[1,14,8,128]{3,2,1,0:T(8,128)S(1)} %fusion.2), channel_id=1, source_target_pairs={{0,12},{1,13},{2,14},{3,15},{4,8},{5,9},{6,10},{7,11},{8,4},{9,5},... | collective-permute-start | bytes 172040 | tf_op jit(solution)/shard_map/ppermute | solution.py:312
  34.8 5.5 %collective-permute-start.12 = (f32[1,14,8,128]{3,2,1,0:T(8,128)S(1)}, f32[1,14,8,128]{3,2,1,0:T(8,128)S(1)}, u32[]{:S(2)}, u32[]{:S(2)}) collective-permute-start(f32[1,14,8,128]{3,2,1,0:T(8,128)S(1)} %fusion.2), channel_id=1, source_target_pairs={{0,8},{1,9},{2,10},{3,11},{4,12},{5,13},{6,14},{7,15},{8,0},{9,1},... | collective-permute-start | bytes 172040 | tf_op jit(solution)/shard_map/ppermute | solution.py:312
  35.6 5.0 %collective-permute-start.11 = (f32[1,14,8,128]{3,2,1,0:T(8,128)S(1)}, f32[1,14,8,128]{3,2,1,0:T(8,128)S(1)}, u32[]{:S(2)}, u32[]{:S(2)}) collective-permute-start(f32[1,14,8,128]{3,2,1,0:T(8,128)S(1)} %fusion.2), channel_id=1, source_target_pairs={{0,4},{1,5},{2,6},{3,7},{4,0},{5,1},{6,2},{7,3},{8,12},{9,13},{10,... | collective-permute-start | bytes 172040 | tf_op jit(solution)/shard_map/ppermute | solution.py:312
  38.2 2.4 %collective-permute-start.14 = (f32[1,1,8,128]{3,2,1,0:T(8,128)S(1)}, f32[1,1,8,128]{3,2,1,0:T(8,128)S(1)}, u32[]{:S(2)}, u32[]{:S(2)}) collective-permute-start(f32[1,1,8,128]{3,2,1,0:T(8,128)S(1)} %slice.86), channel_id=1, source_target_pairs={{0,16},{16,0},{1,17},{17,1},{2,18},{18,2},{3,19},{19,3},{4,20},{20... | collective-permute-start | bytes 12296 | tf_op jit(solution)/shard_map/ppermute | solution.py:308
  40.6 6.1 %collective-permute-start.15 = (f32[4,14,8,128]{3,2,1,0:T(8,128)S(1)}, f32[4,14,8,128]{3,2,1,0:T(8,128)S(1)}, u32[]{:S(2)}, u32[]{:S(2)}) collective-permute-start(f32[4,14,8,128]{3,2,1,0:T(8,128)S(1)} %pad_maximum_fusion), channel_id=1, source_target_pairs={{0,2},{1,3},{2,0},{3,1},{4,6},{5,7},{6,4},{7,5},{8,10},{9,11},{10,... | collective-permute-start | bytes 688136 | tf_op jit(solution)/shard_map/ppermute | solution.py:312
  46.7 8.5 %collective-permute-start.16 = (f32[8,14,8,128]{3,2,1,0:T(8,128)S(1)}, f32[8,14,8,128]{3,2,1,0:T(8,128)S(1)}, u32[]{:S(2)}, u32[]{:S(2)}) collective-permute-start(f32[8,14,8,128]{3,2,1,0:T(8,128)S(1)} %constant_dynamic-update-slice_fusion.refs_1_), channel_id=1, source_target_pairs={{0,1},{1,0},{2,3},{3,2},{4,5},{5,4},{6,7},{7,6},{8,9},{9,8},{10,11... | collective-permute-start | bytes 1376264 | tf_op jit(solution)/shard_map/ppermute | solution.py:312
  48.3 13.5 %copy-start.5 = (f32[256,256]{1,0:T(8,128)S(1)}, f32[256,256]{1,0:T(8,128)}, u32[]{:S(2)}) copy-start(f32[256,256]{1,0:T(8,128)} %refs_5_.1) | copy-start | bytes 786436
  48.3 6.7 %collective-permute-start.18 = (f32[8,2,8,128]{3,2,1,0:T(8,128)S(1)}, f32[8,2,8,128]{3,2,1,0:T(8,128)S(1)}, u32[]{:S(2)}, u32[]{:S(2)}) collective-permute-start(f32[8,2,8,128]{3,2,1,0:T(8,128)S(1)} %slice.87), channel_id=1, source_target_pairs={{0,17},{1,16},{2,19},{3,18},{4,21},{5,20},{6,23},{7,22},{8,25},{9,... | collective-permute-start | bytes 196616 | tf_op jit(solution)/shard_map/ppermute | solution.py:316
  48.4 6.6 %collective-permute-start.17 = (f32[8,2,8,128]{3,2,1,0:T(8,128)S(1)}, f32[8,2,8,128]{3,2,1,0:T(8,128)S(1)}, u32[]{:S(2)}, u32[]{:S(2)}) collective-permute-start(f32[8,2,8,128]{3,2,1,0:T(8,128)S(1)} %slice.87), channel_id=1, source_target_pairs={{0,16},{16,0},{1,17},{17,1},{2,18},{18,2},{3,19},{19,3},{4,20},{20... | collective-permute-start | bytes 196616 | tf_op jit(solution)/shard_map/ppermute | solution.py:308
  61.2 2.9 %collective-permute-start.20 = (f32[320,640]{1,0:T(8,128)S(1)}, f32[320,640]{1,0:T(8,128)S(1)}, u32[]{:S(2)}, u32[]{:S(2)}) collective-permute-start(f32[320,640]{1,0:T(8,128)S(1)} %get-tuple-element.41), channel_id=1, source_target_pairs={{0,16},{16,0},{1,17},{17,1},{2,18},{18,2},{3,19},{19,3},{4,20},{20... | collective-permute-start | bytes 2457608 | tf_op jit(solution)/shard_map/ppermute | solution.py:308
  64.0 1.7 %collective-permute-start.19 = (f32[320,256]{1,0:T(8,128)S(1)}, f32[320,256]{1,0:T(8,128)S(1)}, u32[]{:S(2)}, u32[]{:S(2)}) collective-permute-start(f32[320,256]{1,0:T(8,128)S(1)} %get-tuple-element.39), channel_id=1, source_target_pairs={{0,16},{16,0},{1,17},{17,1},{2,18},{18,2},{3,19},{19,3},{4,20},{20... | collective-permute-start | bytes 983048 | tf_op jit(solution)/shard_map/ppermute | solution.py:308
  64.1 1.6 %copy-start.6 = (f32[2,320,256]{2,1,0:T(8,128)S(1)}, f32[2,320,256]{2,1,0:T(8,128)}, u32[]{:S(2)}) copy-start(f32[2,320,256]{2,1,0:T(8,128)} %param.12) | copy-start | bytes 1966084
  64.1 1.7 %copy-start.7 = (f32[2,320,256]{2,1,0:T(8,128)S(1)}, f32[2,320,256]{2,1,0:T(8,128)}, u32[]{:S(2)}) copy-start(f32[2,320,256]{2,1,0:T(8,128)} %param.13) | copy-start | bytes 1966084
